TPU v7x, 512 devices: a whole 4x8x8 slice. The times are simulated.
512 devices in a mesh: rep: 16 (over x, y_hi, core), tile: 32 (over y_lo, z).
Axes of the slice: x: 4, y: 8 (y_hi: 2, y_lo: 4; y = y_hi * 4 + y_lo), z: 8, core: 2. Of those that a mesh axis runs over, the one named last changes fastest.
Arguments:
- fields: bfloat16 [16, 192, 8, 8, 256], P('rep', 'tile'), may hold values from -6 to 6
- cotangent: bfloat16 [16, 192, 8, 8, 256], P('rep', 'tile'), may hold values from -6 to 6
- weights: float32 [16, 2304, 256], P('rep', 'tile'), may hold values from -6 to 6
- ema: float32 [16, 2304, 256], P('rep', 'tile'), may hold values from -6 to 6
- tile_links: int32 [192, 4], replicated, may hold values from 0 to 191, as said below
- tile_codes: int32 [192, 4], replicated, may hold values from 0 to 3
- corner_links: int32 [192, 4], replicated, may hold values from -1 to 191, as said below
- corner_codes: int32 [192, 4], replicated, may hold values from 0 to 3
- gossip_bit: int32 [1], replicated, may hold values from 0 to 1
- batch_size: int32 [1], replicated, may hold values from 32 to 512
Outputs:
- activations: bfloat16 [16, 192, 8, 8, 256], P('rep', 'tile')
- field_grad: bfloat16 [16, 192, 8, 8, 256], P('rep', 'tile')
- averaged: float32 [16, 2304, 256], P('rep', 'tile')
- ema_out: float32 [16, 2304, 256], P('rep', 'tile')
Inputs may be any that keep to these rules, and one draw needn't show every extreme that they name: tile_links, tile_codes, corner_links and corner_codes describe the tiles of a HEALPix sphere: 12 base faces, each cut into 4 x 4 tiles, numbered face by face (the order of the faces drawn from the seed) and row by row within a face. The relation is symmetric: if tile u lies across edge q of tile t as its edge e, then t lies across edge e of u as its edge q, and cells along a shared edge run in the same order on both tiles; likewise, if corner q of t takes corner cell c of u, then corner c of u takes corner cell q of t. `corner_links`: -1 exactly at the tiles' corners that touch one of the 8 vertices where only three base faces meet.
All inputs are finite; a program needn't handle non-finite values.
Results may differ from a plain program's by a relative error of at most 0.0014.
The roundings to bfloat16 on the way count: a program that leaves them out, or rounds other values in their place, can miss the bound.
Values may be sent and summed in bfloat16 or wider, within the bound.
No kernel may reach another device: no remote copies, remote signals or barrier semaphores. Data moves between devices by JAX's collectives and lax.ppermute only.
A program may use at most 64 MiB of HBM per device.

v0:
```python
import jax
import jax.numpy as jnp
from jax import lax
from jax.sharding import PartitionSpec as P

LEARN = 0.5


def from_partner(value, axis, distance):
    mask = 2**distance
    pairs = [(source, source ^ mask) for source in range(lax.axis_size(axis))]
    return lax.ppermute(value, axis, pairs)


def swap_level(level):

    def run_swap(value):
        return from_partner(value, "rep", level)

    return run_swap


def edge_strips(block):
    return jnp.stack([block[:, 0], block[:, -1], block[:, :, 0], block[:, :, -1]], axis=1)


def corner_cells(block):
    return jnp.stack([block[:, 0, 0], block[:, 0, -1], block[:, -1, 0], block[:, -1, -1]], axis=1)


def padded_sides(block):
    return jnp.stack(
        [block[:, 0, 1:-1], block[:, -1, 1:-1], block[:, 1:-1, 0], block[:, 1:-1, -1]], axis=1
    )


def body(
    fields,
    cotangent,
    weights,
    ema,
    tile_links,
    tile_codes,
    corner_links,
    corner_codes,
    gossip_bit,
    batch_size,
):
    block = fields[0]
    per_device = block.shape[0]
    side_len = block.shape[1]
    channels = block.shape[-1]
    first_tile = lax.axis_index("tile") * per_device
    my_tiles = first_tile + jnp.arange(per_device, dtype=jnp.int32)
    my_links = lax.dynamic_slice_in_dim(tile_links, first_tile, per_device, 0)
    my_codes = lax.dynamic_slice_in_dim(tile_codes, first_tile, per_device, 0)
    my_corner = lax.dynamic_slice_in_dim(corner_links, first_tile, per_device, 0)
    my_corner_codes = lax.dynamic_slice_in_dim(corner_codes, first_tile, per_device, 0)
    my_present = (my_corner >= 0)[:, :, None]
    quarter = jnp.arange(4, dtype=jnp.int32)
    strips_in = lax.all_gather(edge_strips(block), "tile", axis=0, tiled=True)
    cells_in = lax.all_gather(corner_cells(block), "tile", axis=0, tiled=True)
    row_count = strips_in.shape[0]
    source = jnp.arange(row_count, dtype=jnp.int32)
    choose = (
        (my_links[:, :, None, None] == source[None, None, :, None])
        & (my_codes[:, :, None, None] == quarter[None, None, None, :])
    ).astype(jnp.bfloat16)
    gained = jnp.einsum(
        "tepq,pqsc->tesc", choose, strips_in, preferred_element_type=jnp.float32
    ).astype(jnp.bfloat16)
    corner_pick = (
        (my_corner[:, :, None, None] == source[None, None, :, None])
        & (my_corner_codes[:, :, None, None] == quarter[None, None, None, :])
    ).astype(jnp.bfloat16)
    gained_cells = jnp.einsum(
        "tkpq,pqc->tkc", corner_pick, cells_in, preferred_element_type=jnp.float32
    ).astype(jnp.bfloat16)
    top_row = jnp.concatenate([gained_cells[:, 0:1], gained[:, 0], gained_cells[:, 1:2]], axis=1)
    bottom_row = jnp.concatenate([gained_cells[:, 2:3], gained[:, 1], gained_cells[:, 3:4]], axis=1)
    middle = jnp.concatenate([gained[:, 2][:, :, None], block, gained[:, 3][:, :, None]], axis=2)
    padded = jnp.concatenate([top_row[:, None], middle, bottom_row[:, None]], axis=1)
    weight_scale = (9.0 * channels) ** (-0.5)
    w_local = weights[0]
    w_scaled = (w_local * weight_scale).astype(jnp.bfloat16)
    gathered = lax.all_gather(w_scaled, "tile", axis=0, tiled=True)
    kernel = gathered.reshape(channels, 9, channels)
    hidden = jnp.zeros((per_device * side_len * side_len, channels), jnp.float32)
    for tap_index in range(9):
        row_off, col_off = divmod(tap_index, 3)
        window = padded[:, row_off : row_off + side_len, col_off : col_off + side_len].reshape(
            -1, channels
        )
        hidden = hidden + jnp.dot(
            window, kernel[:, tap_index, :], preferred_element_type=jnp.float32
        )
    sigmoid_pre = jax.nn.sigmoid(hidden)
    output = (hidden * sigmoid_pre).astype(jnp.bfloat16)
    grad_pre = (
        cotangent[0].reshape(-1, channels).astype(jnp.float32)
        * (sigmoid_pre * (1.0 + hidden * (1.0 - sigmoid_pre)))
    ).astype(jnp.bfloat16)
    grad_pad = jnp.zeros((per_device, side_len + 2, side_len + 2, channels), jnp.float32)
    for tap_index in range(9):
        row_off, col_off = divmod(tap_index, 3)
        backward = jnp.dot(grad_pre, kernel[:, tap_index, :].T, preferred_element_type=jnp.float32)
        grad_pad = grad_pad.at[:, row_off : row_off + side_len, col_off : col_off + side_len].add(
            backward.reshape(per_device, side_len, side_len, channels)
        )
    row_count = w_local.shape[0] * lax.axis_size("tile")
    chan_count = row_count // 9
    pieces = []
    for tap_index in range(9):
        row_off, col_off = divmod(tap_index, 3)
        window = padded[:, row_off : row_off + side_len, col_off : col_off + side_len].reshape(
            -1, chan_count
        )
        pieces.append(jnp.dot(window.T, grad_pre, preferred_element_type=jnp.float32))
    kernel_grad = lax.psum_scatter(
        jnp.stack(pieces, axis=1).reshape(row_count, channels),
        "tile",
        scatter_dimension=0,
        tiled=True,
    )
    side_grads = padded_sides(grad_pad).astype(jnp.bfloat16)
    corner_grads = jnp.where(my_present, corner_cells(grad_pad), jnp.zeros((), jnp.float32)).astype(
        jnp.bfloat16
    )
    sides_in = lax.all_gather(side_grads, "tile", axis=0, tiled=True)
    corners_in = lax.all_gather(corner_grads, "tile", axis=0, tiled=True)
    route = (
        (tile_links[:, :, None, None] == my_tiles[None, None, :, None])
        & (tile_codes[:, :, None, None] == quarter[None, None, None, :])
    ).astype(jnp.bfloat16)
    added = jnp.einsum("petq,pesc->tqsc", route, sides_in, preferred_element_type=jnp.float32)
    corner_route = (
        (corner_links[:, :, None, None] == my_tiles[None, None, :, None])
        & (corner_codes[:, :, None, None] == quarter[None, None, None, :])
    ).astype(jnp.bfloat16)
    corner_added = jnp.einsum(
        "pktq,pkc->tqc", corner_route, corners_in, preferred_element_type=jnp.float32
    )
    interior = grad_pad[:, 1:-1, 1:-1]
    interior = interior.at[:, 0].add(added[:, 0]).at[:, -1].add(added[:, 1])
    interior = interior.at[:, :, 0].add(added[:, 2]).at[:, :, -1].add(added[:, 3])
    interior = interior.at[:, 0, 0].add(corner_added[:, 0]).at[:, 0, -1].add(corner_added[:, 1])
    interior = interior.at[:, -1, 0].add(corner_added[:, 2]).at[:, -1, -1].add(corner_added[:, 3])
    square_sum = lax.psum(jnp.sum(kernel_grad * kernel_grad), "tile")
    root_mean = jnp.sqrt(square_sum / (9.0 * channels * channels) + 1e-06)
    updated = w_local - LEARN * kernel_grad / root_mean
    level_count = lax.axis_size("rep").bit_length() - 1
    branches = [swap_level(level) for level in range(level_count)]
    partner_rows = lax.switch(jnp.clip(gossip_bit[0], 0, level_count - 1), branches, updated)
    averaged = 0.5 * (updated + partner_rows)
    decay = jnp.power(0.99, batch_size[0].astype(jnp.float32) / 32.0)
    ema_out = decay * ema[0] + (1.0 - decay) * averaged
    return (
        output.reshape(1, per_device, side_len, side_len, channels),
        interior.astype(jnp.bfloat16)[None],
        averaged[None],
        ema_out[None],
    )


def solution(mesh):
    return jax.shard_map(
        body,
        mesh=mesh,
        in_specs=(
            P("rep", "tile", None, None, None),
            P("rep", "tile", None, None, None),
            P("rep", "tile", None),
            P("rep", "tile", None),
            P(),
            P(),
            P(),
            P(),
            P(),
            P(),
        ),
        out_specs=(
            P("rep", "tile", None, None, None),
            P("rep", "tile", None, None, None),
            P("rep", "tile", None),
            P("rep", "tile", None),
        ),
        check_vma=False,
    )
```

profile of v0, /device:TPU:56, one launch (start us, length us, event | category | flops | bytes accessed | tf_op | source)
XLA Modules:
  0.0 671.4 jit_solution(887840589556209083)
XLA Ops:
  7.2 1.5 fusion.63
  8.8 1.0 copy.383
  13.0 70.8 %all_gather.15 = bf16[192,4,256]{2,1,0:T(4,128)(2,1)S(1)} all-gather(bf16[6,4,256]{2,1,0:T(4,128)(2,1)S(1)} %copy.169), channel_id=1, replica_groups=mesh['rep'=16,'tile'=32] {'tile'}, dimensions={0}, use_global_device_ids=true | all-gather | bytes 405504 | tf_op jit(solution)/shard_map/all_gather | solution.py:62
  84.3 75.9 %all-gather.6.cloned.1.call-done = bf16[2304,256]{1,0:T(8,128)(2,1)} async-done(((bf16[72,256]{1,0:T(8,128)(2,1)}), bf16[2304,256]{1,0:T(8,128)(2,1)}) %all-gather.6.cloned.1.call-update) | async-done | bytes 1179664 | tf_op jit(solution)/shard_map/all_gather | solution.py:86
  160.2 2.3 reshape.801
  162.6 2.6 fusion.91
  165.2 149.7 %all-gather.4.cloned.1.call-done = bf16[192,4,8,256]{3,2,1,0:T(8,128)(2,1)} async-done(((bf16[6,4,8,256]{3,2,1,0:T(8,128)(2,1)}), bf16[192,4,8,256]{3,2,1,0:T(8,128)(2,1)}) %all-gather.4.cloned.1.call-update) | async-done | bytes 3145744 | tf_op jit(solution)/shard_map/all_gather | solution.py:61
  314.9 5.5 fusion.25
  327.1 3.5 copy.215
  330.6 4.5 reshape.822
  337.7 1.5 convolution_add_fusion.7
  339.2 3.1 scatter-add.59
  342.3 2.1 fusion.9
  344.5 3.1 scatter-add.60
  348.1 1.8 scatter-add.64
  350.2 1.8 scatter-add.65
  352.6 1.8 scatter-add.69
  355.0 1.8 scatter-add.70
  360.1 71.7 %all_gather.19 = bf16[192,4,256]{2,1,0:T(4,128)(2,1)S(1)} all-gather(bf16[6,4,256]{2,1,0:T(4,128)(2,1)S(1)} %fusion.90), channel_id=1, replica_groups=mesh['rep'=16,'tile'=32] {'tile'}, dimensions={0}, use_global_device_ids=true | all-gather | bytes 405504 | tf_op jit(solution)/shard_map/all_gather | solution.py:130
  432.1 59.5 %reduce-scatter.2.cloned.1.call-done = f32[72,256]{1,0:T(8,128)} async-done(((f32[2304,256]{1,0:T(8,128)}), f32[72,256]{1,0:T(8,128)}) %reduce-scatter.2.cloned.1.call-update) | async-done | bytes 73744 | tf_op jit(solution)/shard_map/reduce_scatter | solution.py:119
  491.7 1.5 multiply_reduce_fusion
  493.2 74.9 %psum.7 = f32[]{:T(128)} all-reduce(f32[]{:T(128)} %multiply_reduce_fusion), channel_id=1, replica_groups=mesh['rep'=16,'tile'=32] {'tile'}, use_global_device_ids=true, to_apply=%region_4.0 | all-reduce | flops 1 | bytes 8 | tf_op jit(solution)/shard_map/psum | solution.py:148
  569.7 10.4 %conditional.1 = (f32[72,256]{1,0:T(8,128)}) conditional(s32[]{:T(128)} %bitcast.102, f32[72,256]{1,0:T(8,128)S(1)} %bitcast_subtract_fusion, f32[72,256]{1,0:T(8,128)S(1)} %bitcast_subtract_fusion, f32[72,256]{1,0:T(8,128)S(1)} %bitcast_subtract_fusion, f32[72,256]{1,0:T(8,128)S(1)} %bitcast_subtract_fusion), branch_computations={%region_5.0_spmd, %region_6.0_spmd, %region_7.0_spmd, %region_8.0_... | conditional | bytes 294960 | solution.py:153
  569.8 5.1 collective-permute-start.1
  574.8 5.3 collective-permute-done.1
  580.1 1.6 fusion.62
  581.7 69.2 %all-gather.8.cloned.1.call-done = bf16[192,4,8,256]{3,2,1,0:T(8,128)(2,1)} async-done(((bf16[6,4,8,256]{3,2,1,0:T(8,128)(2,1)}), bf16[192,4,8,256]{3,2,1,0:T(8,128)(2,1)}) %all-gather.8.cloned.1.call-update) | async-done | bytes 3145744 | tf_op jit(solution)/shard_map/all_gather | solution.py:129
  650.9 5.4 fusion.13
  656.5 2.0 scatter-add.75
  658.6 2.0 scatter-add.76
  660.7 1.9 broadcast_select_fusion
  662.6 1.3 scatter-add.80
  (138 shorter events, 18.6 us)
Async XLA Ops:
  7.2 153.1 %all-gather.6.cloned.1.call-start = ((), (), s32[]{:S(2)}) async-start(), calls=%async_computation.2 | async-start | bytes 1216512 | tf_op jit(solution)/shard_map/all_gather | solution.py:86
  8.7 306.1 %all-gather.4.cloned.1.call-start = ((), (), s32[]{:S(2)}) async-start(), calls=%async_computation.1 | async-start | bytes 3244032 | tf_op jit(solution)/shard_map/all_gather | solution.py:61
  10.6 481.1 %reduce-scatter.2.cloned.1.call-start = ((), (), s32[]{:S(2)}) async-start(), calls=%async_computation.4 | async-start | bytes 2433024 | tf_op jit(solution)/shard_map/reduce_scatter | solution.py:119
  320.8 1.0 copy-start.4
  320.8 1.1 copy-start.3
  320.9 1.2 copy-start.2
  321.0 1.4 copy-start.1
  321.1 1.5 copy-start
  322.6 1.0 copy-start.5
  322.6 1.0 copy-start.15
  335.1 1.5 copy-start.13
  335.1 1.5 copy-start.14
  335.1 315.8 %all-gather.8.cloned.1.call-start = ((), (), s32[]{:S(2)}) async-start(), calls=%async_computation.3 | async-start | bytes 3244032 | tf_op jit(solution)/shard_map/all_gather | solution.py:129
  350.2 4.3 copy-start.6
  354.5 5.3 copy-start.11
  354.5 5.3 copy-start.12
  354.5 5.3 copy-start.9
  354.6 5.3 copy-start.10
  356.8 212.0 %copy-start.7 = (f32[1,72,256]{2,1,0:T(8,128)S(1)}, f32[1,72,256]{2,1,0:T(8,128)}, u32[]{:S(2)}) copy-start(f32[1,72,256]{2,1,0:T(8,128)} %param.50) | copy-start | bytes 221188
  356.8 223.3 %copy-start.8 = (f32[1,72,256]{2,1,0:T(8,128)S(1)}, f32[1,72,256]{2,1,0:T(8,128)}, u32[]{:S(2)}) copy-start(f32[1,72,256]{2,1,0:T(8,128)} %param.51) | copy-start | bytes 221188
  569.8 10.4 %collective-permute-start.1 = (f32[72,256]{1,0:T(8,128)S(1)}, f32[72,256]{1,0:T(8,128)}, u32[]{:S(2)}, u32[]{:S(2)}) collective-permute-start(f32[72,256]{1,0:T(8,128)S(1)} %param.35), channel_id=1, source_target_pairs={{0,64},{32,96},{64,0},{96,32},{128,192},{160,224},{192,128},{224,1... | collective-permute-start | bytes 221192 | tf_op jit(solution)/shard_map/cond/branch_1_fun/ppermute | solution.py:12
Sparse Core Ops, SparseCore 0:
  10.6 149.5 all-gather.5
  162.9 151.9 all-gather.3
  335.2 156.3 reduce-scatter.1
  494.2 156.6 all-gather.7
where the time goes:
time: 681 us; the launch traced here: 671 us
  waiting for transfers between devices  360 us (53%)
  blocking collectives  217 us (32%)
  local copies, waits for them, and re-layouts  38.9 us (6%)
  matrix products  22 us (3%)
  between operations  16.7 us (2%)
  other arithmetic  11.2 us (2%)
    all_gather x1, waiting for transfers between devices, body(): strips_in = lax.all_gather(edge_strips(block), 'tile', axis=0, tiled=True)  150 us
    all_gather x1, waiting for transfers between devices, body(): gathered = lax.all_gather(w_scaled, 'tile', axis=0, tiled=True)  75.9 us
    psum x1, blocking collectives, body(): square_sum = lax.psum(jnp.sum(kernel_grad * kernel_grad), 'tile')  74.9 us
    all_gather x1, blocking collectives, body(): corners_in = lax.all_gather(corner_grads, 'tile', axis=0, tiled=True)  71.7 us
    all_gather x1, blocking collectives, body(): cells_in = lax.all_gather(corner_cells(block), 'tile', axis=0, tiled=True)  70.8 us
    all_gather x1, waiting for transfers between devices, body(): sides_in = lax.all_gather(side_grads, 'tile', axis=0, tiled=True)  69.2 us
    reduce_scatter x1, waiting for transfers between devices, body(): lax.psum_scatter(jnp.stack(pieces, axis=1).reshape(row_count, channels),...  59.5 us
    scatter-add x7, local copies, waits for them, and re-layouts, body(): grad_pad.at[:, row_off:row_off + side_len, col_off:col_off + side_len]  13.6 us
  transfers between devices with their start and end apart: 5, of which 5 were waited for; matrix products, arithmetic and copies ran while one was open for 5% of the time, Pallas kernels for 0%

commit v1 on v0

v1 whole, which is shorter than its diff:
```python
import jax
import jax.numpy as jnp
from jax import lax
from jax.experimental import pallas as pl
from jax.experimental.pallas import tpu as pltpu
from jax.sharding import PartitionSpec as P

LEARN = 0.5
STRIPS = 5
HALO = STRIPS + 1
F32 = jnp.float32
BF16 = jnp.bfloat16
SMEM = pltpu.SMEM


def rows_iota(shape):
    return lax.broadcasted_iota(jnp.int32, shape, len(shape) - 2)


def pick_row(group, row):
    return jnp.sum(jnp.where(rows_iota(group.shape) == row, group, 0.0), axis=0, keepdims=True)


def count_bits(v):
    v = v - ((v >> 1) & 0x55555555)
    v = (v & 0x33333333) + ((v >> 2) & 0x33333333)
    v = (v + (v >> 4)) & 0x0F0F0F0F
    return (v * 0x01010101) >> 24


def link_of(entry):
    return entry & 255


def code_of(entry):
    return (entry >> 8) & 3


def slot_of(entry):
    return (entry >> 10) & 31


def owner_of(entry):
    return entry >> 16


def build_routes(me, links, codes, route, masks, base, per, width):
    def clear(d, c):
        masks[d] = 0
        return c

    lax.fori_loop(0, width + 1, clear, 0)

    def owner_and_bit(k):
        tile = me * per + (k >> 2)
        link = links[k & 3, tile]
        code = codes[k & 3, tile]
        owner = jnp.where(link < 0, width, (link * 10923) >> 16)
        bit = jnp.where(me < owner, k, (link - owner * per) * 4 + code)
        bit = jnp.where(link < 0, 0, bit)
        return link, code, owner, bit

    def mark(k, c):
        _, _, owner, bit = owner_and_bit(k)
        masks[owner] = masks[owner] | (1 << bit)
        return c

    lax.fori_loop(0, 4 * per, mark, 0)

    def number(k, c):
        link, code, owner, bit = owner_and_bit(k)
        slot = count_bits(masks[owner] & ((1 << bit) - 1))
        route[base + k] = (link & 255) | (code << 8) | (slot << 10) | (owner << 16)
        return c

    lax.fori_loop(0, 4 * per, number, 0)


def pack_kernel(me_ref, tl, tc, cl, cc, field, rows, send, strips, route, masks, taps, low, high):
    per, side = field.shape[0], field.shape[1]
    width = send.shape[0]
    entries = 4 * per
    me = me_ref[0]
    build_routes(me, tl, tc, route, masks, 0, per, width)
    build_routes(me, cl, cc, route, masks, entries, per, width)
    scale = (9.0 * rows.shape[1]) ** (-0.5)
    half = rows.shape[1] // 2
    for n, part in enumerate((low, high)):
        part[...] = rows[:, n * half : (n + 1) * half]
    for tap in range(9):
        picked = [part[pl.ds(tap, 8, stride=9), :] for part in (low, high)]
        taps[tap] = (jnp.concatenate(picked, axis=1) * scale).astype(BF16)
    zero = jnp.zeros(taps.shape[1:], BF16)

    def spread(d, c):
        send[d, pl.ds(0, 9)] = taps[...]
        send[d, 9 + STRIPS] = zero
        return c

    lax.fori_loop(0, width, spread, 0)

    def edges(t, c):
        strips[t, 0] = field[t, 0]
        strips[t, 1] = field[t, side - 1]
        shape = (side, field.shape[3])
        where = rows_iota(shape)
        left = jnp.zeros(shape, F32)
        right = jnp.zeros(shape, F32)
        for i in range(side):
            x = field[t, i].astype(F32)
            left = jnp.where(where == i, jnp.broadcast_to(x[0:1], shape), left)
            right = jnp.where(where == i, jnp.broadcast_to(x[side - 1 : side], shape), right)
        strips[t, 2] = left.astype(BF16)
        strips[t, 3] = right.astype(BF16)
        return c

    lax.fori_loop(0, per, edges, 0)

    def place(k, c):
        entry = route[k]

        @pl.when(owner_of(entry) != me)
        def _():
            send[owner_of(entry), 9 + slot_of(entry)] = strips[k >> 2, k & 3]

        corner = route[entries + k]
        owner = owner_of(corner)

        @pl.when((owner != me) & (owner < width))
        def _():
            q = k & 3
            cell = pick_row(strips[k >> 2, q >> 1].astype(F32), (q & 1) * (side - 1))
            old = send[owner, 9 + STRIPS].astype(F32)
            new = jnp.where(rows_iota(old.shape) == slot_of(corner), cell, old)
            send[owner, 9 + STRIPS] = new.astype(BF16)

        return c

    lax.fori_loop(0, entries, place, 0)


def conv_kernel(
    me_ref, route, field, strips, cot, recv, act, send, inner, own_sides, own_corners,
    pad0, pad1, pad2, taps, dpre, acc0, acc1, acc2,
):
    per, side = field.shape[0], field.shape[1]
    width, chans = recv.shape[0], field.shape[3]
    entries = 4 * per
    pairs = per // 2
    me = me_ref[0]
    where = rows_iota((side, chans))

    def near(owner, link, code, slot):
        mine = owner == me
        here = strips[jnp.where(mine, link - me * per, 0), code]
        there = recv[jnp.where(mine, 0, owner), 9 + jnp.where(mine, 0, slot)]
        return jnp.where(mine, here.astype(F32), there.astype(F32))

    def halo(p, c):
        tops, bottoms, lefts, rights, cells = [], [], [], [], []
        for h in range(2):
            t = 2 * p + h
            sides = []
            for e in range(4):
                entry = route[t * 4 + e]
                sides.append(
                    near(owner_of(entry), link_of(entry), code_of(entry), slot_of(entry))
                )
            corner_rows = []
            for q in range(4):
                entry = route[entries + t * 4 + q]
                owner = owner_of(entry)
                mine = owner == me
                lost = owner >= width
                code = code_of(entry)
                here = strips[jnp.where(mine, link_of(entry) - me * per, 0), code >> 1]
                there = recv[jnp.where(mine | lost, 0, owner), 9 + STRIPS]
                group = jnp.where(mine, here.astype(F32), there.astype(F32))
                row = jnp.where(mine, (code & 1) * (side - 1), slot_of(entry))
                row = jnp.where(lost, -1, row)
                corner_rows.append(pick_row(group, row))
            tops.append(sides[0])
            bottoms.append(sides[1])
            lefts.append(sides[2])
            rights.append(sides[3])
            cells.append(corner_rows)
        for r in range(side + 2):
            shifted = ([], [], [])
            for h in range(2):
                if r == 0:
                    x, before, after = tops[h], cells[h][0], cells[h][1]
                elif r == side + 1:
                    x, before, after = bottoms[h], cells[h][2], cells[h][3]
                else:
                    x = field[2 * p + h, r - 1].astype(F32)
                    before, after = lefts[h][r - 1 : r], rights[h][r - 1 : r]
                shifted[0].append(jnp.where(where == 0, before, pltpu.roll(x, 1, 0)))
                shifted[1].append(x)
                shifted[2].append(jnp.where(where == side - 1, after, pltpu.roll(x, side - 1, 0)))
            for pad, halves in zip((pad0, pad1, pad2), shifted):
                pad[p, r] = jnp.concatenate(halves, axis=0).astype(BF16)
        return c

    lax.fori_loop(0, pairs, halo, 0)
    for tap in range(9):
        taps[tap] = recv[:, tap].astype(F32).reshape(chans, chans).astype(BF16)

    pads = (pad0, pad1, pad2)
    cells = per * side * side

    def window(tap):
        a, b = divmod(tap, 3)
        return pads[b][:, a : a + side].reshape(cells, chans)

    pre = jnp.zeros((cells, chans), F32)
    for tap in range(9):
        pre = pre + jnp.dot(window(tap), taps[tap], preferred_element_type=F32)
    gate = jax.nn.sigmoid(pre)
    out = (pre * gate).reshape(pairs, side, 2, side, chans)
    slope = (gate * (1.0 + pre * (1.0 - gate))).reshape(pairs, side, 2, side, chans)
    for p in range(pairs):
        for h in range(2):
            act[2 * p + h] = out[p, :, h].astype(BF16)
        grads = [
            cot[2 * p + h].astype(F32) * slope[p, :, h] for h in range(2)
        ]
        for i in range(side):
            dpre[p, i] = jnp.concatenate([grads[0][i], grads[1][i]], axis=0).astype(BF16)
    flat = dpre[...].reshape(cells, chans)
    for tap in range(9):
        part = lax.dot_general(
            window(tap), flat, (((0,), (0,)), ((), ())), preferred_element_type=F32
        )
        high = part.astype(BF16)
        low = part - high.astype(F32)
        send[:, HALO + 2 * tap] = part.reshape(width, 8, chans).astype(BF16)
        send[:, HALO + 2 * tap + 1] = low.reshape(width, 8, chans).astype(BF16)
    accs = (acc0, acc1, acc2)
    for acc in accs:
        acc[...] = jnp.zeros_like(acc)
    for tap in range(9):
        a, b = divmod(tap, 3)
        back = lax.dot_general(
            flat, taps[tap], (((1,), (1,)), ((), ())), preferred_element_type=F32
        )
        accs[b][:, a : a + side] += back.reshape(pairs, side, 2 * side, chans)

    def clear(d, c):
        send[d, STRIPS] = jnp.zeros((8, chans), BF16)
        return c

    lax.fori_loop(0, width, clear, 0)

    def borders(p, c):
        for h in range(2):
            t = 2 * p + h
            span = slice(h * side, (h + 1) * side)
            left = jnp.zeros((side, chans), F32)
            right = jnp.zeros((side, chans), F32)
            corner = jnp.zeros((side, chans), F32)
            for r in range(side + 2):
                q0, q1, q2 = (acc[p, r, span] for acc in accs)
                up = jnp.where(where == side - 1, 0.0, pltpu.roll(q0, side - 1, 0))
                down = jnp.where(where == 0, 0.0, pltpu.roll(q2, 1, 0))
                mid = up + q1 + down
                first = jnp.broadcast_to(q0[0:1], (side, chans))
                last = jnp.broadcast_to(q2[side - 1 : side], (side, chans))
                if r == 0 or r == side + 1:
                    e = 0 if r == 0 else 1
                    own_sides[t, e] = mid.astype(BF16)
                    corner = jnp.where(where == 2 * e, first, corner)
                    corner = jnp.where(where == 2 * e + 1, last, corner)
                else:
                    inner[t, r - 1] = mid
                    left = jnp.where(where == r - 1, first, left)
                    right = jnp.where(where == r - 1, last, right)
            own_sides[t, 2] = left.astype(BF16)
            own_sides[t, 3] = right.astype(BF16)
            own_corners[t] = corner.astype(BF16)
        return c

    lax.fori_loop(0, pairs, borders, 0)

    def place(k, c):
        entry = route[k]

        @pl.when(owner_of(entry) != me)
        def _():
            send[owner_of(entry), slot_of(entry)] = own_sides[k >> 2, k & 3]

        corner = route[entries + k]
        owner = owner_of(corner)

        @pl.when((owner != me) & (owner < width))
        def _():
            cell = pick_row(own_corners[k >> 2].astype(F32), k & 3)
            old = send[owner, STRIPS].astype(F32)
            new = jnp.where(rows_iota(old.shape) == slot_of(corner), cell, old)
            send[owner, STRIPS] = new.astype(BF16)

        return c

    lax.fori_loop(0, entries, place, 0)


def sum_kernel(recv, rows, squares, total):
    step = pl.program_id(0)
    here = recv.shape[1] // 2

    @pl.when(step == 0)
    def _():
        total[...] = jnp.zeros_like(total)

    for j in range(here):
        g = jnp.sum(recv[:, 2 * j].astype(F32) + recv[:, 2 * j + 1].astype(F32), axis=0)
        rows[step * here + j] = g
        total[...] += g * g
    squares[...] = jnp.full(squares.shape, jnp.sum(total[...]), F32)


def grad_kernel(me_ref, route, inner, own_sides, own_corners, recv, out):
    per, side, chans = inner.shape[0], inner.shape[1], inner.shape[3]
    width = recv.shape[0]
    entries = 4 * per
    me = me_ref[0]
    where = rows_iota((side, chans))

    def tile(t, c):
        sides = []
        for e in range(4):
            entry = route[t * 4 + e]
            owner = owner_of(entry)
            mine = owner == me
            here = own_sides[jnp.where(mine, link_of(entry) - me * per, 0), code_of(entry)]
            there = recv[jnp.where(mine, 0, owner), jnp.where(mine, 0, slot_of(entry))]
            sides.append(jnp.where(mine, here.astype(F32), there.astype(F32)))
        cells = []
        for q in range(4):
            entry = route[entries + t * 4 + q]
            owner = owner_of(entry)
            mine = owner == me
            lost = owner >= width
            here = own_corners[jnp.where(mine, link_of(entry) - me * per, 0)]
            there = recv[jnp.where(mine | lost, 0, owner), STRIPS]
            group = jnp.where(mine, here.astype(F32), there.astype(F32))
            row = jnp.where(lost, -1, jnp.where(mine, code_of(entry), slot_of(entry)))
            cells.append(pick_row(group, row))
        for i in range(side):
            x = inner[t, i]
            if i == 0:
                x = x + sides[0]
            if i == side - 1:
                x = x + sides[1]
            first, last = sides[2][i : i + 1], sides[3][i : i + 1]
            x = x + jnp.where(where == 0, first, jnp.where(where == side - 1, last, 0.0))
            if i == 0 or i == side - 1:
                q = 0 if i == 0 else 2
                x = x + jnp.where(
                    where == 0, cells[q], jnp.where(where == side - 1, cells[q + 1], 0.0)
                )
            out[t, i] = x.astype(BF16)
        return c

    lax.fori_loop(0, per, tile, 0)


def body(
    fields, cotangent, weights, ema, tile_links, tile_codes, corner_links, corner_codes,
    gossip_bit, batch_size,
):
    field, cot, w = fields[0], cotangent[0], weights[0]
    per, side, chans = field.shape[0], field.shape[1], field.shape[3]
    width = lax.axis_size("tile")
    reps = lax.axis_size("rep")
    entries = 4 * per
    me = lax.axis_index("tile").astype(jnp.int32).reshape(1)
    smem = pl.BlockSpec(memory_space=SMEM)
    vmem = pl.BlockSpec(memory_space=pltpu.VMEM)
    sds = jax.ShapeDtypeStruct

    def swap(value, bit):
        pairs = [(i, i ^ (1 << bit)) for i in range(reps)]
        return lax.ppermute(value, "rep", pairs)

    def partner(value):
        return jnp.where(gossip_bit[0] == 0, swap(value, 0), swap(value, 1))

    w_partner = partner(w)

    send, strips, route = pl.pallas_call(
        pack_kernel,
        name="pack",
        out_shape=(
            sds((width, 9 + HALO, 8, chans), BF16),
            sds((per, 4, side, chans), BF16),
            sds((2 * entries,), jnp.int32),
        ),
        in_specs=[smem] * 5 + [vmem] * 2,
        out_specs=(vmem, vmem, smem),
        scratch_shapes=[
            SMEM((width + 1,), jnp.int32),
            pltpu.VMEM((9, 8, chans), BF16),
            pltpu.VMEM((72, chans // 2), F32),
            pltpu.VMEM((72, chans // 2), F32),
        ],
    )(me, tile_links.T, tile_codes.T, corner_links.T, corner_codes.T, field, w)

    recv = lax.all_to_all(send, "tile", 0, 0, tiled=True)

    pad = pltpu.VMEM((per // 2, side + 2, 2 * side, chans), BF16)
    acc = pltpu.VMEM((per // 2, side + 2, 2 * side, chans), F32)
    act, send, inner, own_sides, own_corners = pl.pallas_call(
        conv_kernel,
        name="conv",
        out_shape=(
            sds((per, side, side, chans), BF16),
            sds((width, HALO + 18, 8, chans), BF16),
            sds((per, side, side, chans), F32),
            sds((per, 4, side, chans), BF16),
            sds((per, 8, chans), BF16),
        ),
        in_specs=[smem] * 2 + [vmem] * 4,
        out_specs=(vmem,) * 5,
        scratch_shapes=[
            pad, pad, pad,
            pltpu.VMEM((9, chans, chans), BF16),
            pltpu.VMEM((per // 2, side, 2 * side, chans), BF16),
            acc, acc, acc,
        ],
    )(me, route, field, strips, cot, recv)

    recv = lax.all_to_all(send, "tile", 0, 0, tiled=True)

    grouped, squares = pl.pallas_call(
        sum_kernel,
        name="sum",
        grid=(3,),
        out_shape=(sds((9, 8, chans), F32), sds((width, 1, 128), F32)),
        in_specs=[pl.BlockSpec((width, 6, 8, chans), lambda i: (0, i + 1, 0, 0))],
        out_specs=(
            pl.BlockSpec((9, 8, chans), lambda i: (0, 0, 0)),
            pl.BlockSpec((width, 1, 128), lambda i: (0, 0, 0)),
        ),
        scratch_shapes=[pltpu.VMEM((8, chans), F32)],
    )(recv)
    g_partner = partner(grouped)
    total = jnp.sum(lax.all_to_all(squares, "tile", 0, 0, tiled=True)[:, 0, :], axis=0)
    total_partner = partner(total)

    field_grad = pl.pallas_call(
        grad_kernel,
        name="grad",
        grid=(1,),
        out_shape=sds((per, side, side, chans), BF16),
        in_specs=[smem] * 2
        + [vmem] * 3
        + [pl.BlockSpec((width, HALO, 8, chans), lambda i: (0, 0, 0, 0))],
        out_specs=vmem,
    )(me, route, inner, own_sides, own_corners, recv)

    def ordered(value):
        return value.transpose(1, 0, 2).reshape(72, chans)

    def rms(value):
        return jnp.sqrt(value[0] / (9.0 * chans * chans) + 1e-06)

    updated = w - LEARN * ordered(grouped) / rms(total)
    updated_partner = w_partner - LEARN * ordered(g_partner) / rms(total_partner)
    averaged = 0.5 * (updated + updated_partner)
    decay = jnp.power(0.99, batch_size[0].astype(F32) / 32.0)
    ema_out = decay * ema[0] + (1.0 - decay) * averaged
    return act[None], field_grad[None], averaged[None], ema_out[None]


def solution(mesh):
    tiles = P("rep", "tile", None, None, None)
    rows = P("rep", "tile", None)
    return jax.shard_map(
        body,
        mesh=mesh,
        in_specs=(tiles, tiles, rows, rows) + (P(),) * 6,
        out_specs=(tiles, tiles, rows, rows),
        check_vma=False,
    )
```

time: 681 us -> 198 us (0.29); the launches traced: 671 us -> 197 us
  waiting for transfers between devices: 360 us -> 6.87 us
  blocking collectives: 217 us -> 139 us
  local copies, waits for them, and re-layouts: 38.9 us -> 0.1 us
  starting transfers between devices: 5.42 us -> 28.6 us
  matrix products: 22 us -> 0 us
  Pallas kernels: 0 us -> 19.1 us
  between operations: 16.7 us -> 2.32 us
  other arithmetic: 11.2 us -> 1.39 us
    all_gather x3 -> x0, waiting for transfers between devices: 295 us -> none  [the longest x1 150 us: body(): strips_in = lax.all_gather(edge_strips(block), 'tile', axis=0, tiled=True)]
    all_gather x2 -> x0, blocking collectives: 143 us -> none  [the longest x1 71.7 us: body(): corners_in = lax.all_gather(corner_grads, 'tile', axis=0, tiled=True)]
    all_to_all x0 -> x2, blocking collectives: none -> 139 us  [body(): recv = lax.all_to_all(send, 'tile', 0, 0, tiled=True)]
    psum x1 -> x0, blocking collectives: 74.9 us -> none  [body(): square_sum = lax.psum(jnp.sum(kernel_grad * kernel_grad), 'tile')]
    reduce_scatter x1 -> x0, waiting for transfers between devices: 59.5 us -> none  [body(): lax.psum_scatter(jnp.stack(pieces, axis=1).reshape(row_count, channels),...]
    dot_general x31 -> x0, matrix products: 22 us -> none  [the longest x9 5.51 us: body(): jnp.dot(grad_pre, kernel[:, tap_index, :].T, preferred_element_type=jnp.f...]
    scatter-add x13 -> x0, local copies, waits for them, and re-layouts: 19.2 us -> none  [the longest x7 13.6 us: body(): grad_pad.at[:, row_off:row_off + side_len, col_off:col_off + side_len]]
    pallas_call x0 -> x4, Pallas kernels: none -> 19.1 us  [the longest x1 7.6 us: body(): pl.pallas_call(conv_kernel, name='conv', out_shape=(sds((per, side, side,...]
  transfers between devices with their start and end apart: 5 -> 7, of which waited for: 5 -> 1; matrix products, arithmetic and copies ran while one was open for 5% -> 0% of each run, Pallas kernels for 0% -> 1%
where the time goes in v1:
time: 198 us; the launch traced here: 197 us
  blocking collectives  139 us (70%)
  starting transfers between devices  28.6 us (14%)
  Pallas kernels  19.1 us (10%)
  waiting for transfers between devices  6.87 us (3%)
  between operations  2.32 us (1%)
    all_to_all x2, blocking collectives, body(): recv = lax.all_to_all(send, 'tile', 0, 0, tiled=True)  139 us
    ppermute x6, starting transfers between devices, swap(): return lax.ppermute(value, 'rep', pairs)  20.5 us
    all_to_all x1, starting transfers between devices, body(): lax.all_to_all(squares, 'tile', 0, 0, tiled=True)[:, 0, :]  8.08 us
    pallas_call x1, Pallas kernels, body(): pl.pallas_call(conv_kernel, name='conv', out_shape=(sds((per, side, side,...  7.6 us
    ppermute x6, waiting for transfers between devices, swap(): return lax.ppermute(value, 'rep', pairs)  6.87 us
    pallas_call x1, Pallas kernels, body(): pl.pallas_call(pack_kernel, name='pack', out_shape=(sds((width, 9 + HALO,...  5.71 us
  transfers between devices with their start and end apart: 7, of which 1 were waited for; matrix products, arithmetic and copies ran while one was open for 0% of the time, Pallas kernels for 1%

profile of v1, /device:TPU:56, one launch (start us, length us, event | category | flops | bytes accessed | tf_op | source)
XLA Modules:
  0.0 197.2 jit_solution(6942704364077292696)
XLA Ops:
  0.6 5.7 %pack.1 = (bf16[32,15,8,256]{3,2,1,0:T(8,128)(2,1)}, bf16[6,4,8,256]{3,2,1,0:T(8,128)(2,1)}, s32[48]{0:T(128)}) custom-call(s32[1]{0:T(128)} %bitcast.me_ref, s32[4,192]{1,0:T(4,128)} %bitcast.37, s32[4,192]{1,0:T(4,128)} %bitcast.38, s32[4,192]{1,0:T(4,128)} %bitcast.39, s32[4,192]{1,0:T(4,128)} %bitcast.40, bf16[6,8,8,256]{3,2,1,0:T(8,128)(2,1)} %bitcast.30, ...), custom_call_target="tpu_custom_call" | custom-call | tf_op jit(solution)/shard_map/pack/pallas_call | solution.py:390
  6.4 60.1 %all_to_all.15.recv = bf16[32,15,8,256]{3,2,1,0:T(8,128)(2,1)} all-to-all(bf16[32,15,8,256]{3,2,1,0:T(8,128)(2,1)} %get-tuple-element.16), channel_id=1, replica_groups=mesh['rep'=16,'tile'=32] {'tile'}, dimensions={0} | all-to-all | bytes 3932160 | tf_op jit(solution)/shard_map/all_to_all | solution.py:408
  66.4 7.6 %conv.1 = (bf16[6,8,8,256]{3,2,1,0:T(8,128)(2,1)}, bf16[32,24,8,256]{3,2,1,0:T(8,128)(2,1)}, f32[6,8,8,256]{3,2,1,0:T(8,128)}, bf16[6,4,8,256]{3,2,1,0:T(8,128)(2,1)}, bf16[6,8,256]{2,1,0:T(8,128)(2,1)}) custom-call(s32[1]{0:T(128)} %bitcast.me_ref, s32[48]{0:T(128)} %get-tuple-element.14.route, bf16[6,8,8,256]{3,2,1,0:T(8,128)(2,1)} %bitcast.31, ...), custom_call_target="tpu_custom_call" | custom-call | tf_op jit(solution)/shard_map/conv/pallas_call | solution.py:412
  74.0 78.7 %all_to_all.16.recv = bf16[32,24,8,256]{3,2,1,0:T(8,128)(2,1)} all-to-all(bf16[32,24,8,256]{3,2,1,0:T(8,128)(2,1)} %get-tuple-element.21), channel_id=1, replica_groups=mesh['rep'=16,'tile'=32] {'tile'}, dimensions={0} | all-to-all | bytes 6291456 | tf_op jit(solution)/shard_map/all_to_all | solution.py:432
  152.8 0.0 copy-start
  152.8 3.4 %sum.1 = (f32[9,8,256]{2,1,0:T(8,128)}, f32[32,1,128]{2,1,0:T(1,128)}) custom-call(bf16[32,24,8,256]{3,2,1,0:T(8,128)(2,1)} %all_to_all.16.recv), custom_call_target="tpu_custom_call" | custom-call | tf_op jit(solution)/shard_map/sum/pallas_call | solution.py:434
  156.2 0.0 copy-start.1
  156.2 0.0 copy-start.2
  156.2 8.1 %all-to-all-start.2 = ((f32[32,1,128]{2,1,0:T(1,128)}), f32[32,1,128]{2,1,0:T(1,128)S(1)}, u32[]{:S(2)}, u32[]{:S(2)}) async-start(f32[32,1,128]{2,1,0:T(1,128)} %get-tuple-element.23), calls=%async_computation.2 | async-start | bytes 32768 | tf_op jit(solution)/shard_map/all_to_all | solution.py:447
  164.2 0.0 copy-done
  164.3 1.9 collective-permute-start
  166.2 4.5 %collective-permute-start.1 = (f32[72,256]{1,0:T(8,128)S(1)}, f32[72,256]{1,0:T(8,128)S(1)}, u32[]{:S(2)}, u32[]{:S(2)}) collective-permute-start(f32[72,256]{1,0:T(8,128)S(1)} %bitcast.34), channel_id=1, source_target_pairs={{0,64},{32,96},{64,0},{96,32},{128,192},{160,224},{192,128},{224,1... | collective-permute-start | bytes 221192 | tf_op jit(solution)/shard_map/ppermute | solution.py:383
  172.0 2.1 %collective-permute-start.2 = (f32[9,8,256]{2,1,0:T(8,128)}, f32[9,8,256]{2,1,0:T(8,128)S(1)}, u32[]{:S(2)}, u32[]{:S(2)}) collective-permute-start(f32[9,8,256]{2,1,0:T(8,128)} %get-tuple-element.22), channel_id=1, source_target_pairs={{0,32},{32,0},{64,96},{96,64},{128,160},{160,128},{192,224},{224,1... | collective-permute-start | bytes 221192 | tf_op jit(solution)/shard_map/ppermute | solution.py:383
  174.2 2.4 %grad.1 = bf16[6,8,8,256]{3,2,1,0:T(8,128)(2,1)} custom-call(s32[1]{0:T(128)} %bitcast.me_ref, s32[48]{0:T(128)} %get-tuple-element.14.route, f32[6,8,8,256]{3,2,1,0:T(8,128)} %get-tuple-element.18.inner, bf16[6,4,8,256]{3,2,1,0:T(8,128)(2,1)} %get-tuple-element.19.own_sides, bf16[6,8,256]{2,1,0:T(8,128)(2,1)} %get-tuple-element.20.own_corners, ...), custom_call_target="tpu_custom_call" | custom-call | tf_op jit(solution)/shard_map/grad/pallas_call | solution.py:450
  176.6 0.0 all-to-all-done.2
  176.6 0.1 reduce_sum.9
  176.6 2.2 %collective-permute-start.4 = (f32[128]{0:T(128)S(1)}, f32[128]{0:T(128)S(1)}, u32[]{:S(2)}, u32[]{:S(2)}) collective-permute-start(f32[128]{0:T(128)S(1)} %reduce_sum.9), channel_id=1, source_target_pairs={{0,32},{32,0},{64,96},{96,64},{128,160},{160,128},{192,224},{224,1... | collective-permute-start | bytes 1544 | tf_op jit(solution)/shard_map/ppermute | solution.py:383
  178.8 5.2 %collective-permute-start.5 = (f32[128]{0:T(128)S(1)}, f32[128]{0:T(128)S(1)}, u32[]{:S(2)}, u32[]{:S(2)}) collective-permute-start(f32[128]{0:T(128)S(1)} %reduce_sum.9), channel_id=1, source_target_pairs={{0,64},{32,96},{64,0},{96,32},{128,192},{160,224},{192,128},{224,1... | collective-permute-start | bytes 1544 | tf_op jit(solution)/shard_map/ppermute | solution.py:383
  184.2 0.0 copy-done.1
  184.2 0.0 collective-permute-done.4
  184.3 4.5 %collective-permute-start.3 = (f32[9,8,256]{2,1,0:T(8,128)S(1)}, f32[9,8,256]{2,1,0:T(8,128)S(1)}, u32[]{:S(2)}, u32[]{:S(2)}) collective-permute-start(f32[9,8,256]{2,1,0:T(8,128)S(1)} %copy-done.1), channel_id=1, source_target_pairs={{0,64},{32,96},{64,0},{96,32},{128,192},{160,224},{192,128},{224,1... | collective-permute-start | bytes 221192 | tf_op jit(solution)/shard_map/ppermute | solution.py:383
  188.8 0.0 collective-permute-done.5
  188.9 0.0 collective-permute-done.2
  188.9 6.9 %collective-permute-done.3 = f32[9,8,256]{2,1,0:T(8,128)S(1)} collective-permute-done((f32[9,8,256]{2,1,0:T(8,128)S(1)}, f32[9,8,256]{2,1,0:T(8,128)S(1)}, u32[]{:S(2)}, u32[]{:S(2)}) %collective-permute-start.3) | collective-permute-done | bytes 73760 | tf_op jit(solution)/shard_map/ppermute | solution.py:383
  195.8 0.0 collective-permute-done
  195.8 0.0 collective-permute-done.1
  195.8 0.0 copy-done.2
  195.9 0.7 fusion
  196.5 0.6 multiply_bitcast_fusion
  (7 shorter events, 0.1 us)
Async XLA Ops:
  152.8 11.5 %copy-start = (f32[1,72,256]{2,1,0:T(8,128)S(1)}, f32[1,72,256]{2,1,0:T(8,128)}, u32[]{:S(2)}) copy-start(f32[1,72,256]{2,1,0:T(8,128)} %param.12) | copy-start | bytes 221188
  156.2 28.0 %copy-start.1 = (f32[9,8,256]{2,1,0:T(8,128)S(1)}, f32[9,8,256]{2,1,0:T(8,128)}, u32[]{:S(2)}) copy-start(f32[9,8,256]{2,1,0:T(8,128)} %get-tuple-element.22) | copy-start | bytes 221188
  156.2 39.7 %copy-start.2 = (f32[1,72,256]{2,1,0:T(8,128)S(1)}, f32[1,72,256]{2,1,0:T(8,128)}, u32[]{:S(2)}) copy-start(f32[1,72,256]{2,1,0:T(8,128)} %param.13) | copy-start | bytes 221188
  156.2 20.4 %all-to-all-start.2 = ((f32[32,1,128]{2,1,0:T(1,128)}), f32[32,1,128]{2,1,0:T(1,128)S(1)}, u32[]{:S(2)}, u32[]{:S(2)}) async-start(f32[32,1,128]{2,1,0:T(1,128)} %get-tuple-element.23), calls=%async_computation.2 | async-start | bytes 32768 | tf_op jit(solution)/shard_map/all_to_all | solution.py:447
  164.3 31.6 %collective-permute-start = (f32[72,256]{1,0:T(8,128)S(1)}, f32[72,256]{1,0:T(8,128)S(1)}, u32[]{:S(2)}, u32[]{:S(2)}) collective-permute-start(f32[72,256]{1,0:T(8,128)S(1)} %bitcast.33), channel_id=1, source_target_pairs={{0,32},{32,0},{64,96},{96,64},{128,160},{160,128},{192,224},{224,1... | collective-permute-start | bytes 221192 | tf_op jit(solution)/shard_map/ppermute | solution.py:383
  166.2 29.7 %collective-permute-start.1 = (f32[72,256]{1,0:T(8,128)S(1)}, f32[72,256]{1,0:T(8,128)S(1)}, u32[]{:S(2)}, u32[]{:S(2)}) collective-permute-start(f32[72,256]{1,0:T(8,128)S(1)} %bitcast.34), channel_id=1, source_target_pairs={{0,64},{32,96},{64,0},{96,32},{128,192},{160,224},{192,128},{224,1... | collective-permute-start | bytes 221192 | tf_op jit(solution)/shard_map/ppermute | solution.py:383
  172.0 16.8 %collective-permute-start.2 = (f32[9,8,256]{2,1,0:T(8,128)}, f32[9,8,256]{2,1,0:T(8,128)S(1)}, u32[]{:S(2)}, u32[]{:S(2)}) collective-permute-start(f32[9,8,256]{2,1,0:T(8,128)} %get-tuple-element.22), channel_id=1, source_target_pairs={{0,32},{32,0},{64,96},{96,64},{128,160},{160,128},{192,224},{224,1... | collective-permute-start | bytes 221192 | tf_op jit(solution)/shard_map/ppermute | solution.py:383
  176.6 7.6 %collective-permute-start.4 = (f32[128]{0:T(128)S(1)}, f32[128]{0:T(128)S(1)}, u32[]{:S(2)}, u32[]{:S(2)}) collective-permute-start(f32[128]{0:T(128)S(1)} %reduce_sum.9), channel_id=1, source_target_pairs={{0,32},{32,0},{64,96},{96,64},{128,160},{160,128},{192,224},{224,1... | collective-permute-start | bytes 1544 | tf_op jit(solution)/shard_map/ppermute | solution.py:383
  178.8 9.9 %collective-permute-start.5 = (f32[128]{0:T(128)S(1)}, f32[128]{0:T(128)S(1)}, u32[]{:S(2)}, u32[]{:S(2)}) collective-permute-start(f32[128]{0:T(128)S(1)} %reduce_sum.9), channel_id=1, source_target_pairs={{0,64},{32,96},{64,0},{96,32},{128,192},{160,224},{192,128},{224,1... | collective-permute-start | bytes 1544 | tf_op jit(solution)/shard_map/ppermute | solution.py:383
  184.3 11.5 %collective-permute-start.3 = (f32[9,8,256]{2,1,0:T(8,128)S(1)}, f32[9,8,256]{2,1,0:T(8,128)S(1)}, u32[]{:S(2)}, u32[]{:S(2)}) collective-permute-start(f32[9,8,256]{2,1,0:T(8,128)S(1)} %copy-done.1), channel_id=1, source_target_pairs={{0,64},{32,96},{64,0},{96,32},{128,192},{160,224},{192,128},{224,1... | collective-permute-start | bytes 221192 | tf_op jit(solution)/shard_map/ppermute | solution.py:383

commit v2 on v1

--- a/solution.py
+++ b/solution.py
@@ -4,6 +4,7 @@
 from jax.experimental import pallas as pl
 from jax.experimental.pallas import tpu as pltpu
 from jax.sharding import PartitionSpec as P
+
 
 LEARN = 0.5
 STRIPS = 5
@@ -76,28 +77,32 @@
     lax.fori_loop(0, 4 * per, number, 0)
 
 
-def pack_kernel(me_ref, tl, tc, cl, cc, field, rows, send, strips, route, masks, taps, low, high):
+def taps_kernel(rows, send, low, high):
+    scale = (9.0 * rows.shape[1]) ** (-0.5)
+    half = rows.shape[1] // 2
+    for n, part in enumerate((low, high)):
+        part[...] = rows[:, n * half : (n + 1) * half]
+    for tap in range(9):
+        picked = [part[pl.ds(tap, 8, stride=9), :] for part in (low, high)]
+        value = (jnp.concatenate(picked, axis=1) * scale).astype(BF16)
+        for n in range(send.shape[0]):
+            send[n, tap] = value
+
+
+def edge_kernel(me_ref, tl, tc, cl, cc, field, send, strips, route, masks):
     per, side = field.shape[0], field.shape[1]
     width = send.shape[0]
     entries = 4 * per
     me = me_ref[0]
     build_routes(me, tl, tc, route, masks, 0, per, width)
     build_routes(me, cl, cc, route, masks, entries, per, width)
-    scale = (9.0 * rows.shape[1]) ** (-0.5)
-    half = rows.shape[1] // 2
-    for n, part in enumerate((low, high)):
-        part[...] = rows[:, n * half : (n + 1) * half]
-    for tap in range(9):
-        picked = [part[pl.ds(tap, 8, stride=9), :] for part in (low, high)]
-        taps[tap] = (jnp.concatenate(picked, axis=1) * scale).astype(BF16)
-    zero = jnp.zeros(taps.shape[1:], BF16)
-
-    def spread(d, c):
-        send[d, pl.ds(0, 9)] = taps[...]
-        send[d, 9 + STRIPS] = zero
-        return c
-
-    lax.fori_loop(0, width, spread, 0)
+    zero = jnp.zeros(send.shape[2:], BF16)
+
+    def clear(d, c):
+        send[d, STRIPS] = zero
+        return c
+
+    lax.fori_loop(0, width, clear, 0)
 
     def edges(t, c):
         strips[t, 0] = field[t, 0]
@@ -121,7 +126,7 @@
 
         @pl.when(owner_of(entry) != me)
         def _():
-            send[owner_of(entry), 9 + slot_of(entry)] = strips[k >> 2, k & 3]
+            send[owner_of(entry), slot_of(entry)] = strips[k >> 2, k & 3]
 
         corner = route[entries + k]
         owner = owner_of(corner)
@@ -130,40 +135,78 @@
         def _():
             q = k & 3
             cell = pick_row(strips[k >> 2, q >> 1].astype(F32), (q & 1) * (side - 1))
-            old = send[owner, 9 + STRIPS].astype(F32)
+            old = send[owner, STRIPS].astype(F32)
             new = jnp.where(rows_iota(old.shape) == slot_of(corner), cell, old)
-            send[owner, 9 + STRIPS] = new.astype(BF16)
+            send[owner, STRIPS] = new.astype(BF16)
 
         return c
 
     lax.fori_loop(0, entries, place, 0)
 
 
-def conv_kernel(
-    me_ref, route, field, strips, cot, recv, act, send, inner, own_sides, own_corners,
-    pad0, pad1, pad2, taps, dpre, acc0, acc1, acc2,
+def seat(role, number):
+    y = 2 * (number >> 2) + (role >> 1)
+    z = 4 * ((number >> 1) & 1) + 2 * (number & 1) + (role & 1)
+    return 8 * y + z
+
+
+PEERS = [[seat(m, n) for n in range(8)] for m in range(4)]
+COLUMNS = 30
+GRADS = 42
+MESSAGE = 138
+
+
+def place_of(device):
+    y, z = divmod(device, 8)
+    return 2 * (y & 1) + (z & 1), 4 * (y >> 1) + 2 * (z >> 2) + ((z >> 1) & 1)
+
+
+def kernel_of(rows, tap):
+    parts = []
+    for device in range(32):
+        role, number = place_of(device)
+        parts.append(rows[role, number, tap].astype(F32))
+    return jnp.concatenate(parts, axis=0).astype(BF16)
+
+
+def role_of(me):
+    return 2 * ((me >> 3) & 1) + (me & 1)
+
+
+def forward_kernel(
+    me_ref, route, field, strips, cot, recv, rows0, rows1, rows2, rows3,
+    act, dpre, taps, message0, message1, message2, message3,
+    pad0, pad1, pad2, cols, rows, sems,
 ):
     per, side = field.shape[0], field.shape[1]
     width, chans = recv.shape[0], field.shape[3]
     entries = 4 * per
     pairs = per // 2
     me = me_ref[0]
+    role = role_of(me)
+    messages = (message0, message1, message2, message3)
+    copies = [
+        pltpu.make_async_copy(source, rows.at[role ^ k], sems.at[k])
+        for k, source in enumerate((rows0, rows1, rows2, rows3))
+    ]
+    for copy in copies:
+        copy.start()
     where = rows_iota((side, chans))
 
     def near(owner, link, code, slot):
         mine = owner == me
         here = strips[jnp.where(mine, link - me * per, 0), code]
-        there = recv[jnp.where(mine, 0, owner), 9 + jnp.where(mine, 0, slot)]
+        there = recv[jnp.where(mine, 0, owner), jnp.where(mine, 0, slot)]
         return jnp.where(mine, here.astype(F32), there.astype(F32))
 
     def halo(p, c):
-        tops, bottoms, lefts, rights, cells = [], [], [], [], []
+        sides, cells = [], []
         for h in range(2):
             t = 2 * p + h
-            sides = []
+            found = []
             for e in range(4):
                 entry = route[t * 4 + e]
-                sides.append(
+                found.append(
                     near(owner_of(entry), link_of(entry), code_of(entry), slot_of(entry))
                 )
             corner_rows = []
@@ -174,26 +217,30 @@
                 lost = owner >= width
                 code = code_of(entry)
                 here = strips[jnp.where(mine, link_of(entry) - me * per, 0), code >> 1]
-                there = recv[jnp.where(mine | lost, 0, owner), 9 + STRIPS]
+                there = recv[jnp.where(mine | lost, 0, owner), STRIPS]
                 group = jnp.where(mine, here.astype(F32), there.astype(F32))
                 row = jnp.where(mine, (code & 1) * (side - 1), slot_of(entry))
                 row = jnp.where(lost, -1, row)
                 corner_rows.append(pick_row(group, row))
-            tops.append(sides[0])
-            bottoms.append(sides[1])
-            lefts.append(sides[2])
-            rights.append(sides[3])
+            sides.append(found)
             cells.append(corner_rows)
+        for h in range(2):
+            for n in range(2):
+                column, above, below = sides[h][2 + n], cells[h][n], cells[h][2 + n]
+                upper = jnp.where(where == 0, above, pltpu.roll(column, 1, 0))
+                lower = jnp.where(where == 0, column[side - 1 : side], 0.0)
+                lower = jnp.where(where == 1, below, lower)
+                cols[n, p, h] = jnp.concatenate([upper, lower], axis=0).astype(BF16)
         for r in range(side + 2):
             shifted = ([], [], [])
             for h in range(2):
                 if r == 0:
-                    x, before, after = tops[h], cells[h][0], cells[h][1]
+                    x, before, after = sides[h][0], cells[h][0], cells[h][1]
                 elif r == side + 1:
-                    x, before, after = bottoms[h], cells[h][2], cells[h][3]
+                    x, before, after = sides[h][1], cells[h][2], cells[h][3]
                 else:
                     x = field[2 * p + h, r - 1].astype(F32)
-                    before, after = lefts[h][r - 1 : r], rights[h][r - 1 : r]
+                    before, after = sides[h][2][r - 1 : r], sides[h][3][r - 1 : r]
                 shifted[0].append(jnp.where(where == 0, before, pltpu.roll(x, 1, 0)))
                 shifted[1].append(x)
                 shifted[2].append(jnp.where(where == side - 1, after, pltpu.roll(x, side - 1, 0)))
@@ -202,39 +249,120 @@
         return c
 
     lax.fori_loop(0, pairs, halo, 0)
+
+    for copy in copies:
+        copy.wait()
     for tap in range(9):
-        taps[tap] = recv[:, tap].astype(F32).reshape(chans, chans).astype(BF16)
-
+        taps[tap] = kernel_of(rows, tap)
     pads = (pad0, pad1, pad2)
-    cells = per * side * side
-
-    def window(tap):
+    count = per * side * side
+
+    pre = jnp.zeros((count, chans), F32)
+    for tap in range(9):
         a, b = divmod(tap, 3)
-        return pads[b][:, a : a + side].reshape(cells, chans)
-
-    pre = jnp.zeros((cells, chans), F32)
-    for tap in range(9):
-        pre = pre + jnp.dot(window(tap), taps[tap], preferred_element_type=F32)
+        window = pads[b][:, a : a + side].reshape(count, chans)
+        pre = pre + jnp.dot(window, taps[tap], preferred_element_type=F32)
     gate = jax.nn.sigmoid(pre)
     out = (pre * gate).reshape(pairs, side, 2, side, chans)
     slope = (gate * (1.0 + pre * (1.0 - gate))).reshape(pairs, side, 2, side, chans)
+    half = chans // 2
     for p in range(pairs):
+        grads = []
         for h in range(2):
             act[2 * p + h] = out[p, :, h].astype(BF16)
-        grads = [
-            cot[2 * p + h].astype(F32) * slope[p, :, h] for h in range(2)
-        ]
+            grad = (cot[2 * p + h].astype(F32) * slope[p, :, h]).astype(BF16)
+            for n in range(2):
+                base = GRADS + (2 * h + n) * pairs * side + p * side
+                for message in messages:
+                    message[base : base + side] = grad[:, :, n * half : (n + 1) * half]
+            grads.append(grad.astype(F32))
         for i in range(side):
             dpre[p, i] = jnp.concatenate([grads[0][i], grads[1][i]], axis=0).astype(BF16)
-    flat = dpre[...].reshape(cells, chans)
+
+    lane = lax.broadcasted_iota(jnp.int32, (chans, chans), 1)
+    chan = 8 * seat(lane >> 6, (lane >> 3) & 7) + (lane & 7)
+    sort = (rows_iota((chans, chans)) == chan).astype(F32).astype(BF16)
+
+    def split(value, groups):
+        value = jnp.dot(value, sort, preferred_element_type=F32)
+        value = value.reshape(groups, 2, value.shape[0] // (2 * groups), chans)
+        parts = []
+        for m in range(4):
+            span = slice((m >> 1) * half, (m >> 1) * half + half)
+            first = value[:, 0, :, span].reshape(-1, half)
+            second = value[:, 1, :, span].reshape(-1, half)
+            low = lax.broadcasted_iota(jnp.int32, first.shape, 1) < half // 2
+            if m & 1:
+                first = pltpu.roll(first, half // 2, 1)
+            else:
+                second = pltpu.roll(second, half // 2, 1)
+            parts.append(jnp.where(low, first, second).reshape(-1, 8, half))
+        swapped = role & 1 == 1
+        parts = [jnp.where(swapped, parts[m ^ 1], parts[m]) for m in range(4)]
+        swapped = role >> 1 == 1
+        return [jnp.where(swapped, parts[m ^ 2], parts[m]).astype(BF16) for m in range(4)]
+
+    for message, part in zip(messages, split(pad1[...].reshape(-1, chans), pairs * (side + 2))):
+        message[0:COLUMNS] = part
+    for message, part in zip(messages, split(cols[...].reshape(-1, chans), 2 * pairs)):
+        message[COLUMNS:GRADS] = part
+
+
+def weight_kernel(block0, block1, block2, block3, send, win0, win1, win2, grads):
+    half = block0.shape[2]
+    pairs, side = 3, 8
+    where = rows_iota((side, half))
+
+    for couple, blocks in enumerate(((block0, block1), (block2, block3))):
+
+        def gather(p, c, couple=couple, blocks=blocks):
+            u = couple * pairs + p
+            for r in range(side + 2):
+                shifted = ([], [], [])
+                row = slice(r % 8, r % 8 + 1)
+                for block in blocks:
+                    x = block[p * (side + 2) + r].astype(F32)
+                    left = block[COLUMNS + 2 * p + r // 8].astype(F32)[row]
+                    right = block[COLUMNS + 2 * (p + pairs) + r // 8].astype(F32)[row]
+                    shifted[0].append(jnp.where(where == 0, left, pltpu.roll(x, 1, 0)))
+                    shifted[1].append(x)
+                    shifted[2].append(
+                        jnp.where(where == side - 1, right, pltpu.roll(x, side - 1, 0))
+                    )
+                for win, parts in zip((win0, win1, win2), shifted):
+                    win[u, r] = jnp.concatenate(parts, axis=0).astype(BF16)
+            for i in range(side):
+                for n in range(4):
+                    parts = [
+                        block[GRADS + (n * pairs + p) * side + i].astype(F32) for block in blocks
+                    ]
+                    value = jnp.concatenate(parts, axis=0).astype(BF16)
+                    grads[u, i, :, n * half : (n + 1) * half] = value
+            return c
+
+        lax.fori_loop(0, pairs, gather, 0)
+    flat = grads[...].reshape(-1, 4 * half)
+    wins = (win0, win1, win2)
+    quarter = half // 2
     for tap in range(9):
+        a, b = divmod(tap, 3)
+        window = wins[b][:, a : a + side].reshape(-1, half)
         part = lax.dot_general(
-            window(tap), flat, (((0,), (0,)), ((), ())), preferred_element_type=F32
+            window, flat, (((0,), (0,)), ((), ())), preferred_element_type=F32
         )
-        high = part.astype(BF16)
-        low = part - high.astype(F32)
-        send[:, HALO + 2 * tap] = part.reshape(width, 8, chans).astype(BF16)
-        send[:, HALO + 2 * tap + 1] = low.reshape(width, 8, chans).astype(BF16)
+        part = part[:quarter, : 2 * half] + part[quarter:, 2 * half :]
+        send[:, tap] = part.reshape(8, 8, 2 * half)
+
+
+def backward_kernel(
+    me_ref, route, dpre, taps, send, inner, own_sides, own_corners, acc0, acc1, acc2
+):
+    pairs, side, chans = dpre.shape[0], dpre.shape[1], dpre.shape[3]
+    width = send.shape[0]
+    entries = 8 * pairs
+    me = me_ref[0]
+    where = rows_iota((side, chans))
+    flat = dpre[...].reshape(2 * pairs * side * side, chans)
     accs = (acc0, acc1, acc2)
     for acc in accs:
         acc[...] = jnp.zeros_like(acc)
@@ -303,19 +431,47 @@
     lax.fori_loop(0, entries, place, 0)
 
 
-def sum_kernel(recv, rows, squares, total):
-    step = pl.program_id(0)
-    here = recv.shape[1] // 2
-
-    @pl.when(step == 0)
-    def _():
-        total[...] = jnp.zeros_like(total)
-
-    for j in range(here):
-        g = jnp.sum(recv[:, 2 * j].astype(F32) + recv[:, 2 * j + 1].astype(F32), axis=0)
-        rows[step * here + j] = g
-        total[...] += g * g
-    squares[...] = jnp.full(squares.shape, jnp.sum(total[...]), F32)
+def sum_kernel(recv, rows, squares):
+    g = recv[0]
+    for n in range(1, recv.shape[0]):
+        g = g + recv[n]
+    rows[...] = g
+    squares[...] = jnp.full(squares.shape, jnp.sum(g * g), F32)
+
+
+def final_kernel(
+    mine_ref, bit_ref, decay_ref, squares, w, g, w0, w1, g0, g1, ema, averaged, ema_out,
+    low, high,
+):
+    chans = w.shape[1]
+    half = chans // 2
+    mine = mine_ref[0]
+    bit = bit_ref[0]
+    decay = decay_ref[0]
+    flip = jnp.where(bit == 0, 1, 2)
+    number = lax.broadcasted_iota(jnp.int32, squares.shape, 0) // (squares.shape[0] // 4)
+
+    def rms(replica):
+        total = jnp.sum(jnp.where(number == replica, squares[...], 0.0), axis=0)
+        return jnp.sqrt(total / (9.0 * chans * chans) + 1e-06)
+
+    def ordered(value):
+        for n, part in enumerate((low, high)):
+            for tap in range(9):
+                part[pl.ds(tap, 8, stride=9), :] = value[tap][:, n * half : (n + 1) * half]
+        return low[...], high[...]
+
+    own_rms, other_rms = rms(mine), rms(mine ^ flip)
+    first = bit == 0
+    own = [x for x in ordered(g[...])]
+    other = [x for x in ordered(jnp.where(first, g0[...], g1[...]))]
+    for n in range(2):
+        span = slice(n * half, (n + 1) * half)
+        updated = w[:, span] - LEARN * own[n] / own_rms
+        partner = jnp.where(first, w0[:, span], w1[:, span]) - LEARN * other[n] / other_rms
+        mean = 0.5 * (updated + partner)
+        averaged[:, span] = mean
+        ema_out[:, span] = decay * ema[:, span] + (1.0 - decay) * mean
 
 
 def grad_kernel(me_ref, route, inner, own_sides, own_corners, recv, out):
@@ -379,96 +535,131 @@
     sds = jax.ShapeDtypeStruct
 
     def swap(value, bit):
-        pairs = [(i, i ^ (1 << bit)) for i in range(reps)]
-        return lax.ppermute(value, "rep", pairs)
-
-    def partner(value):
-        return jnp.where(gossip_bit[0] == 0, swap(value, 0), swap(value, 1))
-
-    w_partner = partner(w)
-
-    send, strips, route = pl.pallas_call(
-        pack_kernel,
-        name="pack",
+        return lax.ppermute(value, "rep", [(i, i ^ (1 << bit)) for i in range(reps)])
+
+    def exchange(value, groups=None, axis="tile"):
+        return lax.all_to_all(value, axis, 0, 0, axis_index_groups=groups, tiled=True)
+
+    def share(values):
+        got = []
+        for value, step in zip(values, (1, 8, 9)):
+            got.append(lax.ppermute(value, "tile", [(i, i ^ step) for i in range(width)]))
+        return got
+
+    w0, w1 = swap(w, 0), swap(w, 1)
+
+    rows = pl.pallas_call(
+        taps_kernel,
+        name="taps",
+        out_shape=sds((8, 9, 8, chans), BF16),
+        in_specs=[vmem],
+        out_specs=vmem,
+        scratch_shapes=[pltpu.VMEM((72, chans // 2), F32)] * 2,
+    )(w)
+    rows = exchange(rows, PEERS)
+
+    halo_send, strips, route = pl.pallas_call(
+        edge_kernel,
+        name="edge",
         out_shape=(
-            sds((width, 9 + HALO, 8, chans), BF16),
+            sds((width, HALO, 8, chans), BF16),
             sds((per, 4, side, chans), BF16),
             sds((2 * entries,), jnp.int32),
         ),
-        in_specs=[smem] * 5 + [vmem] * 2,
+        in_specs=[smem] * 5 + [vmem],
         out_specs=(vmem, vmem, smem),
-        scratch_shapes=[
-            SMEM((width + 1,), jnp.int32),
-            pltpu.VMEM((9, 8, chans), BF16),
-            pltpu.VMEM((72, chans // 2), F32),
-            pltpu.VMEM((72, chans // 2), F32),
-        ],
-    )(me, tile_links.T, tile_codes.T, corner_links.T, corner_codes.T, field, w)
-
-    recv = lax.all_to_all(send, "tile", 0, 0, tiled=True)
-
-    pad = pltpu.VMEM((per // 2, side + 2, 2 * side, chans), BF16)
-    acc = pltpu.VMEM((per // 2, side + 2, 2 * side, chans), F32)
-    act, send, inner, own_sides, own_corners = pl.pallas_call(
-        conv_kernel,
-        name="conv",
+        scratch_shapes=[SMEM((width + 1,), jnp.int32)],
+        cost_estimate=pl.CostEstimate(flops=1_000_000, bytes_accessed=8_000_000, transcendentals=0),
+    )(me, tile_links.T, tile_codes.T, corner_links.T, corner_codes.T, field)
+    halo = exchange(halo_send)
+    rows = [rows] + share([rows] * 3)
+
+    pairs = per // 2
+    pad = pltpu.VMEM((pairs, side + 2, 2 * side, chans), BF16)
+    acc = pltpu.VMEM((pairs, side + 2, 2 * side, chans), F32)
+    any_space = pl.BlockSpec(memory_space=pl.ANY)
+    message = sds((MESSAGE, 8, chans // 2), BF16)
+    act, dpre, taps, *messages = pl.pallas_call(
+        forward_kernel,
+        name="forward",
         out_shape=(
             sds((per, side, side, chans), BF16),
-            sds((width, HALO + 18, 8, chans), BF16),
+            sds((pairs, side, 2 * side, chans), BF16),
+            sds((9, chans, chans), BF16),
+            message, message, message, message,
+        ),
+        in_specs=[smem] * 2 + [vmem] * 4 + [any_space] * 4,
+        out_specs=(vmem,) * 7,
+        scratch_shapes=[
+            pad, pad, pad,
+            pltpu.VMEM((2, pairs, 2, 2 * side, chans), BF16),
+            pltpu.VMEM((4, 8, 9, 8, chans), BF16),
+            pltpu.SemaphoreType.DMA((4,)),
+        ],
+    )(me, route, field, strips, cot, halo, *rows)
+
+    blocks = [messages[0]] + share(messages[1:])
+
+    halo_send, inner, own_sides, own_corners = pl.pallas_call(
+        backward_kernel,
+        name="backward",
+        out_shape=(
+            sds((width, HALO, 8, chans), BF16),
             sds((per, side, side, chans), F32),
             sds((per, 4, side, chans), BF16),
             sds((per, 8, chans), BF16),
         ),
-        in_specs=[smem] * 2 + [vmem] * 4,
-        out_specs=(vmem,) * 5,
+        in_specs=[smem] * 2 + [vmem] * 2,
+        out_specs=(vmem,) * 4,
+        scratch_shapes=[acc, acc, acc],
+        cost_estimate=pl.CostEstimate(flops=500_000_000, bytes_accessed=8_000_000, transcendentals=0),
+    )(me, route, dpre, taps)
+    halo = exchange(halo_send)
+
+    win = pltpu.VMEM((6, side + 2, 2 * side, chans // 2), BF16)
+    parts = pl.pallas_call(
+        weight_kernel,
+        name="weight",
+        out_shape=sds((8, 9, 8, chans), F32),
+        in_specs=[vmem] * 4,
+        out_specs=vmem,
         scratch_shapes=[
-            pad, pad, pad,
-            pltpu.VMEM((9, chans, chans), BF16),
-            pltpu.VMEM((per // 2, side, 2 * side, chans), BF16),
-            acc, acc, acc,
+            win, win, win,
+            pltpu.VMEM((6, side, 2 * side, 2 * chans), BF16),
         ],
-    )(me, route, field, strips, cot, recv)
-
-    recv = lax.all_to_all(send, "tile", 0, 0, tiled=True)
-
-    grouped, squares = pl.pallas_call(
+    )(*blocks)
+    parts = exchange(parts, PEERS)
+
+    g, squares = pl.pallas_call(
         sum_kernel,
         name="sum",
-        grid=(3,),
-        out_shape=(sds((9, 8, chans), F32), sds((width, 1, 128), F32)),
-        in_specs=[pl.BlockSpec((width, 6, 8, chans), lambda i: (0, i + 1, 0, 0))],
-        out_specs=(
-            pl.BlockSpec((9, 8, chans), lambda i: (0, 0, 0)),
-            pl.BlockSpec((width, 1, 128), lambda i: (0, 0, 0)),
-        ),
-        scratch_shapes=[pltpu.VMEM((8, chans), F32)],
-    )(recv)
-    g_partner = partner(grouped)
-    total = jnp.sum(lax.all_to_all(squares, "tile", 0, 0, tiled=True)[:, 0, :], axis=0)
-    total_partner = partner(total)
+        out_shape=(sds((9, 8, chans), F32), sds((4 * width, 1, 128), F32)),
+        in_specs=[vmem],
+        out_specs=(vmem, vmem),
+    )(parts)
+    g0, g1 = swap(g, 0), swap(g, 1)
+    groups = [[r * width + i for i in range(4 * width)] for r in range(0, reps, 4)]
+    squares = exchange(squares, groups, ("rep", "tile"))
 
     field_grad = pl.pallas_call(
         grad_kernel,
         name="grad",
-        grid=(1,),
         out_shape=sds((per, side, side, chans), BF16),
-        in_specs=[smem] * 2
-        + [vmem] * 3
-        + [pl.BlockSpec((width, HALO, 8, chans), lambda i: (0, 0, 0, 0))],
+        in_specs=[smem] * 2 + [vmem] * 4,
         out_specs=vmem,
-    )(me, route, inner, own_sides, own_corners, recv)
-
-    def ordered(value):
-        return value.transpose(1, 0, 2).reshape(72, chans)
-
-    def rms(value):
-        return jnp.sqrt(value[0] / (9.0 * chans * chans) + 1e-06)
-
-    updated = w - LEARN * ordered(grouped) / rms(total)
-    updated_partner = w_partner - LEARN * ordered(g_partner) / rms(total_partner)
-    averaged = 0.5 * (updated + updated_partner)
-    decay = jnp.power(0.99, batch_size[0].astype(F32) / 32.0)
-    ema_out = decay * ema[0] + (1.0 - decay) * averaged
+        cost_estimate=pl.CostEstimate(flops=2_000_000, bytes_accessed=4_000_000, transcendentals=0),
+    )(me, route, inner, own_sides, own_corners, halo)
+
+    decay = jnp.power(0.99, batch_size.astype(F32) / 32.0)
+    mine = (lax.axis_index("rep").astype(jnp.int32) & 3).reshape(1)
+    averaged, ema_out = pl.pallas_call(
+        final_kernel,
+        name="final",
+        out_shape=(sds(w.shape, F32), sds(w.shape, F32)),
+        in_specs=[smem] * 3 + [vmem] * 8,
+        out_specs=(vmem, vmem),
+        scratch_shapes=[pltpu.VMEM((72, chans // 2), F32)] * 2,
+    )(mine, gossip_bit, decay, squares, w, g, w0, w1, g0, g1, ema[0])
     return act[None], field_grad[None], averaged[None], ema_out[None]
 
 

time: 198 us -> 180 us (0.909)
  the two profiles are of different devices: /device:TPU:56 before, /device:TPU:70 now
where the time goes in v2:
time: 180 us; the launch traced here: 179 us
  starting transfers between devices  60.3 us (34%)
  waiting for transfers between devices  59 us (33%)
  blocking collectives  27.9 us (16%)
  Pallas kernels  25.8 us (14%)
  local copies, waits for them, and re-layouts  3.34 us (2%)
  between operations  2.19 us (1%)
    ppermute x6, waiting for transfers between devices, share(): lax.ppermute(value, 'tile', [(i, i ^ step) for i in range(width)])  31.7 us
    all_to_all x4, starting transfers between devices, exchange(): lax.all_to_all(value, axis, 0, 0, axis_index_groups=groups, tiled=True)  28.1 us
    all_to_all x1, blocking collectives, exchange(): lax.all_to_all(value, axis, 0, 0, axis_index_groups=groups, tiled=True)  27.9 us
    all_to_all x4, waiting for transfers between devices, exchange(): lax.all_to_all(value, axis, 0, 0, axis_index_groups=groups, tiled=True)  22.7 us
    ppermute x6, starting transfers between devices, share(): lax.ppermute(value, 'tile', [(i, i ^ step) for i in range(width)])  18.4 us
    ppermute x4, starting transfers between devices, swap(): return lax.ppermute(value, 'rep', [(i, i ^ 1 << bit) for i in range(reps)])  13.8 us
    pallas_call x1, Pallas kernels, body(): pl.pallas_call(edge_kernel, name='edge', out_shape=(sds((width, HALO, 8,...  5.26 us
    pallas_call x1, Pallas kernels, body(): pl.pallas_call(forward_kernel, name='forward', out_shape=(sds((per, side,...  4.99 us
  transfers between devices with their start and end apart: 14, of which 9 were waited for; matrix products, arithmetic and copies ran while one was open for 0% of the time, Pallas kernels for 6%

profile of v2, /device:TPU:70, one launch (start us, length us, event | category | flops | bytes accessed | tf_op | source)
XLA Modules:
  0.0 178.6 jit_solution(1772789837520601418)
XLA Ops:
  0.6 1.6 taps.1
  2.3 11.4 %all-to-all-start.1 = ((bf16[8,9,8,256]{3,2,1,0:T(8,128)(2,1)}), bf16[8,9,8,256]{3,2,1,0:T(8,128)(2,1)S(1)}, u32[]{:S(2)}, u32[]{:S(2)}) async-start(bf16[8,9,8,256]{3,2,1,0:T(8,128)(2,1)} %taps.1), calls=%async_computation.1 | async-start | bytes 589824 | tf_op jit(solution)/shard_map/all_to_all | solution.py:541
  13.7 5.3 %edge.1 = (bf16[32,6,8,256]{3,2,1,0:T(8,128)(2,1)}, bf16[6,4,8,256]{3,2,1,0:T(8,128)(2,1)}, s32[48]{0:T(128)}) custom-call(s32[1]{0:T(128)} %bitcast.me_ref, s32[4,192]{1,0:T(4,128)} %bitcast.23, s32[4,192]{1,0:T(4,128)} %bitcast.24, s32[4,192]{1,0:T(4,128)} %bitcast.25, s32[4,192]{1,0:T(4,128)} %bitcast.26, bf16[6,8,8,256]{3,2,1,0:T(8,128)(2,1)} %bitcast.14), custom_call_target="tpu_custom_call" | custom-call | flops 1000000 | bytes 8000000 | tf_op jit(solution)/shard_map/edge/pallas_call | solution.py:561
  19.0 8.5 %all-to-all-done.1.rows0 = bf16[8,9,8,256]{3,2,1,0:T(8,128)(2,1)S(1)} async-done(((bf16[8,9,8,256]{3,2,1,0:T(8,128)(2,1)}), bf16[8,9,8,256]{3,2,1,0:T(8,128)(2,1)S(1)}, u32[]{:S(2)}, u32[]{:S(2)}) %all-to-all-start.1) | async-done | bytes 294944 | tf_op jit(solution)/shard_map/all_to_all | solution.py:541
  27.5 4.7 %all-to-all-start = ((bf16[32,6,8,256]{3,2,1,0:T(8,128)(2,1)}), bf16[32,6,8,256]{3,2,1,0:T(8,128)(2,1)S(1)}, u32[]{:S(2)}, u32[]{:S(2)}) async-start(bf16[32,6,8,256]{3,2,1,0:T(8,128)(2,1)} %get-tuple-element.24), calls=%async_computation | async-start | bytes 1572864 | tf_op jit(solution)/shard_map/all_to_all | solution.py:541
  32.3 2.1 %collective-permute-start = (bf16[8,9,8,256]{3,2,1,0:T(8,128)(2,1)S(1)}, bf16[8,9,8,256]{3,2,1,0:T(8,128)(2,1)S(1)}, u32[]{:S(2)}, u32[]{:S(2)}) collective-permute-start(bf16[8,9,8,256]{3,2,1,0:T(8,128)(2,1)S(1)} %all-to-all-done.1.rows0), channel_id=1, source_target_pairs={{0,1},{1,0},{2,3},{3,2},{4,5},{5,4},{6,7},{7,6},{8,9},{9,8},{10,11... | collective-permute-start | bytes 884744 | tf_op jit(solution)/shard_map/ppermute | solution.py:546
  34.4 3.7 %collective-permute-start.1 = (bf16[8,9,8,256]{3,2,1,0:T(8,128)(2,1)S(1)}, bf16[8,9,8,256]{3,2,1,0:T(8,128)(2,1)S(1)}, u32[]{:S(2)}, u32[]{:S(2)}) collective-permute-start(bf16[8,9,8,256]{3,2,1,0:T(8,128)(2,1)S(1)} %all-to-all-done.1.rows0), channel_id=1, source_target_pairs={{0,8},{1,9},{2,10},{3,11},{4,12},{5,13},{6,14},{7,15},{8,0},{9,1},... | collective-permute-start | bytes 884744 | tf_op jit(solution)/shard_map/ppermute | solution.py:546
  38.1 3.4 %collective-permute-start.2 = (bf16[8,9,8,256]{3,2,1,0:T(8,128)(2,1)S(1)}, bf16[8,9,8,256]{3,2,1,0:T(8,128)(2,1)S(1)}, u32[]{:S(2)}, u32[]{:S(2)}) collective-permute-start(bf16[8,9,8,256]{3,2,1,0:T(8,128)(2,1)S(1)} %all-to-all-done.1.rows0), channel_id=1, source_target_pairs={{0,9},{1,8},{2,11},{3,10},{4,13},{5,12},{6,15},{7,14},{8,1},{9,0},... | collective-permute-start | bytes 884744 | tf_op jit(solution)/shard_map/ppermute | solution.py:546
  41.5 21.4 %collective-permute-done.rows1 = bf16[8,9,8,256]{3,2,1,0:T(8,128)(2,1)S(1)} collective-permute-done((bf16[8,9,8,256]{3,2,1,0:T(8,128)(2,1)S(1)}, bf16[8,9,8,256]{3,2,1,0:T(8,128)(2,1)S(1)}, u32[]{:S(2)}, u32[]{:S(2)}) %collective-permute-start) | collective-permute-done | bytes 294944 | tf_op jit(solution)/shard_map/ppermute | solution.py:546
  64.0 5.0 %forward.1 = (bf16[6,8,8,256]{3,2,1,0:T(8,128)(2,1)}, bf16[3,8,16,256]{3,2,1,0:T(8,128)(2,1)}, bf16[9,256,256]{2,1,0:T(8,128)(2,1)}, bf16[138,8,128]{2,1,0:T(8,1...) custom-call(s32[1]{0:T(128)} %bitcast.me_ref, ...), custom_call_target="tpu_custom_call" | custom-call | tf_op jit(solution)/shard_map/forward/pallas_call | solution.py:582
  69.0 3.0 %collective-permute-start.3 = (bf16[138,8,128]{2,1,0:T(8,128)(2,1)}, bf16[138,8,128]{2,1,0:T(8,128)(2,1)S(1)}, u32[]{:S(2)}, u32[]{:S(2)}) collective-permute-start(bf16[138,8,128]{2,1,0:T(8,128)(2,1)} %get-tuple-element.33), channel_id=1, source_target_pairs={{0,1},{1,0},{2,3},{3,2},{4,5},{5,4},{6,7},{7,6},{8,9},{9,8},{10,11... | collective-permute-start | bytes 847880 | tf_op jit(solution)/shard_map/ppermute | solution.py:546
  72.0 3.3 %collective-permute-start.4 = (bf16[138,8,128]{2,1,0:T(8,128)(2,1)}, bf16[138,8,128]{2,1,0:T(8,128)(2,1)S(1)}, u32[]{:S(2)}, u32[]{:S(2)}) collective-permute-start(bf16[138,8,128]{2,1,0:T(8,128)(2,1)} %get-tuple-element.34), channel_id=1, source_target_pairs={{0,8},{1,9},{2,10},{3,11},{4,12},{5,13},{6,14},{7,15},{8,0},{9,1},... | collective-permute-start | bytes 847880 | tf_op jit(solution)/shard_map/ppermute | solution.py:546
  75.3 2.9 %collective-permute-start.5 = (bf16[138,8,128]{2,1,0:T(8,128)(2,1)}, bf16[138,8,128]{2,1,0:T(8,128)(2,1)S(1)}, u32[]{:S(2)}, u32[]{:S(2)}) collective-permute-start(bf16[138,8,128]{2,1,0:T(8,128)(2,1)} %get-tuple-element.35), channel_id=1, source_target_pairs={{0,9},{1,8},{2,11},{3,10},{4,13},{5,12},{6,15},{7,14},{8,1},{9,0},... | collective-permute-start | bytes 847880 | tf_op jit(solution)/shard_map/ppermute | solution.py:546
  78.3 1.2 collective-permute-done.3.block1
  79.4 4.3 %collective-permute-done.4.block2 = bf16[138,8,128]{2,1,0:T(8,128)(2,1)S(1)} collective-permute-done((bf16[138,8,128]{2,1,0:T(8,128)(2,1)}, bf16[138,8,128]{2,1,0:T(8,128)(2,1)S(1)}, u32[]{:S(2)}, u32[]{:S(2)}) %collective-permute-start.4) | collective-permute-done | bytes 282656 | tf_op jit(solution)/shard_map/ppermute | solution.py:546
  83.7 4.9 %collective-permute-done.5.block3 = bf16[138,8,128]{2,1,0:T(8,128)(2,1)S(1)} collective-permute-done((bf16[138,8,128]{2,1,0:T(8,128)(2,1)}, bf16[138,8,128]{2,1,0:T(8,128)(2,1)S(1)}, u32[]{:S(2)}, u32[]{:S(2)}) %collective-permute-start.5) | collective-permute-done | bytes 282656 | tf_op jit(solution)/shard_map/ppermute | solution.py:546
  89.3 3.5 %weight.1 = f32[8,9,8,256]{3,2,1,0:T(8,128)} custom-call(bf16[138,8,128]{2,1,0:T(8,128)(2,1)} %get-tuple-element.32.block0, bf16[138,8,128]{2,1,0:T(8,128)(2,1)} %copy-done.7, bf16[138,8,128]{2,1,0:T(8,128)(2,1)} %copy-done.8, bf16[138,8,128]{2,1,0:T(8,128)(2,1)} %copy-done.9), custom_call_target="tpu_custom_call" | custom-call | tf_op jit(solution)/shard_map/weight/pallas_call | solution.py:620
  92.8 27.9 %all_to_all.25.recv = f32[8,9,8,256]{3,2,1,0:T(8,128)} all-to-all(f32[8,9,8,256]{3,2,1,0:T(8,128)} %weight.1), channel_id=1, replica_groups={{0,2,4,6,16,18,20,22},{1,3,5,7,17,19,21,23},{8,10,12,14,24,26,28,30},{9..., dimensions={0} | all-to-all | bytes 1179648 | tf_op jit(solution)/shard_map/all_to_all | solution.py:541
  120.7 1.9 %sum.1 = (f32[9,8,256]{2,1,0:T(8,128)}, f32[128,1,128]{2,1,0:T(1,128)}) custom-call(f32[8,9,8,256]{3,2,1,0:T(8,128)} %all_to_all.25.recv), custom_call_target="tpu_custom_call" | custom-call | tf_op jit(solution)/shard_map/sum/pallas_call | solution.py:633
  122.6 7.0 %all-to-all-start.4 = ((f32[128,1,128]{2,1,0:T(1,128)}), f32[128,1,128]{2,1,0:T(1,128)S(1)}, u32[]{:S(2)}, u32[]{:S(2)}) async-start(f32[128,1,128]{2,1,0:T(1,128)} %get-tuple-element.36), calls=%async_computation.4 | async-start | bytes 131072 | tf_op jit(solution)/shard_map/all_to_all | solution.py:541
  129.6 4.2 %backward.1 = (bf16[32,6,8,256]{3,2,1,0:T(8,128)(2,1)}, f32[6,8,8,256]{3,2,1,0:T(8,128)}, bf16[6,4,8,256]{3,2,1,0:T(8,128)(2,1)}, bf16[6,8,256]{2,1,0:T(8,128)(2,1)}) custom-call(s32[1]{0:T(128)} %bitcast.me_ref, s32[48]{0:T(128)} %get-tuple-element.22.route, bf16[3,8,16,256]{3,2,1,0:T(8,128)(2,1)} %get-tuple-element.26.dpre, ...), custom_call_target="tpu_custom_call" | custom-call | flops 500000000 | bytes 8000000 | tf_op jit(solution)/shard_map/backward/pallas_call | solution.py:603
  133.8 7.0 %all-to-all-done.4.squares = f32[128,1,128]{2,1,0:T(1,128)S(1)} async-done(((f32[128,1,128]{2,1,0:T(1,128)}), f32[128,1,128]{2,1,0:T(1,128)S(1)}, u32[]{:S(2)}, u32[]{:S(2)}) %all-to-all-start.4) | async-done | bytes 65568 | tf_op jit(solution)/shard_map/all_to_all | solution.py:541
  140.8 4.9 %all-to-all-start.2 = ((bf16[32,6,8,256]{3,2,1,0:T(8,128)(2,1)}), bf16[32,6,8,256]{3,2,1,0:T(8,128)(2,1)S(1)}, u32[]{:S(2)}, u32[]{:S(2)}) async-start(bf16[32,6,8,256]{3,2,1,0:T(8,128)(2,1)} %get-tuple-element.31), calls=%async_computation.2 | async-start | bytes 1572864 | tf_op jit(solution)/shard_map/all_to_all | solution.py:541
  145.7 1.9 %collective-permute-start.6 = (f32[72,256]{1,0:T(8,128)S(1)}, f32[72,256]{1,0:T(8,128)S(1)}, u32[]{:S(2)}, u32[]{:S(2)}) collective-permute-start(f32[72,256]{1,0:T(8,128)S(1)} %bitcast.18), channel_id=1, source_target_pairs={{0,32},{32,0},{64,96},{96,64},{128,160},{160,128},{192,224},{224,1... | collective-permute-start | bytes 221192 | tf_op jit(solution)/shard_map/ppermute | solution.py:538
  147.6 3.9 %collective-permute-start.7 = (f32[72,256]{1,0:T(8,128)S(1)}, f32[72,256]{1,0:T(8,128)S(1)}, u32[]{:S(2)}, u32[]{:S(2)}) collective-permute-start(f32[72,256]{1,0:T(8,128)S(1)} %bitcast.19), channel_id=1, source_target_pairs={{0,64},{32,96},{64,0},{96,32},{128,192},{160,224},{192,128},{224,1... | collective-permute-start | bytes 221192 | tf_op jit(solution)/shard_map/ppermute | solution.py:538
  151.5 2.1 %collective-permute-start.8 = (f32[9,8,256]{2,1,0:T(8,128)S(1)}, f32[9,8,256]{2,1,0:T(8,128)S(1)}, u32[]{:S(2)}, u32[]{:S(2)}) collective-permute-start(f32[9,8,256]{2,1,0:T(8,128)S(1)} %copy-done.11), channel_id=1, source_target_pairs={{0,32},{32,0},{64,96},{96,64},{128,160},{160,128},{192,224},{224,1... | collective-permute-start | bytes 221192 | tf_op jit(solution)/shard_map/ppermute | solution.py:538
  153.6 5.9 %collective-permute-start.9 = (f32[9,8,256]{2,1,0:T(8,128)S(1)}, f32[9,8,256]{2,1,0:T(8,128)S(1)}, u32[]{:S(2)}, u32[]{:S(2)}) collective-permute-start(f32[9,8,256]{2,1,0:T(8,128)S(1)} %copy-done.11), channel_id=1, source_target_pairs={{0,64},{32,96},{64,0},{96,32},{128,192},{160,224},{192,128},{224,1... | collective-permute-start | bytes 221192 | tf_op jit(solution)/shard_map/ppermute | solution.py:538
  160.9 3.6 %collective-permute-done.7.w1 = f32[72,256]{1,0:T(8,128)S(1)} collective-permute-done((f32[72,256]{1,0:T(8,128)S(1)}, f32[72,256]{1,0:T(8,128)S(1)}, u32[]{:S(2)}, u32[]{:S(2)}) %collective-permute-start.7) | collective-permute-done | bytes 73760 | tf_op jit(solution)/shard_map/ppermute | solution.py:538
  164.5 1.0 collective-permute-done.9.g1
  166.1 2.0 %final.1 = (f32[72,256]{1,0:T(8,128)}, f32[72,256]{1,0:T(8,128)}) custom-call(s32[1]{0:T(128)} %bitcast.10.mine_ref, s32[1]{0:T(128)S(6)} %copy.14.bit_ref, f32[1]{0:T(128)S(6)} %pow.3.decay_ref, f32[128,1,128]{2,1,0:T(1,128)} %copy-done.10, f32[72,256]{1,0:T(8,128)} %bitcast.17, f32[9,8,256]{2,1,0:T(8,128)} %get-tuple-element.37.g, f32[72,256]{1,0:T(8,128)} %copy-done.12, ...), custom_call_target="tpu_custom_call" | custom-call | tf_op jit(solution)/shard_map/final/pallas_call | solution.py:655
  168.1 7.2 %all-to-all-done.2.recv = bf16[32,6,8,256]{3,2,1,0:T(8,128)(2,1)S(1)} async-done(((bf16[32,6,8,256]{3,2,1,0:T(8,128)(2,1)}), bf16[32,6,8,256]{3,2,1,0:T(8,128)(2,1)S(1)}, u32[]{:S(2)}, u32[]{:S(2)}) %all-to-all-start.2) | async-done | bytes 786464 | tf_op jit(solution)/shard_map/all_to_all | solution.py:541
  176.2 2.4 %grad.1 = bf16[6,8,8,256]{3,2,1,0:T(8,128)(2,1)} custom-call(s32[1]{0:T(128)} %bitcast.me_ref, s32[48]{0:T(128)} %get-tuple-element.22.route, f32[6,8,8,256]{3,2,1,0:T(8,128)} %get-tuple-element.28.inner, bf16[6,4,8,256]{3,2,1,0:T(8,128)(2,1)} %get-tuple-element.29.own_sides, bf16[6,8,256]{2,1,0:T(8,128)(2,1)} %get-tuple-element.30.own_corners, ...), custom_call_target="tpu_custom_call" | custom-call | flops 2000000 | bytes 4000000 | tf_op jit(solution)/shard_map/grad/pallas_call | solution.py:644
  (37 shorter events, 3.4 us)
Async XLA Ops:
  2.3 25.3 %all-to-all-start.1 = ((bf16[8,9,8,256]{3,2,1,0:T(8,128)(2,1)}), bf16[8,9,8,256]{3,2,1,0:T(8,128)(2,1)S(1)}, u32[]{:S(2)}, u32[]{:S(2)}) async-start(bf16[8,9,8,256]{3,2,1,0:T(8,128)(2,1)} %taps.1), calls=%async_computation.1 | async-start | bytes 589824 | tf_op jit(solution)/shard_map/all_to_all | solution.py:541
  27.5 35.4 %copy-start.2 = (bf16[8,9,8,256]{3,2,1,0:T(8,128)(2,1)}, bf16[8,9,8,256]{3,2,1,0:T(8,128)(2,1)S(1)}, u32[]{:S(2)}) copy-start(bf16[8,9,8,256]{3,2,1,0:T(8,128)(2,1)S(1)} %all-to-all-done.1.rows0) | copy-start | bytes 884740
  27.5 35.4 %all-to-all-start = ((bf16[32,6,8,256]{3,2,1,0:T(8,128)(2,1)}), bf16[32,6,8,256]{3,2,1,0:T(8,128)(2,1)S(1)}, u32[]{:S(2)}, u32[]{:S(2)}) async-start(bf16[32,6,8,256]{3,2,1,0:T(8,128)(2,1)} %get-tuple-element.24), calls=%async_computation | async-start | bytes 1572864 | tf_op jit(solution)/shard_map/all_to_all | solution.py:541
  32.3 30.6 %collective-permute-start = (bf16[8,9,8,256]{3,2,1,0:T(8,128)(2,1)S(1)}, bf16[8,9,8,256]{3,2,1,0:T(8,128)(2,1)S(1)}, u32[]{:S(2)}, u32[]{:S(2)}) collective-permute-start(bf16[8,9,8,256]{3,2,1,0:T(8,128)(2,1)S(1)} %all-to-all-done.1.rows0), channel_id=1, source_target_pairs={{0,1},{1,0},{2,3},{3,2},{4,5},{5,4},{6,7},{7,6},{8,9},{9,8},{10,11... | collective-permute-start | bytes 884744 | tf_op jit(solution)/shard_map/ppermute | solution.py:546
  34.4 28.5 %collective-permute-start.1 = (bf16[8,9,8,256]{3,2,1,0:T(8,128)(2,1)S(1)}, bf16[8,9,8,256]{3,2,1,0:T(8,128)(2,1)S(1)}, u32[]{:S(2)}, u32[]{:S(2)}) collective-permute-start(bf16[8,9,8,256]{3,2,1,0:T(8,128)(2,1)S(1)} %all-to-all-done.1.rows0), channel_id=1, source_target_pairs={{0,8},{1,9},{2,10},{3,11},{4,12},{5,13},{6,14},{7,15},{8,0},{9,1},... | collective-permute-start | bytes 884744 | tf_op jit(solution)/shard_map/ppermute | solution.py:546
  38.1 24.8 %collective-permute-start.2 = (bf16[8,9,8,256]{3,2,1,0:T(8,128)(2,1)S(1)}, bf16[8,9,8,256]{3,2,1,0:T(8,128)(2,1)S(1)}, u32[]{:S(2)}, u32[]{:S(2)}) collective-permute-start(bf16[8,9,8,256]{3,2,1,0:T(8,128)(2,1)S(1)} %all-to-all-done.1.rows0), channel_id=1, source_target_pairs={{0,9},{1,8},{2,11},{3,10},{4,13},{5,12},{6,15},{7,14},{8,1},{9,0},... | collective-permute-start | bytes 884744 | tf_op jit(solution)/shard_map/ppermute | solution.py:546
  62.9 0.7 copy-start.3
  62.9 0.8 copy-start.4
  62.9 0.9 copy-start.5
  62.9 1.1 copy-start.1
  69.0 10.4 %collective-permute-start.3 = (bf16[138,8,128]{2,1,0:T(8,128)(2,1)}, bf16[138,8,128]{2,1,0:T(8,128)(2,1)S(1)}, u32[]{:S(2)}, u32[]{:S(2)}) collective-permute-start(bf16[138,8,128]{2,1,0:T(8,128)(2,1)} %get-tuple-element.33), channel_id=1, source_target_pairs={{0,1},{1,0},{2,3},{3,2},{4,5},{5,4},{6,7},{7,6},{8,9},{9,8},{10,11... | collective-permute-start | bytes 847880 | tf_op jit(solution)/shard_map/ppermute | solution.py:546
  72.0 11.7 %collective-permute-start.4 = (bf16[138,8,128]{2,1,0:T(8,128)(2,1)}, bf16[138,8,128]{2,1,0:T(8,128)(2,1)S(1)}, u32[]{:S(2)}, u32[]{:S(2)}) collective-permute-start(bf16[138,8,128]{2,1,0:T(8,128)(2,1)} %get-tuple-element.34), channel_id=1, source_target_pairs={{0,8},{1,9},{2,10},{3,11},{4,12},{5,13},{6,14},{7,15},{8,0},{9,1},... | collective-permute-start | bytes 847880 | tf_op jit(solution)/shard_map/ppermute | solution.py:546
  75.3 13.2 %collective-permute-start.5 = (bf16[138,8,128]{2,1,0:T(8,128)(2,1)}, bf16[138,8,128]{2,1,0:T(8,128)(2,1)S(1)}, u32[]{:S(2)}, u32[]{:S(2)}) collective-permute-start(bf16[138,8,128]{2,1,0:T(8,128)(2,1)} %get-tuple-element.35), channel_id=1, source_target_pairs={{0,9},{1,8},{2,11},{3,10},{4,13},{5,12},{6,15},{7,14},{8,1},{9,0},... | collective-permute-start | bytes 847880 | tf_op jit(solution)/shard_map/ppermute | solution.py:546
  79.4 9.2 %copy-start.7 = (bf16[138,8,128]{2,1,0:T(8,128)(2,1)}, bf16[138,8,128]{2,1,0:T(8,128)(2,1)S(1)}, u32[]{:S(2)}) copy-start(bf16[138,8,128]{2,1,0:T(8,128)(2,1)S(1)} %collective-permute-done.3.block1) | copy-start | bytes 847876
  83.7 4.9 %copy-start.8 = (bf16[138,8,128]{2,1,0:T(8,128)(2,1)}, bf16[138,8,128]{2,1,0:T(8,128)(2,1)S(1)}, u32[]{:S(2)}) copy-start(bf16[138,8,128]{2,1,0:T(8,128)(2,1)S(1)} %collective-permute-done.4.block2) | copy-start | bytes 847876
  88.6 0.7 copy-start.9
  122.6 18.2 %all-to-all-start.4 = ((f32[128,1,128]{2,1,0:T(1,128)}), f32[128,1,128]{2,1,0:T(1,128)S(1)}, u32[]{:S(2)}, u32[]{:S(2)}) async-start(f32[128,1,128]{2,1,0:T(1,128)} %get-tuple-element.36), calls=%async_computation.4 | async-start | bytes 131072 | tf_op jit(solution)/shard_map/all_to_all | solution.py:541
  133.8 11.9 %copy-start.6 = (f32[1,72,256]{2,1,0:T(8,128)S(1)}, f32[1,72,256]{2,1,0:T(8,128)}, u32[]{:S(2)}) copy-start(f32[1,72,256]{2,1,0:T(8,128)} %param.12) | copy-start | bytes 221188
  133.8 17.7 %copy-start.11 = (f32[9,8,256]{2,1,0:T(8,128)S(1)}, f32[9,8,256]{2,1,0:T(8,128)}, u32[]{:S(2)}) copy-start(f32[9,8,256]{2,1,0:T(8,128)} %get-tuple-element.37.g) | copy-start | bytes 221188
  140.8 24.7 %copy-start.10 = (f32[128,1,128]{2,1,0:T(1,128)}, f32[128,1,128]{2,1,0:T(1,128)S(1)}, u32[]{:S(2)}) copy-start(f32[128,1,128]{2,1,0:T(1,128)S(1)} %all-to-all-done.4.squares) | copy-start | bytes 196612
  140.8 34.5 %all-to-all-start.2 = ((bf16[32,6,8,256]{3,2,1,0:T(8,128)(2,1)}), bf16[32,6,8,256]{3,2,1,0:T(8,128)(2,1)S(1)}, u32[]{:S(2)}, u32[]{:S(2)}) async-start(bf16[32,6,8,256]{3,2,1,0:T(8,128)(2,1)} %get-tuple-element.31), calls=%async_computation.2 | async-start | bytes 1572864 | tf_op jit(solution)/shard_map/all_to_all | solution.py:541
  145.7 15.2 %collective-permute-start.6 = (f32[72,256]{1,0:T(8,128)S(1)}, f32[72,256]{1,0:T(8,128)S(1)}, u32[]{:S(2)}, u32[]{:S(2)}) collective-permute-start(f32[72,256]{1,0:T(8,128)S(1)} %bitcast.18), channel_id=1, source_target_pairs={{0,32},{32,0},{64,96},{96,64},{128,160},{160,128},{192,224},{224,1... | collective-permute-start | bytes 221192 | tf_op jit(solution)/shard_map/ppermute | solution.py:538
  147.6 16.9 %collective-permute-start.7 = (f32[72,256]{1,0:T(8,128)S(1)}, f32[72,256]{1,0:T(8,128)S(1)}, u32[]{:S(2)}, u32[]{:S(2)}) collective-permute-start(f32[72,256]{1,0:T(8,128)S(1)} %bitcast.19), channel_id=1, source_target_pairs={{0,64},{32,96},{64,0},{96,32},{128,192},{160,224},{192,128},{224,1... | collective-permute-start | bytes 221192 | tf_op jit(solution)/shard_map/ppermute | solution.py:538
  151.5 13.0 %collective-permute-start.8 = (f32[9,8,256]{2,1,0:T(8,128)S(1)}, f32[9,8,256]{2,1,0:T(8,128)S(1)}, u32[]{:S(2)}, u32[]{:S(2)}) collective-permute-start(f32[9,8,256]{2,1,0:T(8,128)S(1)} %copy-done.11), channel_id=1, source_target_pairs={{0,32},{32,0},{64,96},{96,64},{128,160},{160,128},{192,224},{224,1... | collective-permute-start | bytes 221192 | tf_op jit(solution)/shard_map/ppermute | solution.py:538
  153.6 11.8 %collective-permute-start.9 = (f32[9,8,256]{2,1,0:T(8,128)S(1)}, f32[9,8,256]{2,1,0:T(8,128)S(1)}, u32[]{:S(2)}, u32[]{:S(2)}) collective-permute-start(f32[9,8,256]{2,1,0:T(8,128)S(1)} %copy-done.11), channel_id=1, source_target_pairs={{0,64},{32,96},{64,0},{96,32},{128,192},{160,224},{192,128},{224,1... | collective-permute-start | bytes 221192 | tf_op jit(solution)/shard_map/ppermute | solution.py:538
  160.9 4.6 %copy-start.12 = (f32[72,256]{1,0:T(8,128)}, f32[72,256]{1,0:T(8,128)S(1)}, u32[]{:S(2)}) copy-start(f32[72,256]{1,0:T(8,128)S(1)} %collective-permute-done.6.w0) | copy-start | bytes 221188
  164.5 1.0 copy-start.13
  164.5 1.0 copy-start.14
  165.5 0.6 copy-start.15
  175.3 0.9 copy-start

commit v3 on v2

--- a/solution.py
+++ b/solution.py
@@ -308,7 +308,8 @@
         message[COLUMNS:GRADS] = part
 
 
-def weight_kernel(block0, block1, block2, block3, send, win0, win1, win2, grads):
+def weight_kernel(me_ref, block0, block1, block2, block3, *refs):
+    sends, (win0, win1, win2, grads, parts) = refs[:4], refs[4:]
     half = block0.shape[2]
     pairs, side = 3, 8
     where = rows_iota((side, half))
@@ -351,7 +352,12 @@
             window, flat, (((0,), (0,)), ((), ())), preferred_element_type=F32
         )
         part = part[:quarter, : 2 * half] + part[quarter:, 2 * half :]
-        send[:, tap] = part.reshape(8, 8, 2 * half)
+        parts[:, tap] = part.reshape(8, 8, 2 * half)
+    me = me_ref[0]
+    number = 4 * (me >> 4) + ((me >> 1) & 3)
+    for k, send in enumerate(sends):
+        for high in range(2):
+            send[high] = parts[number ^ (4 * high + k)]
 
 
 def backward_kernel(
@@ -431,25 +437,27 @@
     lax.fori_loop(0, entries, place, 0)
 
 
-def sum_kernel(recv, rows, squares):
-    g = recv[0]
-    for n in range(1, recv.shape[0]):
-        g = g + recv[n]
+def add_kernel(part0, part1, part2, part3, keep, send):
+    for high, out in enumerate((keep, send)):
+        out[...] = (part0[high] + part1[high]) + (part2[high] + part3[high])
+
+
+def sum_kernel(part0, part1, rows, squares):
+    g = part0[...] + part1[...]
     rows[...] = g
     squares[...] = jnp.full(squares.shape, jnp.sum(g * g), F32)
 
 
 def final_kernel(
-    mine_ref, bit_ref, decay_ref, squares, w, g, w0, w1, g0, g1, ema, averaged, ema_out,
+    mine_ref, bit_ref, decay_ref, squares, w, g, w0, w1, g_other, ema, averaged, ema_out,
     low, high,
 ):
     chans = w.shape[1]
     half = chans // 2
     mine = mine_ref[0]
-    bit = bit_ref[0]
     decay = decay_ref[0]
-    flip = jnp.where(bit == 0, 1, 2)
-    number = lax.broadcasted_iota(jnp.int32, squares.shape, 0) // (squares.shape[0] // 4)
+    first = bit_ref[0] == 0
+    number = lax.broadcasted_iota(jnp.int32, squares.shape, 0) // (squares.shape[0] // 2)
 
     def rms(replica):
         total = jnp.sum(jnp.where(number == replica, squares[...], 0.0), axis=0)
@@ -461,10 +469,8 @@
                 part[pl.ds(tap, 8, stride=9), :] = value[tap][:, n * half : (n + 1) * half]
         return low[...], high[...]
 
-    own_rms, other_rms = rms(mine), rms(mine ^ flip)
-    first = bit == 0
-    own = [x for x in ordered(g[...])]
-    other = [x for x in ordered(jnp.where(first, g0[...], g1[...]))]
+    own_rms, other_rms = rms(mine), rms(1 - mine)
+    own, other = ordered(g[...]), ordered(g_other[...])
     for n in range(2):
         span = slice(n * half, (n + 1) * half)
         updated = w[:, span] - LEARN * own[n] / own_rms
@@ -540,9 +546,9 @@
     def exchange(value, groups=None, axis="tile"):
         return lax.all_to_all(value, axis, 0, 0, axis_index_groups=groups, tiled=True)
 
-    def share(values):
+    def share(values, steps=(1, 8, 9)):
         got = []
-        for value, step in zip(values, (1, 8, 9)):
+        for value, step in zip(values, steps):
             got.append(lax.ppermute(value, "tile", [(i, i ^ step) for i in range(width)]))
         return got
 
@@ -620,46 +626,72 @@
     parts = pl.pallas_call(
         weight_kernel,
         name="weight",
-        out_shape=sds((8, 9, 8, chans), F32),
-        in_specs=[vmem] * 4,
-        out_specs=vmem,
+        out_shape=[sds((2, 9, 8, chans), F32)] * 4,
+        in_specs=[smem] + [vmem] * 4,
+        out_specs=[vmem] * 4,
         scratch_shapes=[
             win, win, win,
             pltpu.VMEM((6, side, 2 * side, 2 * chans), BF16),
+            pltpu.VMEM((8, 9, 8, chans), F32),
         ],
-    )(*blocks)
-    parts = exchange(parts, PEERS)
+    )(me, *blocks)
+    parts = [parts[0]] + share(parts[1:], (2, 4, 6))
+    keep, pass_on = pl.pallas_call(
+        add_kernel,
+        name="add",
+        out_shape=[sds((9, 8, chans), F32)] * 2,
+        in_specs=[vmem] * 4,
+        out_specs=[vmem] * 2,
+    )(*parts)
+    parts = [keep] + share([pass_on], (16,))
 
     g, squares = pl.pallas_call(
         sum_kernel,
         name="sum",
-        out_shape=(sds((9, 8, chans), F32), sds((4 * width, 1, 128), F32)),
-        in_specs=[vmem],
+        out_shape=(sds((9, 8, chans), F32), sds((2 * width, 1, 128), F32)),
+        in_specs=[vmem] * 2,
         out_specs=(vmem, vmem),
-    )(parts)
-    g0, g1 = swap(g, 0), swap(g, 1)
-    groups = [[r * width + i for i in range(4 * width)] for r in range(0, reps, 4)]
-    squares = exchange(squares, groups, ("rep", "tile"))
-
-    field_grad = pl.pallas_call(
-        grad_kernel,
-        name="grad",
-        out_shape=sds((per, side, side, chans), BF16),
-        in_specs=[smem] * 2 + [vmem] * 4,
-        out_specs=vmem,
-        cost_estimate=pl.CostEstimate(flops=2_000_000, bytes_accessed=4_000_000, transcendentals=0),
-    )(me, route, inner, own_sides, own_corners, halo)
-
+    )(*parts)
     decay = jnp.power(0.99, batch_size.astype(F32) / 32.0)
-    mine = (lax.axis_index("rep").astype(jnp.int32) & 3).reshape(1)
-    averaged, ema_out = pl.pallas_call(
-        final_kernel,
-        name="final",
-        out_shape=(sds(w.shape, F32), sds(w.shape, F32)),
-        in_specs=[smem] * 3 + [vmem] * 8,
-        out_specs=(vmem, vmem),
-        scratch_shapes=[pltpu.VMEM((72, chans // 2), F32)] * 2,
-    )(mine, gossip_bit, decay, squares, w, g, w0, w1, g0, g1, ema[0])
+    rep = lax.axis_index("rep").astype(jnp.int32)
+
+    def finish(level):
+        flip = 1 << level
+        groups = [
+            [r * width + i for r in (first, first ^ flip) for i in range(width)]
+            for first in range(reps)
+            if not first & flip
+        ]
+
+        def run(g, squares, halo):
+            g_other = swap(g, level)
+            squares = exchange(squares, groups, ("rep", "tile"))
+            field_grad = pl.pallas_call(
+                grad_kernel,
+                name="grad",
+                out_shape=sds((per, side, side, chans), BF16),
+                in_specs=[smem] * 2 + [vmem] * 4,
+                out_specs=vmem,
+                cost_estimate=pl.CostEstimate(
+                    flops=2_000_000, bytes_accessed=4_000_000, transcendentals=0
+                ),
+            )(me, route, inner, own_sides, own_corners, halo)
+            mine = ((rep >> level) & 1).reshape(1)
+            averaged, ema_out = pl.pallas_call(
+                final_kernel,
+                name="final",
+                out_shape=(sds(w.shape, F32), sds(w.shape, F32)),
+                in_specs=[smem] * 3 + [vmem] * 7,
+                out_specs=(vmem, vmem),
+                scratch_shapes=[pltpu.VMEM((72, chans // 2), F32)] * 2,
+            )(mine, gossip_bit, decay, squares, w, g, w0, w1, g_other, ema[0])
+            return field_grad, averaged, ema_out
+
+        return run
+
+    field_grad, averaged, ema_out = lax.cond(
+        gossip_bit[0] == 0, finish(0), finish(1), g, squares, halo
+    )
     return act[None], field_grad[None], averaged[None], ema_out[None]
 
 

time: 180 us -> 193 us (1.072)
  the two profiles are of different devices: /device:TPU:70 before, /device:TPU:2 now
where the time goes in v3:
time: 193 us; the launch traced here: 192 us
  starting transfers between devices  81.3 us (42%)
  waiting for transfers between devices  77.4 us (40%)
  Pallas kernels  26.1 us (14%)
  local copies, waits for them, and re-layouts  4.7 us (2%)
  between operations  2.2 us (1%)
    ppermute x10, waiting for transfers between devices, share(): lax.ppermute(value, 'tile', [(i, i ^ step) for i in range(width)])  54.5 us
    ppermute x10, starting transfers between devices, share(): lax.ppermute(value, 'tile', [(i, i ^ step) for i in range(width)])  34.9 us
    all_to_all x4, starting transfers between devices, exchange(): lax.all_to_all(value, axis, 0, 0, axis_index_groups=groups, tiled=True)  34.2 us
    all_to_all x4, waiting for transfers between devices, exchange(): lax.all_to_all(value, axis, 0, 0, axis_index_groups=groups, tiled=True)  19.6 us
    ppermute x3, starting transfers between devices, swap(): return lax.ppermute(value, 'rep', [(i, i ^ 1 << bit) for i in range(reps)])  12.2 us
    pallas_call x1, Pallas kernels, body(): pl.pallas_call(edge_kernel, name='edge', out_shape=(sds((width, HALO, 8,...  5.28 us
    pallas_call x1, Pallas kernels, body(): pl.pallas_call(forward_kernel, name='forward', out_shape=(sds((per, side,...  5.03 us
    unnamed x36, local copies, waits for them, and re-layouts  4.06 us
  transfers between devices with their start and end apart: 17, of which 7 were waited for; matrix products, arithmetic and copies ran while one was open for 0% of the time, Pallas kernels for 7%

profile of v3, /device:TPU:2, one launch (start us, length us, event | category | flops | bytes accessed | tf_op | source)
XLA Modules:
  0.0 191.8 jit_solution(15544731626528007635)
XLA Ops:
  2.3 12.3 %all-to-all-start.3 = ((bf16[8,9,8,256]{3,2,1,0:T(8,128)(2,1)}), bf16[8,9,8,256]{3,2,1,0:T(8,128)(2,1)S(1)}, u32[]{:S(2)}, u32[]{:S(2)}) async-start(bf16[8,9,8,256]{3,2,1,0:T(8,128)(2,1)} %taps.1), calls=%async_computation.3 | async-start | bytes 589824 | tf_op jit(solution)/shard_map/all_to_all | solution.py:547
  14.6 5.3 %edge.1 = (bf16[32,6,8,256]{3,2,1,0:T(8,128)(2,1)}, bf16[6,4,8,256]{3,2,1,0:T(8,128)(2,1)}, s32[48]{0:T(128)S(1)}) custom-call(s32[1]{0:T(128)} %bitcast.6.me_ref, s32[4,192]{1,0:T(4,128)} %bitcast.30, s32[4,192]{1,0:T(4,128)} %bitcast.31, s32[4,192]{1,0:T(4,128)} %bitcast.32, s32[4,192]{1,0:T(4,128)} %bitcast.33, bf16[6,8,8,256]{3,2,1,0:T(8,128)(2,1)} %bitcast.18), custom_call_target="tpu_custom_call" | custom-call | flops 1000000 | bytes 8000000 | tf_op jit(solution)/shard_map/edge/pallas_call | solution.py:567
  19.9 8.6 %all-to-all-done.3.rows0 = bf16[8,9,8,256]{3,2,1,0:T(8,128)(2,1)S(1)} async-done(((bf16[8,9,8,256]{3,2,1,0:T(8,128)(2,1)}), bf16[8,9,8,256]{3,2,1,0:T(8,128)(2,1)S(1)}, u32[]{:S(2)}, u32[]{:S(2)}) %all-to-all-start.3) | async-done | bytes 294944 | tf_op jit(solution)/shard_map/all_to_all | solution.py:547
  28.5 4.3 %all-to-all-start.2 = ((bf16[32,6,8,256]{3,2,1,0:T(8,128)(2,1)}), bf16[32,6,8,256]{3,2,1,0:T(8,128)(2,1)S(1)}, u32[]{:S(2)}, u32[]{:S(2)}) async-start(bf16[32,6,8,256]{3,2,1,0:T(8,128)(2,1)} %get-tuple-element.134), calls=%async_computation.2 | async-start | bytes 1572864 | tf_op jit(solution)/shard_map/all_to_all | solution.py:547
  32.8 3.7 %collective-permute-start.2 = (bf16[8,9,8,256]{3,2,1,0:T(8,128)(2,1)S(1)}, bf16[8,9,8,256]{3,2,1,0:T(8,128)(2,1)S(1)}, u32[]{:S(2)}, u32[]{:S(2)}) collective-permute-start(bf16[8,9,8,256]{3,2,1,0:T(8,128)(2,1)S(1)} %all-to-all-done.3.rows0), channel_id=1, source_target_pairs={{0,1},{1,0},{2,3},{3,2},{4,5},{5,4},{6,7},{7,6},{8,9},{9,8},{10,11... | collective-permute-start | bytes 884744 | tf_op jit(solution)/shard_map/ppermute | solution.py:552
  36.5 3.4 %collective-permute-start.3 = (bf16[8,9,8,256]{3,2,1,0:T(8,128)(2,1)S(1)}, bf16[8,9,8,256]{3,2,1,0:T(8,128)(2,1)S(1)}, u32[]{:S(2)}, u32[]{:S(2)}) collective-permute-start(bf16[8,9,8,256]{3,2,1,0:T(8,128)(2,1)S(1)} %all-to-all-done.3.rows0), channel_id=1, source_target_pairs={{0,8},{1,9},{2,10},{3,11},{4,12},{5,13},{6,14},{7,15},{8,0},{9,1},... | collective-permute-start | bytes 884744 | tf_op jit(solution)/shard_map/ppermute | solution.py:552
  39.9 2.1 %collective-permute-start.4 = (bf16[8,9,8,256]{3,2,1,0:T(8,128)(2,1)S(1)}, bf16[8,9,8,256]{3,2,1,0:T(8,128)(2,1)S(1)}, u32[]{:S(2)}, u32[]{:S(2)}) collective-permute-start(bf16[8,9,8,256]{3,2,1,0:T(8,128)(2,1)S(1)} %all-to-all-done.3.rows0), channel_id=1, source_target_pairs={{0,9},{1,8},{2,11},{3,10},{4,13},{5,12},{6,15},{7,14},{8,1},{9,0},... | collective-permute-start | bytes 884744 | tf_op jit(solution)/shard_map/ppermute | solution.py:552
  42.1 22.2 %collective-permute-done.2.rows1 = bf16[8,9,8,256]{3,2,1,0:T(8,128)(2,1)S(1)} collective-permute-done((bf16[8,9,8,256]{3,2,1,0:T(8,128)(2,1)S(1)}, bf16[8,9,8,256]{3,2,1,0:T(8,128)(2,1)S(1)}, u32[]{:S(2)}, u32[]{:S(2)}) %collective-permute-start.2) | collective-permute-done | bytes 294944 | tf_op jit(solution)/shard_map/ppermute | solution.py:552
  65.5 5.0 %forward.1 = (bf16[6,8,8,256]{3,2,1,0:T(8,128)(2,1)}, bf16[3,8,16,256]{3,2,1,0:T(8,128)(2,1)}, bf16[9,256,256]{2,1,0:T(8,128)(2,1)}, bf16[138,8,128]{2,1,0:T(8,1...) custom-call(s32[1]{0:T(128)} %bitcast.6.me_ref, ...), custom_call_target="tpu_custom_call" | custom-call | tf_op jit(solution)/shard_map/forward/pallas_call | solution.py:588
  70.5 4.0 %backward.1 = (bf16[32,6,8,256]{3,2,1,0:T(8,128)(2,1)}, f32[6,8,8,256]{3,2,1,0:T(8,128)S(1)}, bf16[6,4,8,256]{3,2,1,0:T(8,128)(2,1)S(1)}, bf16[6,8,256]{2,1,0:T(8,128)(2,1)S(1)}) custom-call(s32[1]{0:T(128)} %bitcast.6.me_ref, s32[48]{0:T(128)S(1)} %get-tuple-element.132.route, bf16[3,8,16,256]{3,2,1,0:T(8,128)(2,1)} %get-tuple-element.148.dpre, ...), custom_call_target="tpu_custom_call" | custom-call | flops 500000000 | bytes 8000000 | tf_op jit(solution)/shard_map/backward/pallas_call | solution.py:609
  74.5 9.0 %all-to-all-start.4 = ((bf16[32,6,8,256]{3,2,1,0:T(8,128)(2,1)}), bf16[32,6,8,256]{3,2,1,0:T(8,128)(2,1)S(1)}, u32[]{:S(2)}, u32[]{:S(2)}) async-start(bf16[32,6,8,256]{3,2,1,0:T(8,128)(2,1)} %get-tuple-element.153), calls=%async_computation.4 | async-start | bytes 1572864 | tf_op jit(solution)/shard_map/all_to_all | solution.py:547
  83.5 3.8 %collective-permute-start.5 = (bf16[138,8,128]{2,1,0:T(8,128)(2,1)S(1)}, bf16[138,8,128]{2,1,0:T(8,128)(2,1)S(1)}, u32[]{:S(2)}, u32[]{:S(2)}) collective-permute-start(bf16[138,8,128]{2,1,0:T(8,128)(2,1)S(1)} %copy-done.21), channel_id=1, source_target_pairs={{0,1},{1,0},{2,3},{3,2},{4,5},{5,4},{6,7},{7,6},{8,9},{9,8},{10,11... | collective-permute-start | bytes 847880 | tf_op jit(solution)/shard_map/ppermute | solution.py:552
  87.4 3.4 %collective-permute-start.6 = (bf16[138,8,128]{2,1,0:T(8,128)(2,1)S(1)}, bf16[138,8,128]{2,1,0:T(8,128)(2,1)S(1)}, u32[]{:S(2)}, u32[]{:S(2)}) collective-permute-start(bf16[138,8,128]{2,1,0:T(8,128)(2,1)S(1)} %copy-done.20), channel_id=1, source_target_pairs={{0,8},{1,9},{2,10},{3,11},{4,12},{5,13},{6,14},{7,15},{8,0},{9,1},... | collective-permute-start | bytes 847880 | tf_op jit(solution)/shard_map/ppermute | solution.py:552
  90.8 2.1 %collective-permute-start.7 = (bf16[138,8,128]{2,1,0:T(8,128)(2,1)S(1)}, bf16[138,8,128]{2,1,0:T(8,128)(2,1)S(1)}, u32[]{:S(2)}, u32[]{:S(2)}) collective-permute-start(bf16[138,8,128]{2,1,0:T(8,128)(2,1)S(1)} %copy-done.19), channel_id=1, source_target_pairs={{0,9},{1,8},{2,11},{3,10},{4,13},{5,12},{6,15},{7,14},{8,1},{9,0},... | collective-permute-start | bytes 847880 | tf_op jit(solution)/shard_map/ppermute | solution.py:552
  92.9 21.7 %collective-permute-done.5.block1 = bf16[138,8,128]{2,1,0:T(8,128)(2,1)S(1)} collective-permute-done((bf16[138,8,128]{2,1,0:T(8,128)(2,1)S(1)}, bf16[138,8,128]{2,1,0:T(8,128)(2,1)S(1)}, u32[]{:S(2)}, u32[]{:S(2)}) %collective-permute-start.5) | collective-permute-done | bytes 282656 | tf_op jit(solution)/shard_map/ppermute | solution.py:552
  115.6 3.4 %weight.1 = (f32[2,9,8,256]{3,2,1,0:T(8,128)}, f32[2,9,8,256]{3,2,1,0:T(8,128)}, f32[2,9,8,256]{3,2,1,0:T(8,128)}, f32[2,9,8,256]{3,2,1,0:T(8,128)}) custom-call(s32[1]{0:T(128)} %bitcast.6.me_ref, bf16[138,8,128]{2,1,0:T(8,128)(2,1)} %get-tuple-element.136.block0, bf16[138,8,128]{2,1,0:T(8,128)(2,1)} %copy-done.7, bf16[138,8,128]{2,1,0:T(8,128)(2,1)} %copy-done.8, ...), custom_call_target="tpu_custom_call" | custom-call | tf_op jit(solution)/shard_map/weight/pallas_call | solution.py:626
  119.0 4.5 %collective-permute-start.10 = (f32[2,9,8,256]{3,2,1,0:T(8,128)}, f32[2,9,8,256]{3,2,1,0:T(8,128)S(1)}, u32[]{:S(2)}, u32[]{:S(2)}) collective-permute-start(f32[2,9,8,256]{3,2,1,0:T(8,128)} %get-tuple-element.143), channel_id=1, source_target_pairs={{0,6},{1,7},{2,4},{3,5},{4,2},{5,3},{6,0},{7,1},{8,14},{9,15},{10,... | collective-permute-start | bytes 442376 | tf_op jit(solution)/shard_map/ppermute | solution.py:552
  123.6 4.3 %collective-permute-start.8 = (f32[2,9,8,256]{3,2,1,0:T(8,128)}, f32[2,9,8,256]{3,2,1,0:T(8,128)S(1)}, u32[]{:S(2)}, u32[]{:S(2)}) collective-permute-start(f32[2,9,8,256]{3,2,1,0:T(8,128)} %get-tuple-element.141), channel_id=1, source_target_pairs={{0,2},{1,3},{2,0},{3,1},{4,6},{5,7},{6,4},{7,5},{8,10},{9,11},{10,... | collective-permute-start | bytes 442376 | tf_op jit(solution)/shard_map/ppermute | solution.py:552
  127.9 3.4 %collective-permute-start.9 = (f32[2,9,8,256]{3,2,1,0:T(8,128)}, f32[2,9,8,256]{3,2,1,0:T(8,128)S(1)}, u32[]{:S(2)}, u32[]{:S(2)}) collective-permute-start(f32[2,9,8,256]{3,2,1,0:T(8,128)} %get-tuple-element.142), channel_id=1, source_target_pairs={{0,4},{1,5},{2,6},{3,7},{4,0},{5,1},{6,2},{7,3},{8,12},{9,13},{10,... | collective-permute-start | bytes 442376 | tf_op jit(solution)/shard_map/ppermute | solution.py:552
  131.3 2.3 %collective-permute-done.8.part1 = f32[2,9,8,256]{3,2,1,0:T(8,128)S(1)} collective-permute-done((f32[2,9,8,256]{3,2,1,0:T(8,128)}, f32[2,9,8,256]{3,2,1,0:T(8,128)S(1)}, u32[]{:S(2)}, u32[]{:S(2)}) %collective-permute-start.8) | collective-permute-done | bytes 147488 | tf_op jit(solution)/shard_map/ppermute | solution.py:552
  133.6 8.2 %collective-permute-done.9.part2 = f32[2,9,8,256]{3,2,1,0:T(8,128)S(1)} collective-permute-done((f32[2,9,8,256]{3,2,1,0:T(8,128)}, f32[2,9,8,256]{3,2,1,0:T(8,128)S(1)}, u32[]{:S(2)}, u32[]{:S(2)}) %collective-permute-start.9) | collective-permute-done | bytes 147488 | tf_op jit(solution)/shard_map/ppermute | solution.py:552
  142.5 1.8 add.1
  144.3 4.2 %collective-permute-start.11 = (f32[9,8,256]{2,1,0:T(8,128)}, f32[9,8,256]{2,1,0:T(8,128)S(1)}, u32[]{:S(2)}, u32[]{:S(2)}) collective-permute-start(f32[9,8,256]{2,1,0:T(8,128)} %get-tuple-element.145), channel_id=1, source_target_pairs={{0,16},{1,17},{2,18},{3,19},{4,20},{5,21},{6,22},{7,23},{8,24},{9,... | collective-permute-start | bytes 221192 | tf_op jit(solution)/shard_map/ppermute | solution.py:552
  148.5 1.9 %collective-permute-start.12 = (f32[72,256]{1,0:T(8,128)S(1)}, f32[72,256]{1,0:T(8,128)S(1)}, u32[]{:S(2)}, u32[]{:S(2)}) collective-permute-start(f32[72,256]{1,0:T(8,128)S(1)} %bitcast.21), channel_id=1, source_target_pairs={{0,32},{32,0},{64,96},{96,64},{128,160},{160,128},{192,224},{224,1... | collective-permute-start | bytes 221192 | tf_op jit(solution)/shard_map/ppermute | solution.py:544
  150.4 5.2 %collective-permute-start.13 = (f32[72,256]{1,0:T(8,128)S(1)}, f32[72,256]{1,0:T(8,128)S(1)}, u32[]{:S(2)}, u32[]{:S(2)}) collective-permute-start(f32[72,256]{1,0:T(8,128)S(1)} %bitcast.22), channel_id=1, source_target_pairs={{0,64},{32,96},{64,0},{96,32},{128,192},{160,224},{192,128},{224,1... | collective-permute-start | bytes 221192 | tf_op jit(solution)/shard_map/ppermute | solution.py:544
  157.5 1.7 sum.1
  159.2 3.2 %collective-permute-done.13 = f32[72,256]{1,0:T(8,128)S(1)} collective-permute-done((f32[72,256]{1,0:T(8,128)S(1)}, f32[72,256]{1,0:T(8,128)S(1)}, u32[]{:S(2)}, u32[]{:S(2)}) %collective-permute-start.13) | collective-permute-done | bytes 73760 | tf_op jit(solution)/shard_map/ppermute | solution.py:544
  162.4 28.7 %conditional.1 = (f32[72,256]{1,0:T(8,128)}, f32[72,256]{1,0:T(8,128)}, bf16[1,6,8,8,256]{4,3,2,1,0:T(8,128)(2,1)S(1)}) conditional(s32[]{:T(128)} %bitcast.15, (s32[]{:T(128)}, f32[1]{0:T(128)}, f32[64,1,128]{2,1,0:T(1,128)}, f32[9,8,256]{2,1,0:T(8,128)S(1)}, f32[1,72,256]{2,1,0:T(8,128)S(1)}, /*index=5*/s32[1]{0:T(128)}, f32[72,256]{1,0:T(8,128)S(1)}, ...), branch_computations={%region_0.0_spmd, %region_1.0_spmd} | conditional | flops 2000003 | bytes 4819400 | solution.py:692
  162.4 5.2 %collective-permute-start = (f32[9,8,256]{2,1,0:T(8,128)S(1)}, f32[9,8,256]{2,1,0:T(8,128)S(1)}, u32[]{:S(2)}, u32[]{:S(2)}) collective-permute-start(f32[9,8,256]{2,1,0:T(8,128)S(1)} %get-tuple-element.74.g), channel_id=1, source_target_pairs={{0,64},{32,96},{64,0},{96,32},{128,192},{160,224},{192,128},{224,1... | collective-permute-start | bytes 221192 | tf_op jit(solution)/shard_map/cond/branch_0_fun/ppermute | solution.py:544
  167.6 8.5 %all-to-all-start = ((f32[64,1,128]{2,1,0:T(1,128)}), f32[64,1,128]{2,1,0:T(1,128)S(1)}, u32[]{:S(2)}, u32[]{:S(2)}) async-start(f32[64,1,128]{2,1,0:T(1,128)} %get-tuple-element.72), calls=%async_computation | async-start | bytes 65536 | tf_op jit(solution)/shard_map/cond/branch_0_fun/all_to_all | solution.py:547
  177.1 11.0 %all-to-all-done.squares = f32[64,1,128]{2,1,0:T(1,128)S(1)} async-done(((f32[64,1,128]{2,1,0:T(1,128)}), f32[64,1,128]{2,1,0:T(1,128)S(1)}, u32[]{:S(2)}, u32[]{:S(2)}) %all-to-all-start) | async-done | bytes 32800 | tf_op jit(solution)/shard_map/cond/branch_0_fun/all_to_all | solution.py:547
  188.8 2.3 %final.2 = (f32[72,256]{1,0:T(8,128)}, f32[72,256]{1,0:T(8,128)}) custom-call(s32[1]{0:T(128)} %bitcast.mine_ref, s32[1]{0:T(128)} %get-tuple-element.70.bit_ref, f32[1]{0:T(128)S(6)} %pow.5.decay_ref, f32[64,1,128]{2,1,0:T(1,128)} %copy-done.15, f32[72,256]{1,0:T(8,128)S(1)} %get-tuple-element.73.w, f32[9,8,256]{2,1,0:T(8,128)S(1)} %get-tuple-element.74.g, ...), custom_call_target="tpu_custom_call" | custom-call | tf_op jit(solution)/shard_map/cond/branch_0_fun/final/pallas_call | solution.py:680
  (52 shorter events, 7.3 us)
Async XLA Ops:
  2.3 26.2 %all-to-all-start.3 = ((bf16[8,9,8,256]{3,2,1,0:T(8,128)(2,1)}), bf16[8,9,8,256]{3,2,1,0:T(8,128)(2,1)S(1)}, u32[]{:S(2)}, u32[]{:S(2)}) async-start(bf16[8,9,8,256]{3,2,1,0:T(8,128)(2,1)} %taps.1), calls=%async_computation.3 | async-start | bytes 589824 | tf_op jit(solution)/shard_map/all_to_all | solution.py:547
  28.5 35.8 %copy-start.1 = (bf16[8,9,8,256]{3,2,1,0:T(8,128)(2,1)}, bf16[8,9,8,256]{3,2,1,0:T(8,128)(2,1)S(1)}, u32[]{:S(2)}) copy-start(bf16[8,9,8,256]{3,2,1,0:T(8,128)(2,1)S(1)} %all-to-all-done.3.rows0) | copy-start | bytes 884740
  28.5 35.8 %all-to-all-start.2 = ((bf16[32,6,8,256]{3,2,1,0:T(8,128)(2,1)}), bf16[32,6,8,256]{3,2,1,0:T(8,128)(2,1)S(1)}, u32[]{:S(2)}, u32[]{:S(2)}) async-start(bf16[32,6,8,256]{3,2,1,0:T(8,128)(2,1)} %get-tuple-element.134), calls=%async_computation.2 | async-start | bytes 1572864 | tf_op jit(solution)/shard_map/all_to_all | solution.py:547
  32.8 31.4 %collective-permute-start.2 = (bf16[8,9,8,256]{3,2,1,0:T(8,128)(2,1)S(1)}, bf16[8,9,8,256]{3,2,1,0:T(8,128)(2,1)S(1)}, u32[]{:S(2)}, u32[]{:S(2)}) collective-permute-start(bf16[8,9,8,256]{3,2,1,0:T(8,128)(2,1)S(1)} %all-to-all-done.3.rows0), channel_id=1, source_target_pairs={{0,1},{1,0},{2,3},{3,2},{4,5},{5,4},{6,7},{7,6},{8,9},{9,8},{10,11... | collective-permute-start | bytes 884744 | tf_op jit(solution)/shard_map/ppermute | solution.py:552
  36.5 27.7 %collective-permute-start.3 = (bf16[8,9,8,256]{3,2,1,0:T(8,128)(2,1)S(1)}, bf16[8,9,8,256]{3,2,1,0:T(8,128)(2,1)S(1)}, u32[]{:S(2)}, u32[]{:S(2)}) collective-permute-start(bf16[8,9,8,256]{3,2,1,0:T(8,128)(2,1)S(1)} %all-to-all-done.3.rows0), channel_id=1, source_target_pairs={{0,8},{1,9},{2,10},{3,11},{4,12},{5,13},{6,14},{7,15},{8,0},{9,1},... | collective-permute-start | bytes 884744 | tf_op jit(solution)/shard_map/ppermute | solution.py:552
  39.9 24.4 %collective-permute-start.4 = (bf16[8,9,8,256]{3,2,1,0:T(8,128)(2,1)S(1)}, bf16[8,9,8,256]{3,2,1,0:T(8,128)(2,1)S(1)}, u32[]{:S(2)}, u32[]{:S(2)}) collective-permute-start(bf16[8,9,8,256]{3,2,1,0:T(8,128)(2,1)S(1)} %all-to-all-done.3.rows0), channel_id=1, source_target_pairs={{0,9},{1,8},{2,11},{3,10},{4,13},{5,12},{6,15},{7,14},{8,1},{9,0},... | collective-permute-start | bytes 884744 | tf_op jit(solution)/shard_map/ppermute | solution.py:552
  64.3 0.7 copy-start.3
  64.3 0.8 copy-start.4
  64.3 0.9 copy-start.5
  64.3 1.2 copy-start
  74.5 9.0 %copy-start.21 = (bf16[138,8,128]{2,1,0:T(8,128)(2,1)S(1)}, bf16[138,8,128]{2,1,0:T(8,128)(2,1)}, u32[]{:S(2)}) copy-start(bf16[138,8,128]{2,1,0:T(8,128)(2,1)} %get-tuple-element.137) | copy-start | bytes 847876
  74.5 12.9 %copy-start.20 = (bf16[138,8,128]{2,1,0:T(8,128)(2,1)S(1)}, bf16[138,8,128]{2,1,0:T(8,128)(2,1)}, u32[]{:S(2)}) copy-start(bf16[138,8,128]{2,1,0:T(8,128)(2,1)} %get-tuple-element.138) | copy-start | bytes 847876
  74.5 16.2 %copy-start.19 = (bf16[138,8,128]{2,1,0:T(8,128)(2,1)S(1)}, bf16[138,8,128]{2,1,0:T(8,128)(2,1)}, u32[]{:S(2)}) copy-start(bf16[138,8,128]{2,1,0:T(8,128)(2,1)} %get-tuple-element.139) | copy-start | bytes 847876
  74.5 87.9 %all-to-all-start.4 = ((bf16[32,6,8,256]{3,2,1,0:T(8,128)(2,1)}), bf16[32,6,8,256]{3,2,1,0:T(8,128)(2,1)S(1)}, u32[]{:S(2)}, u32[]{:S(2)}) async-start(bf16[32,6,8,256]{3,2,1,0:T(8,128)(2,1)} %get-tuple-element.153), calls=%async_computation.4 | async-start | bytes 1572864 | tf_op jit(solution)/shard_map/all_to_all | solution.py:547
  83.5 64.9 %copy-start.2 = (f32[1,72,256]{2,1,0:T(8,128)S(1)}, f32[1,72,256]{2,1,0:T(8,128)}, u32[]{:S(2)}) copy-start(f32[1,72,256]{2,1,0:T(8,128)} %param.14) | copy-start | bytes 221188
  83.5 78.9 %copy-start.6 = (f32[1,72,256]{2,1,0:T(8,128)S(1)}, f32[1,72,256]{2,1,0:T(8,128)}, u32[]{:S(2)}) copy-start(f32[1,72,256]{2,1,0:T(8,128)} %param.15) | copy-start | bytes 221188
  83.5 31.1 %collective-permute-start.5 = (bf16[138,8,128]{2,1,0:T(8,128)(2,1)S(1)}, bf16[138,8,128]{2,1,0:T(8,128)(2,1)S(1)}, u32[]{:S(2)}, u32[]{:S(2)}) collective-permute-start(bf16[138,8,128]{2,1,0:T(8,128)(2,1)S(1)} %copy-done.21), channel_id=1, source_target_pairs={{0,1},{1,0},{2,3},{3,2},{4,5},{5,4},{6,7},{7,6},{8,9},{9,8},{10,11... | collective-permute-start | bytes 847880 | tf_op jit(solution)/shard_map/ppermute | solution.py:552
  87.4 27.3 %collective-permute-start.6 = (bf16[138,8,128]{2,1,0:T(8,128)(2,1)S(1)}, bf16[138,8,128]{2,1,0:T(8,128)(2,1)S(1)}, u32[]{:S(2)}, u32[]{:S(2)}) collective-permute-start(bf16[138,8,128]{2,1,0:T(8,128)(2,1)S(1)} %copy-done.20), channel_id=1, source_target_pairs={{0,8},{1,9},{2,10},{3,11},{4,12},{5,13},{6,14},{7,15},{8,0},{9,1},... | collective-permute-start | bytes 847880 | tf_op jit(solution)/shard_map/ppermute | solution.py:552
  90.8 23.9 %collective-permute-start.7 = (bf16[138,8,128]{2,1,0:T(8,128)(2,1)S(1)}, bf16[138,8,128]{2,1,0:T(8,128)(2,1)S(1)}, u32[]{:S(2)}, u32[]{:S(2)}) collective-permute-start(bf16[138,8,128]{2,1,0:T(8,128)(2,1)S(1)} %copy-done.19), channel_id=1, source_target_pairs={{0,9},{1,8},{2,11},{3,10},{4,13},{5,12},{6,15},{7,14},{8,1},{9,0},... | collective-permute-start | bytes 847880 | tf_op jit(solution)/shard_map/ppermute | solution.py:552
  114.6 0.7 copy-start.7
  114.7 0.8 copy-start.8
  114.7 0.9 copy-start.9
  119.0 12.2 %collective-permute-start.10 = (f32[2,9,8,256]{3,2,1,0:T(8,128)}, f32[2,9,8,256]{3,2,1,0:T(8,128)S(1)}, u32[]{:S(2)}, u32[]{:S(2)}) collective-permute-start(f32[2,9,8,256]{3,2,1,0:T(8,128)} %get-tuple-element.143), channel_id=1, source_target_pairs={{0,6},{1,7},{2,4},{3,5},{4,2},{5,3},{6,0},{7,1},{8,14},{9,15},{10,... | collective-permute-start | bytes 442376 | tf_op jit(solution)/shard_map/ppermute | solution.py:552
  123.6 10.0 %collective-permute-start.8 = (f32[2,9,8,256]{3,2,1,0:T(8,128)}, f32[2,9,8,256]{3,2,1,0:T(8,128)S(1)}, u32[]{:S(2)}, u32[]{:S(2)}) collective-permute-start(f32[2,9,8,256]{3,2,1,0:T(8,128)} %get-tuple-element.141), channel_id=1, source_target_pairs={{0,2},{1,3},{2,0},{3,1},{4,6},{5,7},{6,4},{7,5},{8,10},{9,11},{10,... | collective-permute-start | bytes 442376 | tf_op jit(solution)/shard_map/ppermute | solution.py:552
  127.9 13.9 %collective-permute-start.9 = (f32[2,9,8,256]{3,2,1,0:T(8,128)}, f32[2,9,8,256]{3,2,1,0:T(8,128)S(1)}, u32[]{:S(2)}, u32[]{:S(2)}) collective-permute-start(f32[2,9,8,256]{3,2,1,0:T(8,128)} %get-tuple-element.142), channel_id=1, source_target_pairs={{0,4},{1,5},{2,6},{3,7},{4,0},{5,1},{6,2},{7,3},{8,12},{9,13},{10,... | collective-permute-start | bytes 442376 | tf_op jit(solution)/shard_map/ppermute | solution.py:552
  131.3 10.5 %copy-start.11 = (f32[2,9,8,256]{3,2,1,0:T(8,128)}, f32[2,9,8,256]{3,2,1,0:T(8,128)S(1)}, u32[]{:S(2)}) copy-start(f32[2,9,8,256]{3,2,1,0:T(8,128)S(1)} %collective-permute-done.10.part3) | copy-start | bytes 442372
  133.6 8.3 %copy-start.12 = (f32[2,9,8,256]{3,2,1,0:T(8,128)}, f32[2,9,8,256]{3,2,1,0:T(8,128)S(1)}, u32[]{:S(2)}) copy-start(f32[2,9,8,256]{3,2,1,0:T(8,128)S(1)} %collective-permute-done.8.part1) | copy-start | bytes 442372
  144.3 12.6 %collective-permute-start.11 = (f32[9,8,256]{2,1,0:T(8,128)}, f32[9,8,256]{2,1,0:T(8,128)S(1)}, u32[]{:S(2)}, u32[]{:S(2)}) collective-permute-start(f32[9,8,256]{2,1,0:T(8,128)} %get-tuple-element.145), channel_id=1, source_target_pairs={{0,16},{1,17},{2,18},{3,19},{4,20},{5,21},{6,22},{7,23},{8,24},{9,... | collective-permute-start | bytes 221192 | tf_op jit(solution)/shard_map/ppermute | solution.py:552
  148.5 10.7 %collective-permute-start.12 = (f32[72,256]{1,0:T(8,128)S(1)}, f32[72,256]{1,0:T(8,128)S(1)}, u32[]{:S(2)}, u32[]{:S(2)}) collective-permute-start(f32[72,256]{1,0:T(8,128)S(1)} %bitcast.21), channel_id=1, source_target_pairs={{0,32},{32,0},{64,96},{96,64},{128,160},{160,128},{192,224},{224,1... | collective-permute-start | bytes 221192 | tf_op jit(solution)/shard_map/ppermute | solution.py:544
  150.4 12.1 %collective-permute-start.13 = (f32[72,256]{1,0:T(8,128)S(1)}, f32[72,256]{1,0:T(8,128)S(1)}, u32[]{:S(2)}, u32[]{:S(2)}) collective-permute-start(f32[72,256]{1,0:T(8,128)S(1)} %bitcast.22), channel_id=1, source_target_pairs={{0,64},{32,96},{64,0},{96,32},{128,192},{160,224},{192,128},{224,1... | collective-permute-start | bytes 221192 | tf_op jit(solution)/shard_map/ppermute | solution.py:544
  162.4 25.7 %collective-permute-start = (f32[9,8,256]{2,1,0:T(8,128)S(1)}, f32[9,8,256]{2,1,0:T(8,128)S(1)}, u32[]{:S(2)}, u32[]{:S(2)}) collective-permute-start(f32[9,8,256]{2,1,0:T(8,128)S(1)} %get-tuple-element.74.g), channel_id=1, source_target_pairs={{0,64},{32,96},{64,0},{96,32},{128,192},{160,224},{192,128},{224,1... | collective-permute-start | bytes 221192 | tf_op jit(solution)/shard_map/cond/branch_0_fun/ppermute | solution.py:544
  167.6 20.6 %all-to-all-start = ((f32[64,1,128]{2,1,0:T(1,128)}), f32[64,1,128]{2,1,0:T(1,128)S(1)}, u32[]{:S(2)}, u32[]{:S(2)}) async-start(f32[64,1,128]{2,1,0:T(1,128)} %get-tuple-element.72), calls=%async_computation | async-start | bytes 65536 | tf_op jit(solution)/shard_map/cond/branch_0_fun/all_to_all | solution.py:547
  (5 other events, 3.2 us)

commit v4 on v3

--- a/solution.py
+++ b/solution.py
@@ -12,6 +12,7 @@
 F32 = jnp.float32
 BF16 = jnp.bfloat16
 SMEM = pltpu.SMEM
+LIMIT = pltpu.CompilerParams(vmem_limit_bytes=20 * 2**20)
 
 
 def rows_iota(shape):
@@ -77,14 +78,16 @@
     lax.fori_loop(0, 4 * per, number, 0)
 
 
-def taps_kernel(rows, send, low, high):
+def taps_kernel(rows, send, grouped, low, high):
     scale = (9.0 * rows.shape[1]) ** (-0.5)
     half = rows.shape[1] // 2
     for n, part in enumerate((low, high)):
         part[...] = rows[:, n * half : (n + 1) * half]
     for tap in range(9):
         picked = [part[pl.ds(tap, 8, stride=9), :] for part in (low, high)]
-        value = (jnp.concatenate(picked, axis=1) * scale).astype(BF16)
+        value = jnp.concatenate(picked, axis=1)
+        grouped[tap] = value
+        value = (value * scale).astype(BF16)
         for n in range(send.shape[0]):
             send[n, tap] = value
 
@@ -442,40 +445,35 @@
         out[...] = (part0[high] + part1[high]) + (part2[high] + part3[high])
 
 
-def sum_kernel(part0, part1, rows, squares):
+def sum_kernel(part0, part1, grouped, both, squares):
     g = part0[...] + part1[...]
-    rows[...] = g
+    both[0] = g
+    both[1] = grouped[...]
     squares[...] = jnp.full(squares.shape, jnp.sum(g * g), F32)
 
 
-def final_kernel(
-    mine_ref, bit_ref, decay_ref, squares, w, g, w0, w1, g_other, ema, averaged, ema_out,
-    low, high,
-):
-    chans = w.shape[1]
+def final_kernel(mine_ref, decay_ref, squares, own, other, ema, averaged, ema_out, low, high):
+    chans = ema.shape[1]
     half = chans // 2
     mine = mine_ref[0]
     decay = decay_ref[0]
-    first = bit_ref[0] == 0
     number = lax.broadcasted_iota(jnp.int32, squares.shape, 0) // (squares.shape[0] // 2)
 
     def rms(replica):
         total = jnp.sum(jnp.where(number == replica, squares[...], 0.0), axis=0)
-        return jnp.sqrt(total / (9.0 * chans * chans) + 1e-06)
-
-    def ordered(value):
+        root = jnp.sqrt(total / (9.0 * chans * chans) + 1e-06)
+        return jnp.concatenate([root, root], axis=1)
+
+    own_rms, other_rms = rms(mine), rms(1 - mine)
+    for tap in range(9):
+        updated = own[1, tap] - LEARN * own[0, tap] / own_rms
+        partner = other[1, tap] - LEARN * other[0, tap] / other_rms
+        mean = 0.5 * (updated + partner)
         for n, part in enumerate((low, high)):
-            for tap in range(9):
-                part[pl.ds(tap, 8, stride=9), :] = value[tap][:, n * half : (n + 1) * half]
-        return low[...], high[...]
-
-    own_rms, other_rms = rms(mine), rms(1 - mine)
-    own, other = ordered(g[...]), ordered(g_other[...])
-    for n in range(2):
+            part[pl.ds(tap, 8, stride=9), :] = mean[:, n * half : (n + 1) * half]
+    for n, part in enumerate((low, high)):
         span = slice(n * half, (n + 1) * half)
-        updated = w[:, span] - LEARN * own[n] / own_rms
-        partner = jnp.where(first, w0[:, span], w1[:, span]) - LEARN * other[n] / other_rms
-        mean = 0.5 * (updated + partner)
+        mean = part[...]
         averaged[:, span] = mean
         ema_out[:, span] = decay * ema[:, span] + (1.0 - decay) * mean
 
@@ -552,20 +550,20 @@
             got.append(lax.ppermute(value, "tile", [(i, i ^ step) for i in range(width)]))
         return got
 
-    w0, w1 = swap(w, 0), swap(w, 1)
-
-    rows = pl.pallas_call(
+    rows, grouped = pl.pallas_call(
         taps_kernel,
+        compiler_params=LIMIT,
         name="taps",
-        out_shape=sds((8, 9, 8, chans), BF16),
+        out_shape=(sds((8, 9, 8, chans), BF16), sds((9, 8, chans), F32)),
         in_specs=[vmem],
-        out_specs=vmem,
+        out_specs=(vmem, vmem),
         scratch_shapes=[pltpu.VMEM((72, chans // 2), F32)] * 2,
     )(w)
     rows = exchange(rows, PEERS)
 
     halo_send, strips, route = pl.pallas_call(
         edge_kernel,
+        compiler_params=LIMIT,
         name="edge",
         out_shape=(
             sds((width, HALO, 8, chans), BF16),
@@ -587,6 +585,7 @@
     message = sds((MESSAGE, 8, chans // 2), BF16)
     act, dpre, taps, *messages = pl.pallas_call(
         forward_kernel,
+        compiler_params=LIMIT,
         name="forward",
         out_shape=(
             sds((per, side, side, chans), BF16),
@@ -608,6 +607,7 @@
 
     halo_send, inner, own_sides, own_corners = pl.pallas_call(
         backward_kernel,
+        compiler_params=LIMIT,
         name="backward",
         out_shape=(
             sds((width, HALO, 8, chans), BF16),
@@ -625,6 +625,7 @@
     win = pltpu.VMEM((6, side + 2, 2 * side, chans // 2), BF16)
     parts = pl.pallas_call(
         weight_kernel,
+        compiler_params=LIMIT,
         name="weight",
         out_shape=[sds((2, 9, 8, chans), F32)] * 4,
         in_specs=[smem] + [vmem] * 4,
@@ -638,6 +639,7 @@
     parts = [parts[0]] + share(parts[1:], (2, 4, 6))
     keep, pass_on = pl.pallas_call(
         add_kernel,
+        compiler_params=LIMIT,
         name="add",
         out_shape=[sds((9, 8, chans), F32)] * 2,
         in_specs=[vmem] * 4,
@@ -645,13 +647,14 @@
     )(*parts)
     parts = [keep] + share([pass_on], (16,))
 
-    g, squares = pl.pallas_call(
+    both, squares = pl.pallas_call(
         sum_kernel,
+        compiler_params=LIMIT,
         name="sum",
-        out_shape=(sds((9, 8, chans), F32), sds((2 * width, 1, 128), F32)),
-        in_specs=[vmem] * 2,
+        out_shape=(sds((2, 9, 8, chans), F32), sds((2 * width, 1, 128), F32)),
+        in_specs=[vmem] * 3,
         out_specs=(vmem, vmem),
-    )(*parts)
+    )(*parts, grouped)
     decay = jnp.power(0.99, batch_size.astype(F32) / 32.0)
     rep = lax.axis_index("rep").astype(jnp.int32)
 
@@ -663,12 +666,13 @@
             if not first & flip
         ]
 
-        def run(g, squares, halo):
-            g_other = swap(g, level)
+        def run(own, squares, halo):
+            other = swap(own, level)
             squares = exchange(squares, groups, ("rep", "tile"))
             field_grad = pl.pallas_call(
                 grad_kernel,
-                name="grad",
+                compiler_params=LIMIT,
+        name="grad",
                 out_shape=sds((per, side, side, chans), BF16),
                 in_specs=[smem] * 2 + [vmem] * 4,
                 out_specs=vmem,
@@ -679,18 +683,19 @@
             mine = ((rep >> level) & 1).reshape(1)
             averaged, ema_out = pl.pallas_call(
                 final_kernel,
-                name="final",
+                compiler_params=LIMIT,
+        name="final",
                 out_shape=(sds(w.shape, F32), sds(w.shape, F32)),
-                in_specs=[smem] * 3 + [vmem] * 7,
+                in_specs=[smem] * 2 + [vmem] * 4,
                 out_specs=(vmem, vmem),
                 scratch_shapes=[pltpu.VMEM((72, chans // 2), F32)] * 2,
-            )(mine, gossip_bit, decay, squares, w, g, w0, w1, g_other, ema[0])
+            )(mine, decay, squares, own, other, ema[0])
             return field_grad, averaged, ema_out
 
         return run
 
     field_grad, averaged, ema_out = lax.cond(
-        gossip_bit[0] == 0, finish(0), finish(1), g, squares, halo
+        gossip_bit[0] == 0, finish(0), finish(1), both, squares, halo
     )
     return act[None], field_grad[None], averaged[None], ema_out[None]
 

time: 193 us -> 174 us (0.902)
  the two profiles are of different devices: /device:TPU:2 before, /device:TPU:6 now
where the time goes in v4:
time: 174 us; the launch traced here: 173 us
  starting transfers between devices  76.6 us (44%)
  waiting for transfers between devices  72.1 us (41%)
  Pallas kernels  15.7 us (9%)
  local copies, waits for them, and re-layouts  5.94 us (3%)
  between operations  2.13 us (1%)
    ppermute x10, waiting for transfers between devices, share(): lax.ppermute(value, 'tile', [(i, i ^ step) for i in range(width)])  56 us
    all_to_all x4, starting transfers between devices, exchange(): lax.all_to_all(value, axis, 0, 0, axis_index_groups=groups, tiled=True)  36.9 us
    ppermute x10, starting transfers between devices, share(): lax.ppermute(value, 'tile', [(i, i ^ step) for i in range(width)])  34.7 us
    all_to_all x4, waiting for transfers between devices, exchange(): lax.all_to_all(value, axis, 0, 0, axis_index_groups=groups, tiled=True)  16.1 us
    unnamed x24, local copies, waits for them, and re-layouts  5.94 us
    pallas_call x1, Pallas kernels, body(): pl.pallas_call(edge_kernel, compiler_params=LIMIT, name='edge', out_shape...  5.09 us
    ppermute x1, starting transfers between devices, swap(): return lax.ppermute(value, 'rep', [(i, i ^ 1 << bit) for i in range(reps)])  4.94 us
  transfers between devices with their start and end apart: 15, of which 7 were waited for; matrix products, arithmetic and copies ran while one was open for 0% of the time, Pallas kernels for 5%

profile of v4, /device:TPU:6, one launch (start us, length us, event | category | flops | bytes accessed | tf_op | source)
XLA Modules:
  0.0 172.6 jit_solution(11933773002655542273)
XLA Ops:
  0.6 0.9 copy-done.3
  2.3 12.5 %all-to-all-start.3 = ((bf16[8,9,8,256]{3,2,1,0:T(8,128)(2,1)}), bf16[8,9,8,256]{3,2,1,0:T(8,128)(2,1)S(1)}, u32[]{:S(2)}, u32[]{:S(2)}) async-start(bf16[8,9,8,256]{3,2,1,0:T(8,128)(2,1)} %get-tuple-element.113), calls=%async_computation.3 | async-start | bytes 589824 | tf_op jit(solution)/shard_map/all_to_all | solution.py:545
  14.7 0.9 copy-done
  18.4 5.1 %edge.1 = (bf16[32,6,8,256]{3,2,1,0:T(8,128)(2,1)}, bf16[6,4,8,256]{3,2,1,0:T(8,128)(2,1)S(1)}, s32[48]{0:T(128)S(1)}) custom-call(s32[1]{0:T(128)} %bitcast.6.me_ref, s32[4,192]{1,0:T(4,128)S(1)} %bitcast.22, s32[4,192]{1,0:T(4,128)S(1)} %bitcast.23, s32[4,192]{1,0:T(4,128)S(1)} %bitcast.24, s32[4,192]{1,0:T(4,128)S(1)} %bitcast.25, ...), custom_call_target="tpu_custom_call" | custom-call | flops 1000000 | bytes 8000000 | tf_op jit(solution)/shard_map/edge/pallas_call | solution.py:564
  23.5 5.1 %all-to-all-done.3.rows0 = bf16[8,9,8,256]{3,2,1,0:T(8,128)(2,1)S(1)} async-done(((bf16[8,9,8,256]{3,2,1,0:T(8,128)(2,1)}), bf16[8,9,8,256]{3,2,1,0:T(8,128)(2,1)S(1)}, u32[]{:S(2)}, u32[]{:S(2)}) %all-to-all-start.3) | async-done | bytes 294944 | tf_op jit(solution)/shard_map/all_to_all | solution.py:545
  28.6 5.3 %all-to-all-start.2 = ((bf16[32,6,8,256]{3,2,1,0:T(8,128)(2,1)}), bf16[32,6,8,256]{3,2,1,0:T(8,128)(2,1)S(1)}, u32[]{:S(2)}, u32[]{:S(2)}) async-start(bf16[32,6,8,256]{3,2,1,0:T(8,128)(2,1)} %get-tuple-element.112), calls=%async_computation.2 | async-start | bytes 1572864 | tf_op jit(solution)/shard_map/all_to_all | solution.py:545
  34.0 3.7 %collective-permute-start.2 = (bf16[8,9,8,256]{3,2,1,0:T(8,128)(2,1)S(1)}, bf16[8,9,8,256]{3,2,1,0:T(8,128)(2,1)S(1)}, u32[]{:S(2)}, u32[]{:S(2)}) collective-permute-start(bf16[8,9,8,256]{3,2,1,0:T(8,128)(2,1)S(1)} %all-to-all-done.3.rows0), channel_id=1, source_target_pairs={{0,1},{1,0},{2,3},{3,2},{4,5},{5,4},{6,7},{7,6},{8,9},{9,8},{10,11... | collective-permute-start | bytes 884744 | tf_op jit(solution)/shard_map/ppermute | solution.py:550
  37.7 3.4 %collective-permute-start.3 = (bf16[8,9,8,256]{3,2,1,0:T(8,128)(2,1)S(1)}, bf16[8,9,8,256]{3,2,1,0:T(8,128)(2,1)S(1)}, u32[]{:S(2)}, u32[]{:S(2)}) collective-permute-start(bf16[8,9,8,256]{3,2,1,0:T(8,128)(2,1)S(1)} %all-to-all-done.3.rows0), channel_id=1, source_target_pairs={{0,8},{1,9},{2,10},{3,11},{4,12},{5,13},{6,14},{7,15},{8,0},{9,1},... | collective-permute-start | bytes 884744 | tf_op jit(solution)/shard_map/ppermute | solution.py:550
  41.1 2.1 %collective-permute-start.4 = (bf16[8,9,8,256]{3,2,1,0:T(8,128)(2,1)S(1)}, bf16[8,9,8,256]{3,2,1,0:T(8,128)(2,1)S(1)}, u32[]{:S(2)}, u32[]{:S(2)}) collective-permute-start(bf16[8,9,8,256]{3,2,1,0:T(8,128)(2,1)S(1)} %all-to-all-done.3.rows0), channel_id=1, source_target_pairs={{0,9},{1,8},{2,11},{3,10},{4,13},{5,12},{6,15},{7,14},{8,1},{9,0},... | collective-permute-start | bytes 884744 | tf_op jit(solution)/shard_map/ppermute | solution.py:550
  43.2 21.7 %collective-permute-done.2.rows1 = bf16[8,9,8,256]{3,2,1,0:T(8,128)(2,1)S(1)} collective-permute-done((bf16[8,9,8,256]{3,2,1,0:T(8,128)(2,1)S(1)}, bf16[8,9,8,256]{3,2,1,0:T(8,128)(2,1)S(1)}, u32[]{:S(2)}, u32[]{:S(2)}) %collective-permute-start.2) | collective-permute-done | bytes 294944 | tf_op jit(solution)/shard_map/ppermute | solution.py:550
  65.0 2.8 %forward.1 = (bf16[6,8,8,256]{3,2,1,0:T(8,128)(2,1)}, bf16[3,8,16,256]{3,2,1,0:T(8,128)(2,1)S(1)}, bf16[9,256,256]{2,1,0:T(8,128)(2,1)S(1)}, bf16[138,8,128]{2,1...) custom-call(s32[1]{0:T(128)} %bitcast.6.me_ref, ...), custom_call_target="tpu_custom_call" | custom-call | tf_op jit(solution)/shard_map/forward/pallas_call | solution.py:586
  68.5 3.1 %backward.1 = (bf16[32,6,8,256]{3,2,1,0:T(8,128)(2,1)}, f32[6,8,8,256]{3,2,1,0:T(8,128)S(1)}, bf16[6,4,8,256]{3,2,1,0:T(8,128)(2,1)S(1)}, bf16[6,8,256]{2,1,0:T(8,128)(2,1)S(1)}) custom-call(s32[1]{0:T(128)} %bitcast.6.me_ref, s32[48]{0:T(128)S(1)} %get-tuple-element.110.route, bf16[3,8,16,256]{3,2,1,0:T(8,128)(2,1)S(1)} %get-tuple-element.128.dpre, ...), custom_call_target="tpu_custom_call" | custom-call | flops 500000000 | bytes 8000000 | tf_op jit(solution)/shard_map/backward/pallas_call | solution.py:608
  71.6 9.0 %all-to-all-start.4 = ((bf16[32,6,8,256]{3,2,1,0:T(8,128)(2,1)}), bf16[32,6,8,256]{3,2,1,0:T(8,128)(2,1)S(1)}, u32[]{:S(2)}, u32[]{:S(2)}) async-start(bf16[32,6,8,256]{3,2,1,0:T(8,128)(2,1)} %get-tuple-element.133), calls=%async_computation.4 | async-start | bytes 1572864 | tf_op jit(solution)/shard_map/all_to_all | solution.py:545
  80.6 3.8 %collective-permute-start.5 = (bf16[138,8,128]{2,1,0:T(8,128)(2,1)S(1)}, bf16[138,8,128]{2,1,0:T(8,128)(2,1)S(1)}, u32[]{:S(2)}, u32[]{:S(2)}) collective-permute-start(bf16[138,8,128]{2,1,0:T(8,128)(2,1)S(1)} %copy-done.9), channel_id=1, source_target_pairs={{0,1},{1,0},{2,3},{3,2},{4,5},{5,4},{6,7},{7,6},{8,9},{9,8},{10,11... | collective-permute-start | bytes 847880 | tf_op jit(solution)/shard_map/ppermute | solution.py:550
  84.5 3.4 %collective-permute-start.6 = (bf16[138,8,128]{2,1,0:T(8,128)(2,1)S(1)}, bf16[138,8,128]{2,1,0:T(8,128)(2,1)S(1)}, u32[]{:S(2)}, u32[]{:S(2)}) collective-permute-start(bf16[138,8,128]{2,1,0:T(8,128)(2,1)S(1)} %get-tuple-element.117), channel_id=1, source_target_pairs={{0,8},{1,9},{2,10},{3,11},{4,12},{5,13},{6,14},{7,15},{8,0},{9,1},... | collective-permute-start | bytes 847880 | tf_op jit(solution)/shard_map/ppermute | solution.py:550
  87.8 2.1 %collective-permute-start.7 = (bf16[138,8,128]{2,1,0:T(8,128)(2,1)S(1)}, bf16[138,8,128]{2,1,0:T(8,128)(2,1)S(1)}, u32[]{:S(2)}, u32[]{:S(2)}) collective-permute-start(bf16[138,8,128]{2,1,0:T(8,128)(2,1)S(1)} %get-tuple-element.118), channel_id=1, source_target_pairs={{0,9},{1,8},{2,11},{3,10},{4,13},{5,12},{6,15},{7,14},{8,1},{9,0},... | collective-permute-start | bytes 847880 | tf_op jit(solution)/shard_map/ppermute | solution.py:550
  90.0 21.8 %collective-permute-done.5.block1 = bf16[138,8,128]{2,1,0:T(8,128)(2,1)S(1)} collective-permute-done((bf16[138,8,128]{2,1,0:T(8,128)(2,1)S(1)}, bf16[138,8,128]{2,1,0:T(8,128)(2,1)S(1)}, u32[]{:S(2)}, u32[]{:S(2)}) %collective-permute-start.5) | collective-permute-done | bytes 282656 | tf_op jit(solution)/shard_map/ppermute | solution.py:550
  111.8 1.4 weight.1
  113.2 4.6 %collective-permute-start.10 = (f32[2,9,8,256]{3,2,1,0:T(8,128)S(1)}, f32[2,9,8,256]{3,2,1,0:T(8,128)S(1)}, u32[]{:S(2)}, u32[]{:S(2)}) collective-permute-start(f32[2,9,8,256]{3,2,1,0:T(8,128)S(1)} %get-tuple-element.122), channel_id=1, source_target_pairs={{0,6},{1,7},{2,4},{3,5},{4,2},{5,3},{6,0},{7,1},{8,14},{9,15},{10,... | collective-permute-start | bytes 442376 | tf_op jit(solution)/shard_map/ppermute | solution.py:550
  117.8 4.3 %collective-permute-start.8 = (f32[2,9,8,256]{3,2,1,0:T(8,128)S(1)}, f32[2,9,8,256]{3,2,1,0:T(8,128)S(1)}, u32[]{:S(2)}, u32[]{:S(2)}) collective-permute-start(f32[2,9,8,256]{3,2,1,0:T(8,128)S(1)} %get-tuple-element.120), channel_id=1, source_target_pairs={{0,2},{1,3},{2,0},{3,1},{4,6},{5,7},{6,4},{7,5},{8,10},{9,11},{10,... | collective-permute-start | bytes 442376 | tf_op jit(solution)/shard_map/ppermute | solution.py:550
  122.1 3.4 %collective-permute-start.9 = (f32[2,9,8,256]{3,2,1,0:T(8,128)S(1)}, f32[2,9,8,256]{3,2,1,0:T(8,128)S(1)}, u32[]{:S(2)}, u32[]{:S(2)}) collective-permute-start(f32[2,9,8,256]{3,2,1,0:T(8,128)S(1)} %get-tuple-element.121), channel_id=1, source_target_pairs={{0,4},{1,5},{2,6},{3,7},{4,0},{5,1},{6,2},{7,3},{8,12},{9,13},{10,... | collective-permute-start | bytes 442376 | tf_op jit(solution)/shard_map/ppermute | solution.py:550
  125.5 2.1 %collective-permute-done.8.part1 = f32[2,9,8,256]{3,2,1,0:T(8,128)S(1)} collective-permute-done((f32[2,9,8,256]{3,2,1,0:T(8,128)S(1)}, f32[2,9,8,256]{3,2,1,0:T(8,128)S(1)}, u32[]{:S(2)}, u32[]{:S(2)}) %collective-permute-start.8) | collective-permute-done | bytes 147488 | tf_op jit(solution)/shard_map/ppermute | solution.py:550
  127.5 8.5 %collective-permute-done.9.part2 = f32[2,9,8,256]{3,2,1,0:T(8,128)S(1)} collective-permute-done((f32[2,9,8,256]{3,2,1,0:T(8,128)S(1)}, f32[2,9,8,256]{3,2,1,0:T(8,128)S(1)}, u32[]{:S(2)}, u32[]{:S(2)}) %collective-permute-start.9) | collective-permute-done | bytes 147488 | tf_op jit(solution)/shard_map/ppermute | solution.py:550
  136.1 3.9 %collective-permute-start.11 = (f32[9,8,256]{2,1,0:T(8,128)S(1)}, f32[9,8,256]{2,1,0:T(8,128)S(1)}, u32[]{:S(2)}, u32[]{:S(2)}) collective-permute-start(f32[9,8,256]{2,1,0:T(8,128)S(1)} %get-tuple-element.124), channel_id=1, source_target_pairs={{0,16},{1,17},{2,18},{3,19},{4,20},{5,21},{6,22},{7,23},{8,24},{9,... | collective-permute-start | bytes 221192 | tf_op jit(solution)/shard_map/ppermute | solution.py:550
  141.3 1.9 %collective-permute-done.11.part1 = f32[9,8,256]{2,1,0:T(8,128)S(1)} collective-permute-done((f32[9,8,256]{2,1,0:T(8,128)S(1)}, f32[9,8,256]{2,1,0:T(8,128)S(1)}, u32[]{:S(2)}, u32[]{:S(2)}) %collective-permute-start.11) | collective-permute-done | bytes 73760 | tf_op jit(solution)/shard_map/ppermute | solution.py:550
  143.3 0.8 sum.1
  144.1 27.8 %conditional.1 = (f32[72,256]{1,0:T(8,128)}, f32[72,256]{1,0:T(8,128)}, bf16[1,6,8,8,256]{4,3,2,1,0:T(8,128)(2,1)S(1)}) conditional(s32[]{:T(128)} %bitcast.15, (s32[]{:T(128)}, f32[1]{0:T(128)}, f32[64,1,128]{2,1,0:T(1,128)}, f32[2,9,8,256]{3,2,1,0:T(8,128)S(1)}, f32[1,72,256]{2,1,0:T(8,128)S(1)}, /*index=5*/s32[1]{0:T(128)}, s32[48]{0:T(128)S(1)}, ...), branch_computations={%region_0.0_spmd, %region_1.0_spmd} | conditional | flops 2000003 | bytes 4688272 | solution.py:697
  144.1 4.9 %collective-permute-start = (f32[2,9,8,256]{3,2,1,0:T(8,128)S(1)}, f32[2,9,8,256]{3,2,1,0:T(8,128)S(1)}, u32[]{:S(2)}, u32[]{:S(2)}) collective-permute-start(f32[2,9,8,256]{3,2,1,0:T(8,128)S(1)} %get-tuple-element.56.own), channel_id=1, source_target_pairs={{0,64},{32,96},{64,0},{96,32},{128,192},{160,224},{192,128},{224,1... | collective-permute-start | bytes 442376 | tf_op jit(solution)/shard_map/cond/branch_0_fun/ppermute | solution.py:542
  149.0 10.1 %all-to-all-start = ((f32[64,1,128]{2,1,0:T(1,128)}), f32[64,1,128]{2,1,0:T(1,128)S(1)}, u32[]{:S(2)}, u32[]{:S(2)}) async-start(f32[64,1,128]{2,1,0:T(1,128)} %get-tuple-element.55), calls=%async_computation | async-start | bytes 65536 | tf_op jit(solution)/shard_map/cond/branch_0_fun/all_to_all | solution.py:545
  159.2 0.9 grad.2
  160.1 11.0 %all-to-all-done.squares = f32[64,1,128]{2,1,0:T(1,128)S(1)} async-done(((f32[64,1,128]{2,1,0:T(1,128)}), f32[64,1,128]{2,1,0:T(1,128)S(1)}, u32[]{:S(2)}, u32[]{:S(2)}) %all-to-all-start) | async-done | bytes 32800 | tf_op jit(solution)/shard_map/cond/branch_0_fun/all_to_all | solution.py:545
  171.1 0.8 final.2
  (32 shorter events, 5.0 us)
Async XLA Ops:
  0.6 0.9 copy-start.3
  2.3 62.7 %copy-start.1 = (bf16[1,6,8,8,256]{4,3,2,1,0:T(8,128)(2,1)S(1)}, bf16[1,6,8,8,256]{4,3,2,1,0:T(8,128)(2,1)}, u32[]{:S(2)}) copy-start(bf16[1,6,8,8,256]{4,3,2,1,0:T(8,128)(2,1)} %param.12) | copy-start | bytes 589828
  2.3 62.7 %copy-start.2 = (bf16[1,6,8,8,256]{4,3,2,1,0:T(8,128)(2,1)S(1)}, bf16[1,6,8,8,256]{4,3,2,1,0:T(8,128)(2,1)}, u32[]{:S(2)}) copy-start(bf16[1,6,8,8,256]{4,3,2,1,0:T(8,128)(2,1)} %param.13) | copy-start | bytes 589828
  2.3 26.4 %all-to-all-start.3 = ((bf16[8,9,8,256]{3,2,1,0:T(8,128)(2,1)}), bf16[8,9,8,256]{3,2,1,0:T(8,128)(2,1)S(1)}, u32[]{:S(2)}, u32[]{:S(2)}) async-start(bf16[8,9,8,256]{3,2,1,0:T(8,128)(2,1)} %get-tuple-element.113), calls=%async_computation.3 | async-start | bytes 589824 | tf_op jit(solution)/shard_map/all_to_all | solution.py:545
  14.7 0.9 copy-start
  15.7 0.7 copy-start.4
  16.3 0.7 copy-start.5
  17.0 0.7 copy-start.6
  17.7 0.7 copy-start.7
  28.6 36.3 %all-to-all-start.2 = ((bf16[32,6,8,256]{3,2,1,0:T(8,128)(2,1)}), bf16[32,6,8,256]{3,2,1,0:T(8,128)(2,1)S(1)}, u32[]{:S(2)}, u32[]{:S(2)}) async-start(bf16[32,6,8,256]{3,2,1,0:T(8,128)(2,1)} %get-tuple-element.112), calls=%async_computation.2 | async-start | bytes 1572864 | tf_op jit(solution)/shard_map/all_to_all | solution.py:545
  34.0 30.9 %collective-permute-start.2 = (bf16[8,9,8,256]{3,2,1,0:T(8,128)(2,1)S(1)}, bf16[8,9,8,256]{3,2,1,0:T(8,128)(2,1)S(1)}, u32[]{:S(2)}, u32[]{:S(2)}) collective-permute-start(bf16[8,9,8,256]{3,2,1,0:T(8,128)(2,1)S(1)} %all-to-all-done.3.rows0), channel_id=1, source_target_pairs={{0,1},{1,0},{2,3},{3,2},{4,5},{5,4},{6,7},{7,6},{8,9},{9,8},{10,11... | collective-permute-start | bytes 884744 | tf_op jit(solution)/shard_map/ppermute | solution.py:550
  37.7 27.2 %collective-permute-start.3 = (bf16[8,9,8,256]{3,2,1,0:T(8,128)(2,1)S(1)}, bf16[8,9,8,256]{3,2,1,0:T(8,128)(2,1)S(1)}, u32[]{:S(2)}, u32[]{:S(2)}) collective-permute-start(bf16[8,9,8,256]{3,2,1,0:T(8,128)(2,1)S(1)} %all-to-all-done.3.rows0), channel_id=1, source_target_pairs={{0,8},{1,9},{2,10},{3,11},{4,12},{5,13},{6,14},{7,15},{8,0},{9,1},... | collective-permute-start | bytes 884744 | tf_op jit(solution)/shard_map/ppermute | solution.py:550
  41.1 23.9 %collective-permute-start.4 = (bf16[8,9,8,256]{3,2,1,0:T(8,128)(2,1)S(1)}, bf16[8,9,8,256]{3,2,1,0:T(8,128)(2,1)S(1)}, u32[]{:S(2)}, u32[]{:S(2)}) collective-permute-start(bf16[8,9,8,256]{3,2,1,0:T(8,128)(2,1)S(1)} %all-to-all-done.3.rows0), channel_id=1, source_target_pairs={{0,9},{1,8},{2,11},{3,10},{4,13},{5,12},{6,15},{7,14},{8,1},{9,0},... | collective-permute-start | bytes 884744 | tf_op jit(solution)/shard_map/ppermute | solution.py:550
  67.8 0.7 copy-start.8
  71.6 9.0 %copy-start.9 = (bf16[138,8,128]{2,1,0:T(8,128)(2,1)S(1)}, bf16[138,8,128]{2,1,0:T(8,128)(2,1)}, u32[]{:S(2)}) copy-start(bf16[138,8,128]{2,1,0:T(8,128)(2,1)} %copy-done.8) | copy-start | bytes 847876
  71.6 72.5 %all-to-all-start.4 = ((bf16[32,6,8,256]{3,2,1,0:T(8,128)(2,1)}), bf16[32,6,8,256]{3,2,1,0:T(8,128)(2,1)S(1)}, u32[]{:S(2)}, u32[]{:S(2)}) async-start(bf16[32,6,8,256]{3,2,1,0:T(8,128)(2,1)} %get-tuple-element.133), calls=%async_computation.4 | async-start | bytes 1572864 | tf_op jit(solution)/shard_map/all_to_all | solution.py:545
  80.6 63.4 %copy-start.10 = (f32[1,72,256]{2,1,0:T(8,128)S(1)}, f32[1,72,256]{2,1,0:T(8,128)}, u32[]{:S(2)}) copy-start(f32[1,72,256]{2,1,0:T(8,128)} %param.15) | copy-start | bytes 221188
  80.6 31.1 %collective-permute-start.5 = (bf16[138,8,128]{2,1,0:T(8,128)(2,1)S(1)}, bf16[138,8,128]{2,1,0:T(8,128)(2,1)S(1)}, u32[]{:S(2)}, u32[]{:S(2)}) collective-permute-start(bf16[138,8,128]{2,1,0:T(8,128)(2,1)S(1)} %copy-done.9), channel_id=1, source_target_pairs={{0,1},{1,0},{2,3},{3,2},{4,5},{5,4},{6,7},{7,6},{8,9},{9,8},{10,11... | collective-permute-start | bytes 847880 | tf_op jit(solution)/shard_map/ppermute | solution.py:550
  84.5 27.3 %collective-permute-start.6 = (bf16[138,8,128]{2,1,0:T(8,128)(2,1)S(1)}, bf16[138,8,128]{2,1,0:T(8,128)(2,1)S(1)}, u32[]{:S(2)}, u32[]{:S(2)}) collective-permute-start(bf16[138,8,128]{2,1,0:T(8,128)(2,1)S(1)} %get-tuple-element.117), channel_id=1, source_target_pairs={{0,8},{1,9},{2,10},{3,11},{4,12},{5,13},{6,14},{7,15},{8,0},{9,1},... | collective-permute-start | bytes 847880 | tf_op jit(solution)/shard_map/ppermute | solution.py:550
  87.8 23.9 %collective-permute-start.7 = (bf16[138,8,128]{2,1,0:T(8,128)(2,1)S(1)}, bf16[138,8,128]{2,1,0:T(8,128)(2,1)S(1)}, u32[]{:S(2)}, u32[]{:S(2)}) collective-permute-start(bf16[138,8,128]{2,1,0:T(8,128)(2,1)S(1)} %get-tuple-element.118), channel_id=1, source_target_pairs={{0,9},{1,8},{2,11},{3,10},{4,13},{5,12},{6,15},{7,14},{8,1},{9,0},... | collective-permute-start | bytes 847880 | tf_op jit(solution)/shard_map/ppermute | solution.py:550
  113.2 12.2 %collective-permute-start.10 = (f32[2,9,8,256]{3,2,1,0:T(8,128)S(1)}, f32[2,9,8,256]{3,2,1,0:T(8,128)S(1)}, u32[]{:S(2)}, u32[]{:S(2)}) collective-permute-start(f32[2,9,8,256]{3,2,1,0:T(8,128)S(1)} %get-tuple-element.122), channel_id=1, source_target_pairs={{0,6},{1,7},{2,4},{3,5},{4,2},{5,3},{6,0},{7,1},{8,14},{9,15},{10,... | collective-permute-start | bytes 442376 | tf_op jit(solution)/shard_map/ppermute | solution.py:550
  117.8 9.8 %collective-permute-start.8 = (f32[2,9,8,256]{3,2,1,0:T(8,128)S(1)}, f32[2,9,8,256]{3,2,1,0:T(8,128)S(1)}, u32[]{:S(2)}, u32[]{:S(2)}) collective-permute-start(f32[2,9,8,256]{3,2,1,0:T(8,128)S(1)} %get-tuple-element.120), channel_id=1, source_target_pairs={{0,2},{1,3},{2,0},{3,1},{4,6},{5,7},{6,4},{7,5},{8,10},{9,11},{10,... | collective-permute-start | bytes 442376 | tf_op jit(solution)/shard_map/ppermute | solution.py:550
  122.1 14.0 %collective-permute-start.9 = (f32[2,9,8,256]{3,2,1,0:T(8,128)S(1)}, f32[2,9,8,256]{3,2,1,0:T(8,128)S(1)}, u32[]{:S(2)}, u32[]{:S(2)}) collective-permute-start(f32[2,9,8,256]{3,2,1,0:T(8,128)S(1)} %get-tuple-element.121), channel_id=1, source_target_pairs={{0,4},{1,5},{2,6},{3,7},{4,0},{5,1},{6,2},{7,3},{8,12},{9,13},{10,... | collective-permute-start | bytes 442376 | tf_op jit(solution)/shard_map/ppermute | solution.py:550
  136.1 7.2 %collective-permute-start.11 = (f32[9,8,256]{2,1,0:T(8,128)S(1)}, f32[9,8,256]{2,1,0:T(8,128)S(1)}, u32[]{:S(2)}, u32[]{:S(2)}) collective-permute-start(f32[9,8,256]{2,1,0:T(8,128)S(1)} %get-tuple-element.124), channel_id=1, source_target_pairs={{0,16},{1,17},{2,18},{3,19},{4,20},{5,21},{6,22},{7,23},{8,24},{9,... | collective-permute-start | bytes 221192 | tf_op jit(solution)/shard_map/ppermute | solution.py:550
  144.1 27.1 %collective-permute-start = (f32[2,9,8,256]{3,2,1,0:T(8,128)S(1)}, f32[2,9,8,256]{3,2,1,0:T(8,128)S(1)}, u32[]{:S(2)}, u32[]{:S(2)}) collective-permute-start(f32[2,9,8,256]{3,2,1,0:T(8,128)S(1)} %get-tuple-element.56.own), channel_id=1, source_target_pairs={{0,64},{32,96},{64,0},{96,32},{128,192},{160,224},{192,128},{224,1... | collective-permute-start | bytes 442376 | tf_op jit(solution)/shard_map/cond/branch_0_fun/ppermute | solution.py:542
  149.0 22.1 %all-to-all-start = ((f32[64,1,128]{2,1,0:T(1,128)}), f32[64,1,128]{2,1,0:T(1,128)S(1)}, u32[]{:S(2)}, u32[]{:S(2)}) async-start(f32[64,1,128]{2,1,0:T(1,128)} %get-tuple-element.55), calls=%async_computation | async-start | bytes 65536 | tf_op jit(solution)/shard_map/cond/branch_0_fun/all_to_all | solution.py:545
  171.9 0.7 copy-start.11

commit v5 on v4

--- a/solution.py
+++ b/solution.py
@@ -153,7 +153,7 @@
     return 8 * y + z
 
 
-PEERS = [[seat(m, n) for n in range(8)] for m in range(4)]
+COLOURS = [[seat(m, n) for m in pair for n in range(8)] for pair in ((0, 3), (1, 2))]
 COLUMNS = 30
 GRADS = 42
 MESSAGE = 138
@@ -177,7 +177,7 @@
 
 
 def forward_kernel(
-    me_ref, route, field, strips, cot, recv, rows0, rows1, rows2, rows3,
+    me_ref, route, field, strips, cot, recv, rows0, rows1, rows2,
     act, dpre, taps, message0, message1, message2, message3,
     pad0, pad1, pad2, cols, rows, sems,
 ):
@@ -188,9 +188,16 @@
     me = me_ref[0]
     role = role_of(me)
     messages = (message0, message1, message2, message3)
+    upper = role >> 1
+    sources = (
+        rows0.at[pl.ds(8 * upper, 8)],
+        rows1,
+        rows2,
+        rows0.at[pl.ds(8 * (1 - upper), 8)],
+    )
     copies = [
         pltpu.make_async_copy(source, rows.at[role ^ k], sems.at[k])
-        for k, source in enumerate((rows0, rows1, rows2, rows3))
+        for k, source in enumerate(sources)
     ]
     for copy in copies:
         copy.start()
@@ -554,12 +561,12 @@
         taps_kernel,
         compiler_params=LIMIT,
         name="taps",
-        out_shape=(sds((8, 9, 8, chans), BF16), sds((9, 8, chans), F32)),
+        out_shape=(sds((16, 9, 8, chans), BF16), sds((9, 8, chans), F32)),
         in_specs=[vmem],
         out_specs=(vmem, vmem),
         scratch_shapes=[pltpu.VMEM((72, chans // 2), F32)] * 2,
     )(w)
-    rows = exchange(rows, PEERS)
+    rows = exchange(rows, COLOURS)
 
     halo_send, strips, route = pl.pallas_call(
         edge_kernel,
@@ -576,7 +583,8 @@
         cost_estimate=pl.CostEstimate(flops=1_000_000, bytes_accessed=8_000_000, transcendentals=0),
     )(me, tile_links.T, tile_codes.T, corner_links.T, corner_codes.T, field)
     halo = exchange(halo_send)
-    rows = [rows] + share([rows] * 3)
+    kept = lax.dynamic_slice_in_dim(rows, 8 * (role_of(me[0]) >> 1), 8, 0)
+    rows = [rows] + share([kept] * 2, (1, 8))
 
     pairs = per // 2
     pad = pltpu.VMEM((pairs, side + 2, 2 * side, chans), BF16)
@@ -593,7 +601,7 @@
             sds((9, chans, chans), BF16),
             message, message, message, message,
         ),
-        in_specs=[smem] * 2 + [vmem] * 4 + [any_space] * 4,
+        in_specs=[smem] * 2 + [vmem] * 4 + [any_space] * 3,
         out_specs=(vmem,) * 7,
         scratch_shapes=[
             pad, pad, pad,

time: 174 us -> 175 us (level)
  the two profiles are of different devices: /device:TPU:6 before, /device:TPU:4 now
where the time goes in v5:
time: 175 us; the launch traced here: 174 us
  waiting for transfers between devices  78 us (45%)
  starting transfers between devices  75.6 us (43%)
  Pallas kernels  15.9 us (9%)
  local copies, waits for them, and re-layouts  2.35 us (1%)
  between operations  2.19 us (1%)
    ppermute x9, waiting for transfers between devices, share(): lax.ppermute(value, 'tile', [(i, i ^ step) for i in range(width)])  53.8 us
    all_to_all x4, starting transfers between devices, exchange(): lax.all_to_all(value, axis, 0, 0, axis_index_groups=groups, tiled=True)  37.8 us
    ppermute x9, starting transfers between devices, share(): lax.ppermute(value, 'tile', [(i, i ^ step) for i in range(width)])  32.8 us
    all_to_all x4, waiting for transfers between devices, exchange(): lax.all_to_all(value, axis, 0, 0, axis_index_groups=groups, tiled=True)  24.2 us
    pallas_call x1, Pallas kernels, body(): pl.pallas_call(edge_kernel, compiler_params=LIMIT, name='edge', out_shape...  5.1 us
    ppermute x1, starting transfers between devices, swap(): return lax.ppermute(value, 'rep', [(i, i ^ 1 << bit) for i in range(reps)])  5.01 us
  transfers between devices with their start and end apart: 14, of which 7 were waited for; matrix products, arithmetic and copies ran while one was open for 0% of the time, Pallas kernels for 5%

profile of v5, /device:TPU:4, one launch (start us, length us, event | category | flops | bytes accessed | tf_op | source)
XLA Modules:
  0.0 174.1 jit_solution(16411967600822917232)
XLA Ops:
  0.7 0.9 copy-done.2
  1.6 0.9 taps.1
  2.5 13.5 %all-to-all-start.3 = ((bf16[16,9,8,256]{3,2,1,0:T(8,128)(2,1)}), bf16[16,9,8,256]{3,2,1,0:T(8,128)(2,1)S(1)}, u32[]{:S(2)}, u32[]{:S(2)}) async-start(bf16[16,9,8,256]{3,2,1,0:T(8,128)(2,1)} %get-tuple-element.113), calls=%async_computation.3 | async-start | bytes 1179648 | tf_op jit(solution)/shard_map/all_to_all | solution.py:552
  16.0 5.1 %edge.1 = (bf16[32,6,8,256]{3,2,1,0:T(8,128)(2,1)}, bf16[6,4,8,256]{3,2,1,0:T(8,128)(2,1)S(1)}, s32[48]{0:T(128)S(1)}) custom-call(s32[1]{0:T(128)} %bitcast.6.me_ref, s32[4,192]{1,0:T(4,128)S(1)} %bitcast.22, s32[4,192]{1,0:T(4,128)S(1)} %bitcast.23, s32[4,192]{1,0:T(4,128)S(1)} %bitcast.24, s32[4,192]{1,0:T(4,128)S(1)} %bitcast.25, ...), custom_call_target="tpu_custom_call" | custom-call | flops 1000000 | bytes 8000000 | tf_op jit(solution)/shard_map/edge/pallas_call | solution.py:571
  21.1 13.3 %all-to-all-done.3.rows0 = bf16[16,9,8,256]{3,2,1,0:T(8,128)(2,1)S(1)} async-done(((bf16[16,9,8,256]{3,2,1,0:T(8,128)(2,1)}), bf16[16,9,8,256]{3,2,1,0:T(8,128)(2,1)S(1)}, u32[]{:S(2)}, u32[]{:S(2)}) %all-to-all-start.3) | async-done | bytes 589856 | tf_op jit(solution)/shard_map/all_to_all | solution.py:552
  34.4 5.9 %all-to-all-start.2 = ((bf16[32,6,8,256]{3,2,1,0:T(8,128)(2,1)}), bf16[32,6,8,256]{3,2,1,0:T(8,128)(2,1)S(1)}, u32[]{:S(2)}, u32[]{:S(2)}) async-start(bf16[32,6,8,256]{3,2,1,0:T(8,128)(2,1)} %get-tuple-element.112), calls=%async_computation.2 | async-start | bytes 1572864 | tf_op jit(solution)/shard_map/all_to_all | solution.py:552
  40.4 3.7 %collective-permute-start.2 = (bf16[8,9,8,256]{3,2,1,0:T(8,128)(2,1)S(1)}, bf16[8,9,8,256]{3,2,1,0:T(8,128)(2,1)S(1)}, u32[]{:S(2)}, u32[]{:S(2)}) collective-permute-start(bf16[8,9,8,256]{3,2,1,0:T(8,128)(2,1)S(1)} %constant_dynamic-slice_fusion), channel_id=1, source_target_pairs={{0,1},{1,0},{2,3},{3,2},{4,5},{5,4},{6,7},{7,6},{8,9},{9,8},{10,11... | collective-permute-start | bytes 884744 | tf_op jit(solution)/shard_map/ppermute | solution.py:557
  44.1 3.4 %collective-permute-start.3 = (bf16[8,9,8,256]{3,2,1,0:T(8,128)(2,1)S(1)}, bf16[8,9,8,256]{3,2,1,0:T(8,128)(2,1)S(1)}, u32[]{:S(2)}, u32[]{:S(2)}) collective-permute-start(bf16[8,9,8,256]{3,2,1,0:T(8,128)(2,1)S(1)} %constant_dynamic-slice_fusion), channel_id=1, source_target_pairs={{0,8},{1,9},{2,10},{3,11},{4,12},{5,13},{6,14},{7,15},{8,0},{9,1},... | collective-permute-start | bytes 884744 | tf_op jit(solution)/shard_map/ppermute | solution.py:557
  47.5 18.1 %collective-permute-done.2.rows1 = bf16[8,9,8,256]{3,2,1,0:T(8,128)(2,1)S(1)} collective-permute-done((bf16[8,9,8,256]{3,2,1,0:T(8,128)(2,1)S(1)}, bf16[8,9,8,256]{3,2,1,0:T(8,128)(2,1)S(1)}, u32[]{:S(2)}, u32[]{:S(2)}) %collective-permute-start.2) | collective-permute-done | bytes 294944 | tf_op jit(solution)/shard_map/ppermute | solution.py:557
  65.5 2.8 %forward.1 = (bf16[6,8,8,256]{3,2,1,0:T(8,128)(2,1)}, bf16[3,8,16,256]{3,2,1,0:T(8,128)(2,1)S(1)}, bf16[9,256,256]{2,1,0:T(8,128)(2,1)S(1)}, bf16[138,8,128]{2,1...) custom-call(s32[1]{0:T(128)} %bitcast.6.me_ref, ...), custom_call_target="tpu_custom_call" | custom-call | tf_op jit(solution)/shard_map/forward/pallas_call | solution.py:594
  68.3 0.7 copy-done.7
  69.0 3.1 %backward.1 = (bf16[32,6,8,256]{3,2,1,0:T(8,128)(2,1)}, f32[6,8,8,256]{3,2,1,0:T(8,128)S(1)}, bf16[6,4,8,256]{3,2,1,0:T(8,128)(2,1)S(1)}, bf16[6,8,256]{2,1,0:T(8,128)(2,1)S(1)}) custom-call(s32[1]{0:T(128)} %bitcast.6.me_ref, s32[48]{0:T(128)S(1)} %get-tuple-element.110.route, bf16[3,8,16,256]{3,2,1,0:T(8,128)(2,1)S(1)} %get-tuple-element.128.dpre, ...), custom_call_target="tpu_custom_call" | custom-call | flops 500000000 | bytes 8000000 | tf_op jit(solution)/shard_map/backward/pallas_call | solution.py:616
  72.2 9.0 %all-to-all-start.4 = ((bf16[32,6,8,256]{3,2,1,0:T(8,128)(2,1)}), bf16[32,6,8,256]{3,2,1,0:T(8,128)(2,1)S(1)}, u32[]{:S(2)}, u32[]{:S(2)}) async-start(bf16[32,6,8,256]{3,2,1,0:T(8,128)(2,1)} %get-tuple-element.133), calls=%async_computation.4 | async-start | bytes 1572864 | tf_op jit(solution)/shard_map/all_to_all | solution.py:552
  81.2 3.8 %collective-permute-start.4 = (bf16[138,8,128]{2,1,0:T(8,128)(2,1)S(1)}, bf16[138,8,128]{2,1,0:T(8,128)(2,1)S(1)}, u32[]{:S(2)}, u32[]{:S(2)}) collective-permute-start(bf16[138,8,128]{2,1,0:T(8,128)(2,1)S(1)} %copy-done.8), channel_id=1, source_target_pairs={{0,1},{1,0},{2,3},{3,2},{4,5},{5,4},{6,7},{7,6},{8,9},{9,8},{10,11... | collective-permute-start | bytes 847880 | tf_op jit(solution)/shard_map/ppermute | solution.py:557
  85.0 3.4 %collective-permute-start.5 = (bf16[138,8,128]{2,1,0:T(8,128)(2,1)S(1)}, bf16[138,8,128]{2,1,0:T(8,128)(2,1)S(1)}, u32[]{:S(2)}, u32[]{:S(2)}) collective-permute-start(bf16[138,8,128]{2,1,0:T(8,128)(2,1)S(1)} %get-tuple-element.117), channel_id=1, source_target_pairs={{0,8},{1,9},{2,10},{3,11},{4,12},{5,13},{6,14},{7,15},{8,0},{9,1},... | collective-permute-start | bytes 847880 | tf_op jit(solution)/shard_map/ppermute | solution.py:557
  88.4 2.1 %collective-permute-start.6 = (bf16[138,8,128]{2,1,0:T(8,128)(2,1)S(1)}, bf16[138,8,128]{2,1,0:T(8,128)(2,1)S(1)}, u32[]{:S(2)}, u32[]{:S(2)}) collective-permute-start(bf16[138,8,128]{2,1,0:T(8,128)(2,1)S(1)} %get-tuple-element.118), channel_id=1, source_target_pairs={{0,9},{1,8},{2,11},{3,10},{4,13},{5,12},{6,15},{7,14},{8,1},{9,0},... | collective-permute-start | bytes 847880 | tf_op jit(solution)/shard_map/ppermute | solution.py:557
  90.5 21.8 %collective-permute-done.4.block1 = bf16[138,8,128]{2,1,0:T(8,128)(2,1)S(1)} collective-permute-done((bf16[138,8,128]{2,1,0:T(8,128)(2,1)S(1)}, bf16[138,8,128]{2,1,0:T(8,128)(2,1)S(1)}, u32[]{:S(2)}, u32[]{:S(2)}) %collective-permute-start.4) | collective-permute-done | bytes 282656 | tf_op jit(solution)/shard_map/ppermute | solution.py:557
  112.3 1.4 weight.1
  113.8 4.7 %collective-permute-start.7 = (f32[2,9,8,256]{3,2,1,0:T(8,128)S(1)}, f32[2,9,8,256]{3,2,1,0:T(8,128)S(1)}, u32[]{:S(2)}, u32[]{:S(2)}) collective-permute-start(f32[2,9,8,256]{3,2,1,0:T(8,128)S(1)} %get-tuple-element.120), channel_id=1, source_target_pairs={{0,2},{1,3},{2,0},{3,1},{4,6},{5,7},{6,4},{7,5},{8,10},{9,11},{10,... | collective-permute-start | bytes 442376 | tf_op jit(solution)/shard_map/ppermute | solution.py:557
  118.4 4.2 %collective-permute-start.8 = (f32[2,9,8,256]{3,2,1,0:T(8,128)S(1)}, f32[2,9,8,256]{3,2,1,0:T(8,128)S(1)}, u32[]{:S(2)}, u32[]{:S(2)}) collective-permute-start(f32[2,9,8,256]{3,2,1,0:T(8,128)S(1)} %get-tuple-element.121), channel_id=1, source_target_pairs={{0,4},{1,5},{2,6},{3,7},{4,0},{5,1},{6,2},{7,3},{8,12},{9,13},{10,... | collective-permute-start | bytes 442376 | tf_op jit(solution)/shard_map/ppermute | solution.py:557
  122.6 3.4 %collective-permute-start.9 = (f32[2,9,8,256]{3,2,1,0:T(8,128)S(1)}, f32[2,9,8,256]{3,2,1,0:T(8,128)S(1)}, u32[]{:S(2)}, u32[]{:S(2)}) collective-permute-start(f32[2,9,8,256]{3,2,1,0:T(8,128)S(1)} %get-tuple-element.122), channel_id=1, source_target_pairs={{0,6},{1,7},{2,4},{3,5},{4,2},{5,3},{6,0},{7,1},{8,14},{9,15},{10,... | collective-permute-start | bytes 442376 | tf_op jit(solution)/shard_map/ppermute | solution.py:557
  126.0 3.6 %collective-permute-done.8.part2 = f32[2,9,8,256]{3,2,1,0:T(8,128)S(1)} collective-permute-done((f32[2,9,8,256]{3,2,1,0:T(8,128)S(1)}, f32[2,9,8,256]{3,2,1,0:T(8,128)S(1)}, u32[]{:S(2)}, u32[]{:S(2)}) %collective-permute-start.8) | collective-permute-done | bytes 147488 | tf_op jit(solution)/shard_map/ppermute | solution.py:557
  129.6 7.1 %collective-permute-done.9.part3 = f32[2,9,8,256]{3,2,1,0:T(8,128)S(1)} collective-permute-done((f32[2,9,8,256]{3,2,1,0:T(8,128)S(1)}, f32[2,9,8,256]{3,2,1,0:T(8,128)S(1)}, u32[]{:S(2)}, u32[]{:S(2)}) %collective-permute-start.9) | collective-permute-done | bytes 147488 | tf_op jit(solution)/shard_map/ppermute | solution.py:557
  136.8 4.2 %collective-permute-start.10 = (f32[9,8,256]{2,1,0:T(8,128)S(1)}, f32[9,8,256]{2,1,0:T(8,128)S(1)}, u32[]{:S(2)}, u32[]{:S(2)}) collective-permute-start(f32[9,8,256]{2,1,0:T(8,128)S(1)} %get-tuple-element.124), channel_id=1, source_target_pairs={{0,16},{1,17},{2,18},{3,19},{4,20},{5,21},{6,22},{7,23},{8,24},{9,... | collective-permute-start | bytes 221192 | tf_op jit(solution)/shard_map/ppermute | solution.py:557
  142.3 3.2 %collective-permute-done.10.part1 = f32[9,8,256]{2,1,0:T(8,128)S(1)} collective-permute-done((f32[9,8,256]{2,1,0:T(8,128)S(1)}, f32[9,8,256]{2,1,0:T(8,128)S(1)}, u32[]{:S(2)}, u32[]{:S(2)}) %collective-permute-start.10) | collective-permute-done | bytes 73760 | tf_op jit(solution)/shard_map/ppermute | solution.py:557
  145.5 0.8 sum.1
  146.2 27.2 %conditional.1 = (f32[72,256]{1,0:T(8,128)}, f32[72,256]{1,0:T(8,128)}, bf16[1,6,8,8,256]{4,3,2,1,0:T(8,128)(2,1)S(1)}) conditional(s32[]{:T(128)} %bitcast.15, (s32[]{:T(128)}, f32[1]{0:T(128)}, f32[64,1,128]{2,1,0:T(1,128)}, f32[2,9,8,256]{3,2,1,0:T(8,128)S(1)}, f32[1,72,256]{2,1,0:T(8,128)S(1)}, /*index=5*/s32[1]{0:T(128)}, s32[48]{0:T(128)S(1)}, ...), branch_computations={%region_0.0_spmd, %region_1.0_spmd} | conditional | flops 2000003 | bytes 4688272 | solution.py:705
  146.2 5.0 %collective-permute-start = (f32[2,9,8,256]{3,2,1,0:T(8,128)S(1)}, f32[2,9,8,256]{3,2,1,0:T(8,128)S(1)}, u32[]{:S(2)}, u32[]{:S(2)}) collective-permute-start(f32[2,9,8,256]{3,2,1,0:T(8,128)S(1)} %get-tuple-element.56.own), channel_id=1, source_target_pairs={{0,64},{32,96},{64,0},{96,32},{128,192},{160,224},{192,128},{224,1... | collective-permute-start | bytes 442376 | tf_op jit(solution)/shard_map/cond/branch_0_fun/ppermute | solution.py:549
  151.3 9.4 %all-to-all-start = ((f32[64,1,128]{2,1,0:T(1,128)}), f32[64,1,128]{2,1,0:T(1,128)S(1)}, u32[]{:S(2)}, u32[]{:S(2)}) async-start(f32[64,1,128]{2,1,0:T(1,128)} %get-tuple-element.55), calls=%async_computation | async-start | bytes 65536 | tf_op jit(solution)/shard_map/cond/branch_0_fun/all_to_all | solution.py:552
  160.8 0.9 grad.2
  161.7 11.0 %all-to-all-done.squares = f32[64,1,128]{2,1,0:T(1,128)S(1)} async-done(((f32[64,1,128]{2,1,0:T(1,128)}), f32[64,1,128]{2,1,0:T(1,128)S(1)}, u32[]{:S(2)}, u32[]{:S(2)}) %all-to-all-start) | async-done | bytes 32800 | tf_op jit(solution)/shard_map/cond/branch_0_fun/all_to_all | solution.py:552
  172.7 0.8 final.2
  (29 shorter events, 0.8 us)
Async XLA Ops:
  0.6 15.3 %copy-start = (bf16[1,6,8,8,256]{4,3,2,1,0:T(8,128)(2,1)S(1)}, bf16[1,6,8,8,256]{4,3,2,1,0:T(8,128)(2,1)}, u32[]{:S(2)}) copy-start(bf16[1,6,8,8,256]{4,3,2,1,0:T(8,128)(2,1)} %param.12) | copy-start | bytes 589828
  0.6 0.9 copy-start.2
  1.6 14.4 %copy-start.3 = (s32[192,4]{0,1:T(4,128)S(1)}, s32[192,4]{0,1:T(4,128)}, u32[]{:S(2)}) copy-start(s32[192,4]{0,1:T(4,128)} %param.16) | copy-start | bytes 9220
  1.6 14.4 %copy-start.4 = (s32[192,4]{0,1:T(4,128)S(1)}, s32[192,4]{0,1:T(4,128)}, u32[]{:S(2)}) copy-start(s32[192,4]{0,1:T(4,128)} %param.17) | copy-start | bytes 9220
  1.6 14.4 %copy-start.5 = (s32[192,4]{0,1:T(4,128)S(1)}, s32[192,4]{0,1:T(4,128)}, u32[]{:S(2)}) copy-start(s32[192,4]{0,1:T(4,128)} %param.18) | copy-start | bytes 9220
  1.6 14.4 %copy-start.6 = (s32[192,4]{0,1:T(4,128)S(1)}, s32[192,4]{0,1:T(4,128)}, u32[]{:S(2)}) copy-start(s32[192,4]{0,1:T(4,128)} %param.19) | copy-start | bytes 9220
  2.5 31.9 %all-to-all-start.3 = ((bf16[16,9,8,256]{3,2,1,0:T(8,128)(2,1)}), bf16[16,9,8,256]{3,2,1,0:T(8,128)(2,1)S(1)}, u32[]{:S(2)}, u32[]{:S(2)}) async-start(bf16[16,9,8,256]{3,2,1,0:T(8,128)(2,1)} %get-tuple-element.113), calls=%async_computation.3 | async-start | bytes 1179648 | tf_op jit(solution)/shard_map/all_to_all | solution.py:552
  16.0 49.5 %copy-start.1 = (bf16[1,6,8,8,256]{4,3,2,1,0:T(8,128)(2,1)S(1)}, bf16[1,6,8,8,256]{4,3,2,1,0:T(8,128)(2,1)}, u32[]{:S(2)}) copy-start(bf16[1,6,8,8,256]{4,3,2,1,0:T(8,128)(2,1)} %param.13) | copy-start | bytes 589828
  34.4 31.1 %all-to-all-start.2 = ((bf16[32,6,8,256]{3,2,1,0:T(8,128)(2,1)}), bf16[32,6,8,256]{3,2,1,0:T(8,128)(2,1)S(1)}, u32[]{:S(2)}, u32[]{:S(2)}) async-start(bf16[32,6,8,256]{3,2,1,0:T(8,128)(2,1)} %get-tuple-element.112), calls=%async_computation.2 | async-start | bytes 1572864 | tf_op jit(solution)/shard_map/all_to_all | solution.py:552
  40.4 25.1 %collective-permute-start.2 = (bf16[8,9,8,256]{3,2,1,0:T(8,128)(2,1)S(1)}, bf16[8,9,8,256]{3,2,1,0:T(8,128)(2,1)S(1)}, u32[]{:S(2)}, u32[]{:S(2)}) collective-permute-start(bf16[8,9,8,256]{3,2,1,0:T(8,128)(2,1)S(1)} %constant_dynamic-slice_fusion), channel_id=1, source_target_pairs={{0,1},{1,0},{2,3},{3,2},{4,5},{5,4},{6,7},{7,6},{8,9},{9,8},{10,11... | collective-permute-start | bytes 884744 | tf_op jit(solution)/shard_map/ppermute | solution.py:557
  44.1 21.4 %collective-permute-start.3 = (bf16[8,9,8,256]{3,2,1,0:T(8,128)(2,1)S(1)}, bf16[8,9,8,256]{3,2,1,0:T(8,128)(2,1)S(1)}, u32[]{:S(2)}, u32[]{:S(2)}) collective-permute-start(bf16[8,9,8,256]{3,2,1,0:T(8,128)(2,1)S(1)} %constant_dynamic-slice_fusion), channel_id=1, source_target_pairs={{0,8},{1,9},{2,10},{3,11},{4,12},{5,13},{6,14},{7,15},{8,0},{9,1},... | collective-permute-start | bytes 884744 | tf_op jit(solution)/shard_map/ppermute | solution.py:557
  68.3 0.7 copy-start.7
  72.2 9.0 %copy-start.8 = (bf16[138,8,128]{2,1,0:T(8,128)(2,1)S(1)}, bf16[138,8,128]{2,1,0:T(8,128)(2,1)}, u32[]{:S(2)}) copy-start(bf16[138,8,128]{2,1,0:T(8,128)(2,1)} %copy-done.7) | copy-start | bytes 847876
  72.2 74.1 %all-to-all-start.4 = ((bf16[32,6,8,256]{3,2,1,0:T(8,128)(2,1)}), bf16[32,6,8,256]{3,2,1,0:T(8,128)(2,1)S(1)}, u32[]{:S(2)}, u32[]{:S(2)}) async-start(bf16[32,6,8,256]{3,2,1,0:T(8,128)(2,1)} %get-tuple-element.133), calls=%async_computation.4 | async-start | bytes 1572864 | tf_op jit(solution)/shard_map/all_to_all | solution.py:552
  81.1 65.1 %copy-start.9 = (f32[1,72,256]{2,1,0:T(8,128)S(1)}, f32[1,72,256]{2,1,0:T(8,128)}, u32[]{:S(2)}) copy-start(f32[1,72,256]{2,1,0:T(8,128)} %param.15) | copy-start | bytes 221188
  81.2 31.1 %collective-permute-start.4 = (bf16[138,8,128]{2,1,0:T(8,128)(2,1)S(1)}, bf16[138,8,128]{2,1,0:T(8,128)(2,1)S(1)}, u32[]{:S(2)}, u32[]{:S(2)}) collective-permute-start(bf16[138,8,128]{2,1,0:T(8,128)(2,1)S(1)} %copy-done.8), channel_id=1, source_target_pairs={{0,1},{1,0},{2,3},{3,2},{4,5},{5,4},{6,7},{7,6},{8,9},{9,8},{10,11... | collective-permute-start | bytes 847880 | tf_op jit(solution)/shard_map/ppermute | solution.py:557
  85.0 27.3 %collective-permute-start.5 = (bf16[138,8,128]{2,1,0:T(8,128)(2,1)S(1)}, bf16[138,8,128]{2,1,0:T(8,128)(2,1)S(1)}, u32[]{:S(2)}, u32[]{:S(2)}) collective-permute-start(bf16[138,8,128]{2,1,0:T(8,128)(2,1)S(1)} %get-tuple-element.117), channel_id=1, source_target_pairs={{0,8},{1,9},{2,10},{3,11},{4,12},{5,13},{6,14},{7,15},{8,0},{9,1},... | collective-permute-start | bytes 847880 | tf_op jit(solution)/shard_map/ppermute | solution.py:557
  88.4 23.9 %collective-permute-start.6 = (bf16[138,8,128]{2,1,0:T(8,128)(2,1)S(1)}, bf16[138,8,128]{2,1,0:T(8,128)(2,1)S(1)}, u32[]{:S(2)}, u32[]{:S(2)}) collective-permute-start(bf16[138,8,128]{2,1,0:T(8,128)(2,1)S(1)} %get-tuple-element.118), channel_id=1, source_target_pairs={{0,9},{1,8},{2,11},{3,10},{4,13},{5,12},{6,15},{7,14},{8,1},{9,0},... | collective-permute-start | bytes 847880 | tf_op jit(solution)/shard_map/ppermute | solution.py:557
  113.8 12.2 %collective-permute-start.7 = (f32[2,9,8,256]{3,2,1,0:T(8,128)S(1)}, f32[2,9,8,256]{3,2,1,0:T(8,128)S(1)}, u32[]{:S(2)}, u32[]{:S(2)}) collective-permute-start(f32[2,9,8,256]{3,2,1,0:T(8,128)S(1)} %get-tuple-element.120), channel_id=1, source_target_pairs={{0,2},{1,3},{2,0},{3,1},{4,6},{5,7},{6,4},{7,5},{8,10},{9,11},{10,... | collective-permute-start | bytes 442376 | tf_op jit(solution)/shard_map/ppermute | solution.py:557
  118.4 11.2 %collective-permute-start.8 = (f32[2,9,8,256]{3,2,1,0:T(8,128)S(1)}, f32[2,9,8,256]{3,2,1,0:T(8,128)S(1)}, u32[]{:S(2)}, u32[]{:S(2)}) collective-permute-start(f32[2,9,8,256]{3,2,1,0:T(8,128)S(1)} %get-tuple-element.121), channel_id=1, source_target_pairs={{0,4},{1,5},{2,6},{3,7},{4,0},{5,1},{6,2},{7,3},{8,12},{9,13},{10,... | collective-permute-start | bytes 442376 | tf_op jit(solution)/shard_map/ppermute | solution.py:557
  122.6 14.1 %collective-permute-start.9 = (f32[2,9,8,256]{3,2,1,0:T(8,128)S(1)}, f32[2,9,8,256]{3,2,1,0:T(8,128)S(1)}, u32[]{:S(2)}, u32[]{:S(2)}) collective-permute-start(f32[2,9,8,256]{3,2,1,0:T(8,128)S(1)} %get-tuple-element.122), channel_id=1, source_target_pairs={{0,6},{1,7},{2,4},{3,5},{4,2},{5,3},{6,0},{7,1},{8,14},{9,15},{10,... | collective-permute-start | bytes 442376 | tf_op jit(solution)/shard_map/ppermute | solution.py:557
  136.8 8.7 %collective-permute-start.10 = (f32[9,8,256]{2,1,0:T(8,128)S(1)}, f32[9,8,256]{2,1,0:T(8,128)S(1)}, u32[]{:S(2)}, u32[]{:S(2)}) collective-permute-start(f32[9,8,256]{2,1,0:T(8,128)S(1)} %get-tuple-element.124), channel_id=1, source_target_pairs={{0,16},{1,17},{2,18},{3,19},{4,20},{5,21},{6,22},{7,23},{8,24},{9,... | collective-permute-start | bytes 221192 | tf_op jit(solution)/shard_map/ppermute | solution.py:557
  146.2 26.4 %collective-permute-start = (f32[2,9,8,256]{3,2,1,0:T(8,128)S(1)}, f32[2,9,8,256]{3,2,1,0:T(8,128)S(1)}, u32[]{:S(2)}, u32[]{:S(2)}) collective-permute-start(f32[2,9,8,256]{3,2,1,0:T(8,128)S(1)} %get-tuple-element.56.own), channel_id=1, source_target_pairs={{0,64},{32,96},{64,0},{96,32},{128,192},{160,224},{192,128},{224,1... | collective-permute-start | bytes 442376 | tf_op jit(solution)/shard_map/cond/branch_0_fun/ppermute | solution.py:549
  151.3 21.4 %all-to-all-start = ((f32[64,1,128]{2,1,0:T(1,128)}), f32[64,1,128]{2,1,0:T(1,128)S(1)}, u32[]{:S(2)}, u32[]{:S(2)}) async-start(f32[64,1,128]{2,1,0:T(1,128)} %get-tuple-element.55), calls=%async_computation | async-start | bytes 65536 | tf_op jit(solution)/shard_map/cond/branch_0_fun/all_to_all | solution.py:552
  173.4 0.7 copy-start.10
